TPU v7x, 32 devices: a whole 2x2x4 slice. The times are simulated.
32 devices in a mesh: seq: 8 (over y, x, core), head: 4 (over z).
Axes of the slice: x: 2, y: 2, z: 4, core: 2. Of those that a mesh axis runs over, the one named last changes fastest.
Arguments:
- tokens: bfloat16 [2048, 2048], P('seq'), may hold values from -18 to 18
- qkv_weight: bfloat16 [3, 2048, 2048], P(None, None, 'head'), may hold values from -1 to 1
- beta_logit: float32 [16, 2048], P('head', 'seq'), may hold values from -5.8 to -3.5
- log_decay: float32 [16, 2048], P('head', 'seq'), may hold values from -1 to 0
- out_grad: bfloat16 [2048, 2048], P('seq', 'head'), may hold values from -24 to 24
Outputs:
- input_grad: bfloat16 [2048, 2048], P('seq', 'head')
All inputs are finite; a program needn't handle non-finite values.
Results may differ from a plain program's by a relative error of at most 0.008.
Values may be sent and summed in bfloat16 or wider, within the bound.
No kernel may reach another device: no remote copies, remote signals or barrier semaphores. Data moves between devices by JAX's collectives and lax.ppermute only.
A program may use at most 64 MiB of HBM per device.

v0:
```python
import jax
import jax.numpy as jnp
from jax import lax
from jax.sharding import PartitionSpec as P

HIGH = lax.Precision.HIGHEST


def prefix(part, axis, combine, identity, reverse):
    count = lax.axis_size(axis)
    place = lax.axis_index(axis)
    ahead = count - 1 - place if reverse else place
    gathered = lax.all_gather(part, axis)
    state = jnp.zeros_like(part) + jnp.asarray(identity, part.dtype)

    def one(turn, state):
        source = count - 1 - turn if reverse else turn
        return combine(state, lax.dynamic_index_in_dim(gathered, source, 0, False))

    return lax.fori_loop(0, ahead, one, state)


def product(left, right):
    return jnp.dot(left, right, precision=HIGH)


def unit_rows(tensor):
    return tensor * lax.rsqrt(jnp.sum(tensor * tensor, axis=-1, keepdims=True) + 1e-06)


def block_step(memory, pieces, want_out):
    queries, key_rows, values, gate_rows, strengths = pieces
    block_size = key_rows.shape[0]
    row_ids = lax.broadcasted_iota(jnp.int32, (block_size, block_size), 0)
    col_ids = lax.broadcasted_iota(jnp.int32, (block_size, block_size), 1)
    causal = row_ids >= col_ids
    strict = row_ids > col_ids
    cumulative = jnp.cumsum(gate_rows)
    spread = jnp.where(causal, cumulative[:, None] - cumulative[None, :], 0.0)
    decays = jnp.where(causal, jnp.exp(spread), 0.0)
    opening = jnp.exp(cumulative)[:, None]
    couplings = jnp.where(strict, strengths[:, None] * decays * product(key_rows, key_rows.T), 0.0)
    system = jnp.eye(block_size, dtype=jnp.float32) + couplings
    target = strengths[:, None] * (values - opening * product(key_rows, memory))
    update = jax.scipy.linalg.solve_triangular(system, target, lower=True, unit_diagonal=True)
    fading = jnp.exp(cumulative[-1] - cumulative)[:, None]
    new_memory = jnp.exp(cumulative[-1]) * memory + product((key_rows * fading).T, update)
    if want_out:
        result = opening * product(queries, memory) + product(
            decays * product(queries, key_rows.T), update
        )
        return (new_memory, result)
    return (new_memory, None)


def run_segment(queries, key_rows, values, gate_rows, strengths, memory, want_out):
    length = key_rows.shape[0]
    block_size = min(64, length)
    blocks = length // block_size

    def blocked(tensor):
        return tensor.reshape((blocks, block_size) + tensor.shape[1:])

    def advance(carried, pieces):
        return block_step(carried, pieces, want_out)

    closing, results = lax.scan(
        advance,
        memory,
        (
            blocked(queries),
            blocked(key_rows),
            blocked(values),
            blocked(gate_rows),
            blocked(strengths),
        ),
    )
    if want_out:
        results = results.reshape(length, results.shape[-1])
    return (closing, results)


def transit(key_rows, values, gate_rows, strengths):
    head_width = key_rows.shape[-1]
    unit_keys = unit_rows(key_rows)
    opening = jnp.concatenate(
        [jnp.eye(head_width, dtype=jnp.float32), jnp.zeros((head_width, head_width), jnp.float32)],
        axis=1,
    )
    widened = jnp.concatenate([jnp.zeros_like(values), values], axis=1)
    closing, _ = run_segment(unit_keys, unit_keys, widened, gate_rows, strengths, opening, False)
    return closing


def seed_grad(queries, key_rows, gate_rows, strengths, cotangent):
    head_width = key_rows.shape[-1]
    unit_queries = unit_rows(queries)
    unit_keys = unit_rows(key_rows)
    vacant = jnp.zeros_like(unit_keys)

    def outputs(memory):
        return run_segment(unit_queries, unit_keys, vacant, gate_rows, strengths, memory, True)[1]

    _, pullback = jax.vjp(outputs, jnp.zeros((head_width, head_width), jnp.float32))
    return pullback(cotangent)[0]


def pull_back(queries, key_rows, values, gate_rows, strengths, memory, cotangent, beyond):

    def forward(query_in, key_in, value_in):
        return run_segment(
            unit_rows(query_in), unit_rows(key_in), value_in, gate_rows, strengths, memory, True
        )

    _, pullback = jax.vjp(forward, queries, key_rows, values)
    return pullback((beyond, cotangent))


def compose(earlier, later):
    head_width = earlier.shape[-2]
    leading = later[..., :head_width]
    shifted = jnp.einsum("hij,hjk->hik", leading, earlier, precision=HIGH)
    return shifted + jnp.concatenate([jnp.zeros_like(leading), later[..., head_width:]], axis=-1)


def split_product(grads, weights):
    upper = grads.astype(jnp.bfloat16)
    lower = (grads - upper.astype(jnp.float32)).astype(jnp.bfloat16)
    first = jnp.einsum("ptc,pdc->td", upper, weights, preferred_element_type=jnp.float32)
    second = jnp.einsum("ptc,pdc->td", lower, weights, preferred_element_type=jnp.float32)
    return first + second


def on_device(tokens, qkv_weight, beta_logit, log_decay, out_grad):
    heads_here, length = beta_logit.shape
    head_width = qkv_weight.shape[-1] // heads_here

    def per_head(tensor):
        return tensor.reshape(length, heads_here, head_width).transpose(1, 0, 2)

    projected = [
        per_head(jnp.dot(tokens, qkv_weight[member], preferred_element_type=jnp.float32))
        for member in range(3)
    ]
    queries, key_rows, values = projected
    strengths = jax.nn.sigmoid(beta_logit)
    cotangent = per_head(out_grad.astype(jnp.float32))
    transitions = jax.vmap(transit)(key_rows, values, log_decay, strengths)
    seeds = jax.vmap(seed_grad)(queries, key_rows, log_decay, strengths, cotangent)
    eyes = jnp.broadcast_to(
        jnp.eye(head_width, dtype=jnp.float32), (heads_here, head_width, head_width)
    )
    identity = jnp.concatenate(
        [eyes, jnp.zeros((heads_here, head_width, head_width), jnp.float32)], axis=-1
    )
    reached = prefix(transitions, "seq", compose, identity, False)
    entering = reached[..., head_width:]
    mirrored = jnp.concatenate([jnp.swapaxes(transitions[..., :head_width], 1, 2), seeds], axis=-1)
    returned = prefix(mirrored, "seq", compose, identity, True)
    leaving = returned[..., head_width:]
    grads = jax.vmap(pull_back)(
        queries, key_rows, values, log_decay, strengths, entering, cotangent, leaving
    )
    stacked = jnp.stack(grads)
    qkv_grad = stacked.transpose(0, 2, 1, 3).reshape(3, length, heads_here * head_width)
    partial_sums = split_product(qkv_grad, qkv_weight)
    assembled = lax.psum_scatter(partial_sums, "head", scatter_dimension=1, tiled=True)
    return assembled.astype(jnp.bfloat16)


def solution(mesh):
    return jax.shard_map(
        on_device,
        mesh=mesh,
        in_specs=(
            P("seq", None),
            P(None, None, "head"),
            P("head", "seq"),
            P("head", "seq"),
            P("seq", "head"),
        ),
        out_specs=P("seq", "head"),
        check_vma=False,
    )
```

profile of v0, /device:TPU:0, one launch (start us, length us, event | category | flops | bytes accessed | tf_op | source)
XLA Modules:
  0.0 743.3 jit_solution(4689616812996333202)
XLA Ops:
  6.6 5.7 slice_bitcast_fusion.1
  12.2 4.0 copy.111
  16.2 2.3 multiply_reduce_fusion.3
  19.4 4.0 copy.119
  23.4 2.3 multiply_reduce_fusion.2
  28.5 10.9 %while.137 = (s32[]{:T(128)}, f32[4,4,64,1]{2,1,3,0:T(4,128)S(1)}, f32[4,4,64,1]{2,1,3,0:T(4,128)S(1)}, f32[4,4,64,64]{3,2,1,0:T(8,128)S(1)}, f32[4,4]{1,0:T(4,1...) while((s32[]{:T(128)}, f32[4,4,64,1]{2,1,3,0:T(4,128)S(1)}, ...), condition=%wide.region_7.8_spmd.clone.clone, body=%wide.region_5.7_spmd.clone.clone.sunk | while | flops 50577408 | bytes 1030393 | solution.py:67
  43.4 99.5 %while.139 = (s32[]{:T(128)}, f32[4,128,128]{2,1,0:T(8,128)S(1)}, f32[4,4,64,128]{3,2,1,0:T(8,128)S(1)}, f32[4,4,64,1]{2,1,3,0:T(4,128)S(1)}, f32[4,4,64,128]{3,...) while((s32[]{:T(128)}, f32[4,128,128]{2,1,0:T(8,128)S(1)}, ...), condition=%wide.region_9.11_spmd.clone, body=%wide.region_8.10_spmd.clone.sunk | while | flops 201863232 | bytes 3133135 | solution.py:67
  47.0 19.7 %custom-call.44 = f32[4,1,64,64]{2,3,1,0:T(8,128)S(1)} custom-call(f32[4,1,64,64]{3,2,1,0:T(8,128)S(1)} %fusion.393), custom_call_target="InvertDiagBlocksLowerTriangular" | custom-call | tf_op jit(solution)/shard_map/vmap(transpose(jvp()))/while/body/eval_jaxpr/jit(_solve_triangular)/triangular_solve/custom-call.0 | solution.py:45
  71.9 19.7 %custom-call.44 = f32[4,1,64,64]{2,3,1,0:T(8,128)S(1)} custom-call(f32[4,1,64,64]{3,2,1,0:T(8,128)S(1)} %fusion.393), custom_call_target="InvertDiagBlocksLowerTriangular" | custom-call | tf_op jit(solution)/shard_map/vmap(transpose(jvp()))/while/body/eval_jaxpr/jit(_solve_triangular)/triangular_solve/custom-call.0 | solution.py:45
  96.8 19.7 %custom-call.44 = f32[4,1,64,64]{2,3,1,0:T(8,128)S(1)} custom-call(f32[4,1,64,64]{3,2,1,0:T(8,128)S(1)} %fusion.393), custom_call_target="InvertDiagBlocksLowerTriangular" | custom-call | tf_op jit(solution)/shard_map/vmap(transpose(jvp()))/while/body/eval_jaxpr/jit(_solve_triangular)/triangular_solve/custom-call.0 | solution.py:45
  121.6 19.7 %custom-call.44 = f32[4,1,64,64]{2,3,1,0:T(8,128)S(1)} custom-call(f32[4,1,64,64]{3,2,1,0:T(8,128)S(1)} %fusion.393), custom_call_target="InvertDiagBlocksLowerTriangular" | custom-call | tf_op jit(solution)/shard_map/vmap(transpose(jvp()))/while/body/eval_jaxpr/jit(_solve_triangular)/triangular_solve/custom-call.0 | solution.py:45
  142.9 4.0 copy.113
  146.9 2.3 fusion.189
  150.4 93.3 %while.133 = (s32[]{:T(128)}, f32[4,128,256]{2,1,0:T(8,128)S(1)}, f32[4,4,64]{2,1,0:T(4,128)S(1)}, f32[4,4,64,128]{3,2,1,0:T(8,128)S(1)}, f32[4,4,64]{2,1,0:T(4,...) while((s32[]{:T(128)}, f32[4,128,256]{2,1,0:T(8,128)S(1)}, f32[4,4,64]{2,1,0:T(4,128)S(1)}, ...), condition=%wide.region_3.4_spmd, body=%wide.region_1.3_spmd.sunk | while | flops 277508160 | bytes 3566773 | solution.py:67
  151.0 1.4 fusion.314
  152.9 19.7 %custom-call.40 = f32[4,1,64,64]{2,3,1,0:T(8,128)S(1)} custom-call(f32[4,1,64,64]{3,2,1,0:T(8,128)S(1)} %fusion.316), custom_call_target="InvertDiagBlocksLowerTriangular" | custom-call | tf_op jit(solution)/shard_map/vmap()/while/body/eval_jaxpr/jit(_solve_triangular)/triangular_solve | solution.py:45
  174.3 1.4 fusion.314
  176.2 19.7 %custom-call.40 = f32[4,1,64,64]{2,3,1,0:T(8,128)S(1)} custom-call(f32[4,1,64,64]{3,2,1,0:T(8,128)S(1)} %fusion.316), custom_call_target="InvertDiagBlocksLowerTriangular" | custom-call | tf_op jit(solution)/shard_map/vmap()/while/body/eval_jaxpr/jit(_solve_triangular)/triangular_solve | solution.py:45
  197.6 1.4 fusion.314
  199.5 19.7 %custom-call.40 = f32[4,1,64,64]{2,3,1,0:T(8,128)S(1)} custom-call(f32[4,1,64,64]{3,2,1,0:T(8,128)S(1)} %fusion.316), custom_call_target="InvertDiagBlocksLowerTriangular" | custom-call | tf_op jit(solution)/shard_map/vmap()/while/body/eval_jaxpr/jit(_solve_triangular)/triangular_solve | solution.py:45
  220.9 1.4 fusion.314
  222.8 19.7 %custom-call.40 = f32[4,1,64,64]{2,3,1,0:T(8,128)S(1)} custom-call(f32[4,1,64,64]{3,2,1,0:T(8,128)S(1)} %fusion.316), custom_call_target="InvertDiagBlocksLowerTriangular" | custom-call | tf_op jit(solution)/shard_map/vmap()/while/body/eval_jaxpr/jit(_solve_triangular)/triangular_solve | solution.py:45
  245.8 1.9 copy.172
  247.7 36.6 %all-gather.5.cloned.1.call-done = f32[32,128,256]{2,1,0:T(8,128)} async-done(((f32[4,128,256]{2,1,0:T(8,128)}), f32[32,128,256]{2,1,0:T(8,128)}) %all-gather.5.cloned.1.call-update) | async-done | bytes 4194320 | tf_op jit(solution)/shard_map/all_gather | solution.py:13
  284.3 12.5 %while.134 = (s32[]{:T(128)}, f32[4,128,256]{2,1,0:T(8,128)S(1)}, s32[]{:T(128)}, f32[8,4,128,256]{3,2,1,0:T(8,128)}, s32[]{:T(128)}, /*index=5*/s32[]{:T(128)}, s32[]{:T(128)}, s32[]{:T(128)}) while((s32[]{:T(128)}, f32[4,128,256]{2,1,0:T(8,128)S(1)}, s32[]{:T(128)}, f32[8,4,128,256]{3,2,1,0:T(8,128)}, s32[]{:T(128)}, ...), condition=%wide.region_11.13_spmd, body=%wide.region_10.12_spmd.sunk | while | flops 201457664 | bytes 4194439 | solution.py:20
  296.8 26.0 %all-gather.7.cloned.1.call-done = f32[32,128,256]{2,1,0:T(8,128)} async-done(((f32[4,128,256]{2,1,0:T(8,128)}), f32[32,128,256]{2,1,0:T(8,128)}) %all-gather.7.cloned.1.call-update) | async-done | bytes 4194320 | tf_op jit(solution)/shard_map/all_gather | solution.py:13
  328.0 108.7 %while.138 = (s32[]{:T(128)}, f32[4,128,128]{2,1,0:T(8,128)S(1)}, f32[4,4,128,64]{2,3,1,0:T(8,128)}, f32[4,4,64,64]{3,2,1,0:T(8,128)}, f32[4,4,128,128]{3,2,1,0:...) while((s32[]{:T(128)}, f32[4,128,128]{2,1,0:T(8,128)S(1)}, ...), condition=%wide.region_16.18_spmd.clone.clone, body=%wide.region_14.17_spmd.clone.clone.sunk | while | flops 176779584 | bytes 4178785 | solution.py:67
  331.0 19.7 %custom-call.43 = f32[4,1,64,64]{2,3,1,0:T(8,128)S(1)} custom-call(f32[4,1,64,64]{3,2,1,0:T(8,128)S(1)} %add_bitcast_fusion.5), custom_call_target="InvertDiagBlocksLowerTriangular" | custom-call | tf_op jit(solution)/shard_map/vmap(jvp())/while/body/eval_jaxpr/jit(_solve_triangular)/triangular_solve | solution.py:45
  358.1 19.7 %custom-call.43 = f32[4,1,64,64]{2,3,1,0:T(8,128)S(1)} custom-call(f32[4,1,64,64]{3,2,1,0:T(8,128)S(1)} %add_bitcast_fusion.5), custom_call_target="InvertDiagBlocksLowerTriangular" | custom-call | tf_op jit(solution)/shard_map/vmap(jvp())/while/body/eval_jaxpr/jit(_solve_triangular)/triangular_solve | solution.py:45
  385.3 19.7 %custom-call.43 = f32[4,1,64,64]{2,3,1,0:T(8,128)S(1)} custom-call(f32[4,1,64,64]{3,2,1,0:T(8,128)S(1)} %add_bitcast_fusion.5), custom_call_target="InvertDiagBlocksLowerTriangular" | custom-call | tf_op jit(solution)/shard_map/vmap(jvp())/while/body/eval_jaxpr/jit(_solve_triangular)/triangular_solve | solution.py:45
  412.5 19.7 %custom-call.43 = f32[4,1,64,64]{2,3,1,0:T(8,128)S(1)} custom-call(f32[4,1,64,64]{3,2,1,0:T(8,128)S(1)} %add_bitcast_fusion.5), custom_call_target="InvertDiagBlocksLowerTriangular" | custom-call | tf_op jit(solution)/shard_map/vmap(jvp())/while/body/eval_jaxpr/jit(_solve_triangular)/triangular_solve | solution.py:45
  439.2 221.7 %while.136 = (s32[]{:T(128)}, f32[4,128,128]{2,1,0:T(8,128)S(1)}, f32[4,4,64,128]{3,2,0,1:T(8,128)}, f32[4,4,64,128]{3,2,0,1:T(8,128)}, f32[4,4,64,128]{3,2,0,1:...) while((s32[]{:T(128)}, f32[4,128,128]{2,1,0:T(8,128)S(1)}, ...), condition=%wide.region_18.20_spmd.clone, body=%wide.region_17.19_spmd.clone.sunk | while | flops 516722752 | bytes 12292689 | solution.py:67
  442.8 19.7 %custom-call.41 = f32[4,1,64,64]{2,3,1,0:T(8,128)S(1)} custom-call(f32[4,1,64,64]{3,2,1,0:T(8,128)S(1)} %fusion.350), custom_call_target="InvertDiagBlocksLowerTriangular" | custom-call | tf_op jit(solution)/shard_map/vmap(transpose(jvp()))/while/body/eval_jaxpr/jit(_solve_triangular)/triangular_solve/custom-call.0 | solution.py:45
  464.7 19.7 %custom-call.42 = f32[4,1,64,64]{2,3,1,0:T(8,128)S(1)} custom-call(f32[4,1,64,64]{3,2,1,0:T(8,128)S(1)} %add_bitcast_fusion.4), custom_call_target="InvertDiagBlocksLowerTriangular" | custom-call | tf_op jit(solution)/shard_map/vmap(transpose(jvp()))/while/body/eval_jaxpr/jit(_solve_triangular)/triangular_solve | solution.py:45
  498.2 19.7 %custom-call.41 = f32[4,1,64,64]{2,3,1,0:T(8,128)S(1)} custom-call(f32[4,1,64,64]{3,2,1,0:T(8,128)S(1)} %fusion.350), custom_call_target="InvertDiagBlocksLowerTriangular" | custom-call | tf_op jit(solution)/shard_map/vmap(transpose(jvp()))/while/body/eval_jaxpr/jit(_solve_triangular)/triangular_solve/custom-call.0 | solution.py:45
  520.1 19.7 %custom-call.42 = f32[4,1,64,64]{2,3,1,0:T(8,128)S(1)} custom-call(f32[4,1,64,64]{3,2,1,0:T(8,128)S(1)} %add_bitcast_fusion.4), custom_call_target="InvertDiagBlocksLowerTriangular" | custom-call | tf_op jit(solution)/shard_map/vmap(transpose(jvp()))/while/body/eval_jaxpr/jit(_solve_triangular)/triangular_solve | solution.py:45
  553.6 19.7 %custom-call.41 = f32[4,1,64,64]{2,3,1,0:T(8,128)S(1)} custom-call(f32[4,1,64,64]{3,2,1,0:T(8,128)S(1)} %fusion.350), custom_call_target="InvertDiagBlocksLowerTriangular" | custom-call | tf_op jit(solution)/shard_map/vmap(transpose(jvp()))/while/body/eval_jaxpr/jit(_solve_triangular)/triangular_solve/custom-call.0 | solution.py:45
  575.5 19.7 %custom-call.42 = f32[4,1,64,64]{2,3,1,0:T(8,128)S(1)} custom-call(f32[4,1,64,64]{3,2,1,0:T(8,128)S(1)} %add_bitcast_fusion.4), custom_call_target="InvertDiagBlocksLowerTriangular" | custom-call | tf_op jit(solution)/shard_map/vmap(transpose(jvp()))/while/body/eval_jaxpr/jit(_solve_triangular)/triangular_solve | solution.py:45
  600.4 1.3 fusion.360
  609.1 19.7 %custom-call.41 = f32[4,1,64,64]{2,3,1,0:T(8,128)S(1)} custom-call(f32[4,1,64,64]{3,2,1,0:T(8,128)S(1)} %fusion.350), custom_call_target="InvertDiagBlocksLowerTriangular" | custom-call | tf_op jit(solution)/shard_map/vmap(transpose(jvp()))/while/body/eval_jaxpr/jit(_solve_triangular)/triangular_solve/custom-call.0 | solution.py:45
  630.9 19.7 %custom-call.42 = f32[4,1,64,64]{2,3,1,0:T(8,128)S(1)} custom-call(f32[4,1,64,64]{3,2,1,0:T(8,128)S(1)} %add_bitcast_fusion.4), custom_call_target="InvertDiagBlocksLowerTriangular" | custom-call | tf_op jit(solution)/shard_map/vmap(transpose(jvp()))/while/body/eval_jaxpr/jit(_solve_triangular)/triangular_solve | solution.py:45
  655.8 1.3 fusion.360
  660.9 1.3 copy.144
  665.3 1.7 copy.148
  667.0 5.7 convolution_bitcast_fusion
  672.7 6.1 fusion.187
  678.9 56.1 %reduce-scatter.2.cloned.1.call-done = f32[256,512]{1,0:T(8,128)} async-done(((f32[256,2048]{1,0:T(8,128)}), f32[256,512]{1,0:T(8,128)}) %reduce-scatter.2.cloned.1.call-update) | async-done | bytes 524304 | tf_op jit(solution)/shard_map/reduce_scatter | solution.py:167
  734.9 1.8 convert_element_type.37
  (444 shorter events, 164.7 us)
Async XLA Ops:
  6.5 9.7 %copy-start = (bf16[256,2048]{1,0:T(8,128)(2,1)S(1)}, bf16[256,2048]{1,0:T(8,128)(2,1)}, u32[]{:S(2)}) copy-start(bf16[256,2048]{1,0:T(8,128)(2,1)} %param.21) | copy-start | bytes 3145732
  6.5 277.8 %all-gather.5.cloned.1.call-start = ((), (), s32[]{:S(2)}) async-start(), calls=%async_computation.2 | async-start | bytes 4718592 | tf_op jit(solution)/shard_map/all_gather | solution.py:13
  18.5 0.8 copy-start.6
  25.7 0.8 copy-start.8
  25.7 0.8 copy-start.15
  25.7 0.9 copy-start.14
  28.5 10.9 %copy-start.13 = (bf16[256,512]{1,0:T(8,128)(2,1)S(1)}, bf16[256,512]{1,0:T(8,128)(2,1)}, u32[]{:S(2)}) copy-start(bf16[256,512]{1,0:T(8,128)(2,1)} %param.25) | copy-start | bytes 786436
  39.5 2.9 copy-start.10
  149.2 1.2 copy-start.11
  243.7 1.2 copy-start.2
  244.9 78.0 %all-gather.7.cloned.1.call-start = ((), (), s32[]{:S(2)}) async-start(), calls=%async_computation.3 | async-start | bytes 4718592 | tf_op jit(solution)/shard_map/all_gather | solution.py:13
  245.6 489.3 %reduce-scatter.2.cloned.1.call-start = ((), (), s32[]{:S(2)}) async-start(), calls=%async_computation.1 | async-start | bytes 2621440 | tf_op jit(solution)/shard_map/reduce_scatter | solution.py:167
  322.8 5.2 copy-start.3
  484.3 5.2 copy-start.4
  539.8 5.2 copy-start.4
  595.2 5.2 copy-start.4
  650.6 5.2 copy-start.4
  660.9 3.8 copy-start.9
  660.9 3.9 copy-start.12
  662.3 2.8 copy-start.7
  667.0 5.7 copy-start.5
  672.7 64.0 %copy-start.1 = (bf16[256,2048]{1,0:T(8,128)(2,1)S(1)}, bf16[256,2048]{1,0:T(8,128)(2,1)}, u32[]{:S(2)}) copy-start(bf16[256,2048]{1,0:T(8,128)(2,1)} %param.21) | copy-start | bytes 3145732
Sparse Core Ops, SparseCore 0:
  245.0 39.2 all-gather.4
  286.2 36.5 all-gather.6
  679.0 55.9 reduce-scatter.1
where the time goes:
time: 745 us; the launch traced here: 743 us
  other arithmetic  425 us (57%)
  matrix products  130 us (17%)
  waiting for transfers between devices  119 us (16%)
  local copies, waits for them, and re-layouts  53.4 us (7%)
  between operations  13.6 us (2%)
    another operation x72, other arithmetic, block_step(): jax.scipy.linalg.solve_triangular(system, target, lower=True, unit_diagon...  406 us
    dot_general x100, matrix products, product(): return jnp.dot(left, right, precision=HIGH)  92.4 us
    all_gather x2, waiting for transfers between devices, prefix(): gathered = lax.all_gather(part, axis)  62.6 us
    reduce_scatter x1, waiting for transfers between devices, on_device(): lax.psum_scatter(partial_sums, 'head', scatter_dimension=1, tiled=True)  56.1 us
    dot_general x4, local copies, waits for them, and re-layouts, on_device(): jnp.dot(tokens, qkv_weight[member], preferred_element_type=jnp.float32)  17.6 us
  transfers between devices with their start and end apart: 3, of which 3 were waited for; matrix products, arithmetic and copies ran while one was open for 2% of the time, Pallas kernels for 0%

commit v1 on v0

v1 whole, which is shorter than its diff:
```python
import functools

import jax
import jax.numpy as jnp
from jax import lax
from jax.experimental import pallas as pl
from jax.experimental.pallas import tpu as pltpu
from jax.sharding import PartitionSpec as P

F32 = jnp.float32
BF16 = jnp.bfloat16
HIGH = lax.Precision.HIGHEST
FAR = -1e30
BASE = 64


def nn(a, b):
    return lax.dot_general(a, b, (((1,), (0,)), ((), ())), preferred_element_type=F32)


def nt(a, b):
    return lax.dot_general(a, b, (((1,), (1,)), ((), ())), preferred_element_type=F32)


def fine(a, b, dims=(1, 0)):
    return lax.dot_general(
        a, b, (((dims[0],), (dims[1],)), ((), ())), precision=HIGH, preferred_element_type=F32
    )


def grid_ids(size):
    rows = lax.broadcasted_iota(jnp.int32, (size, size), 0)
    cols = lax.broadcasted_iota(jnp.int32, (size, size), 1)
    return rows, cols


def gates(logit, decay):
    size = decay.shape[1]
    rows, cols = grid_ids(size)
    lower = jnp.where(rows >= cols, 1.0, 0.0).astype(F32)
    eye = jnp.where(rows == cols, 1.0, 0.0).astype(F32)
    strength = 1.0 / (1.0 + jnp.exp(-logit))
    run_row = fine(decay, lower, (1, 1))
    run_col = fine(lower, decay, (1, 1))
    strength_col = fine(eye, strength, (1, 1))
    return strength, strength_col, run_row, run_col


def unit_rows(tensor):
    scale = lax.rsqrt(jnp.sum(tensor * tensor, axis=-1, keepdims=True) + 1e-06)
    return tensor * scale, scale


def unit_lower_inverse(couplings, rows, cols):
    size = couplings[0].shape[0]
    base = min(BASE, size)
    same = (rows // base) == (cols // base)
    power = [jnp.where(same, a, 0.0).astype(BF16) for a in couplings]
    rest = [-jnp.where(same, a, 0.0) for a in couplings]
    reach = 2
    if reach < base:
        power = [nn(a, a) for a in power]
    while reach < base:
        narrow = [a.astype(BF16) for a in power]
        rest = [n + p + nn(n.astype(BF16), b) for n, p, b in zip(rest, power, narrow)]
        reach *= 2
        if reach < base:
            power = [nn(b, b) for b in narrow]
    while base < size:
        wide = 2 * base
        off = jnp.logical_and((rows // wide) == (cols // wide), (rows // base) != (cols // base))
        outer = [jnp.where(off, a, 0.0) for a in couplings]
        narrow = [n.astype(BF16) for n in rest]
        half = [a + nn(a.astype(BF16), n) for a, n in zip(outer, narrow)]
        rest = [n - (y + nn(b, y.astype(BF16))) for n, b, y in zip(rest, narrow, half)]
        base = wide
    return rest


def prepare_kernel(
    heads, half, tok_ref, w_ref, logit_ref, decay_ref, og_ref,
    proj_ref, u_ref, wk_ref, dbt_ref, ktt_ref, keep_ref, send_ref,
    value_scr, pay_scr,
):
    member = pl.program_id(0)
    result = nn(tok_ref[...], w_ref[0])

    @pl.when(member < 2)
    def _():
        proj_ref[member] = result

    @pl.when(member == 2)
    def _():
        value_scr[...] = result
        size = tok_ref.shape[0]
        width = w_ref.shape[2] // heads
        rows, cols = grid_ids(size)
        causal = rows >= cols
        strict = rows > cols
        strength, strength_col, run_row, run_col = gates(logit_ref[...], decay_ref[...])
        every = range(heads)
        spans = [slice(h * width, (h + 1) * width) for h in every]
        queries = [unit_rows(proj_ref[0, :, s])[0] for s in spans]
        keys = [unit_rows(proj_ref[1, :, s])[0] for s in spans]
        key_b = [k.astype(BF16) for k in keys]
        query_b = [q.astype(BF16) for q in queries]
        gamma = [
            jnp.exp(jnp.where(causal, run_col[:, h : h + 1] - run_row[h : h + 1, :], FAR))
            for h in every
        ]
        couplings = [
            jnp.where(strict, strength_col[:, h : h + 1] * gamma[h] * nt(key_b[h], key_b[h]), 0.0)
            for h in every
        ]
        scores = [(gamma[h] * nt(query_b[h], key_b[h])).astype(BF16) for h in every]
        inverse = [n.astype(BF16) for n in unit_lower_inverse(couplings, rows, cols)]
        last = [run_col[size - 1 : size, h : h + 1] for h in every]
        open_col = [jnp.exp(run_col[:, h : h + 1]) for h in every]
        fade_row = [jnp.exp(last[h] - run_row[h : h + 1, :]) for h in every]
        write_key = [strength_col[:, h : h + 1] * open_col[h] * keys[h] for h in every]
        right = [
            jnp.concatenate(
                [strength_col[:, h : h + 1] * value_scr[:, spans[h]], write_key[h]], axis=1
            )
            for h in every
        ]
        solved = [right[h] + nn(inverse[h], right[h].astype(BF16)) for h in every]
        grad_t = [og_ref[:, s].astype(F32).T.astype(BF16) for s in spans]
        fade_t = [keys[h].T * fade_row[h] for h in every]
        left = [jnp.concatenate([nn(grad_t[h], scores[h]), fade_t[h]], axis=0) for h in every]
        back = [left[h] + nn(left[h].astype(BF16), inverse[h]) for h in every]
        e_rows, e_cols = grid_ids(width)
        for h in every:
            state = nn(fade_t[h].astype(BF16), solved[h].astype(BF16))
            unit = jnp.where(e_rows == e_cols, jnp.exp(last[h]), 0.0)
            seed = nn(grad_t[h], (open_col[h] * queries[h]).astype(BF16)) - nn(
                back[h][:width].astype(BF16), write_key[h].astype(BF16)
            )
            pay_scr[h, 0] = (unit - state[:, width:]).astype(BF16)
            pay_scr[h, 1] = state[:, :width].astype(BF16)
            pay_scr[h, 2] = seed.astype(BF16)
            u_ref[h] = solved[h][:, :width]
            wk_ref[h] = solved[h][:, width:].astype(BF16)
            dbt_ref[h] = back[h][:width]
            ktt_ref[h] = back[h][width:].astype(BF16)
        if half:
            core = lax.rem(lax.axis_index("seq"), 2)
            keep_ref[...] = pay_scr[pl.ds(core * half, half)]
            send_ref[...] = pay_scr[pl.ds((1 - core) * half, half)]
        else:
            keep_ref[...] = pay_scr[...]
            send_ref[...] = pay_scr[...]


def prepare(tokens, weights, logit, decay, out_grad, half):
    heads, size = logit.shape
    members, depth, columns = weights.shape
    width = columns // heads
    part = half or heads
    whole = lambda *shape: pl.BlockSpec(shape, lambda p: (0,) * len(shape))
    return pl.pallas_call(
        functools.partial(prepare_kernel, heads, half),
        grid=(members,),
        in_specs=[
            whole(size, depth),
            pl.BlockSpec((1, depth, columns), lambda p: (p, 0, 0)),
            whole(heads, size),
            whole(heads, size),
            whole(size, columns),
        ],
        out_specs=[
            whole(2, size, columns),
            whole(heads, size, width),
            whole(heads, size, width),
            whole(heads, width, size),
            whole(heads, width, size),
            whole(part, 3, width, width),
            whole(part, 3, width, width),
        ],
        out_shape=[
            jax.ShapeDtypeStruct((2, size, columns), F32),
            jax.ShapeDtypeStruct((heads, size, width), F32),
            jax.ShapeDtypeStruct((heads, size, width), BF16),
            jax.ShapeDtypeStruct((heads, width, size), F32),
            jax.ShapeDtypeStruct((heads, width, size), BF16),
            jax.ShapeDtypeStruct((part, 3, width, width), BF16),
            jax.ShapeDtypeStruct((part, 3, width, width), BF16),
        ],
        scratch_shapes=[
            pltpu.VMEM((size, columns), F32),
            pltpu.VMEM((heads, 3, width, width), BF16),
        ],
        name="prepare",
    )(tokens, weights, logit, decay, out_grad)


def pair_kernel(levels, keep_ref, recv_ref, *pay_refs):
    place = lax.axis_index("seq")
    first = lax.rem(place, 2) == 0
    chip = place // 2
    for h in range(keep_ref.shape[0]):
        mine = [keep_ref[h, i].astype(F32) for i in range(3)]
        other = [recv_ref[h, i].astype(F32) for i in range(3)]
        early = [jnp.where(first, a, b) for a, b in zip(mine, other)]
        late = [jnp.where(first, b, a) for a, b in zip(mine, other)]
        joint = fine(late[0], early[0]).astype(BF16)
        up = (fine(late[0], early[1]) + late[1]).astype(BF16)
        down = (fine(late[2], early[0]) + early[2]).astype(BF16)
        for level in range(levels):
            upward = lax.rem(chip // (1 << level), 2) == 0
            pay_refs[level][h, 0] = joint
            pay_refs[level][h, 1] = jnp.where(upward, up.astype(F32), down.astype(F32)).astype(BF16)


def join_pair(keep, recv, levels):
    half, _, width, _ = keep.shape
    shape = jax.ShapeDtypeStruct((half, 2, width, width), BF16)
    return pl.pallas_call(
        functools.partial(pair_kernel, levels), out_shape=[shape] * levels, name="join_pair"
    )(keep, recv)


def scan_kernel(chips, keep_ref, recv_ref, *refs):
    got_refs, (own_ref, send_ref, store, state) = refs[: chips - 1], refs[chips - 1 :]
    place = lax.axis_index("seq")
    first = lax.rem(place, 2) == 0
    chip = place // 2
    half = keep_ref.shape[0]
    for d in range(1, chips):
        store[d] = got_refs[d - 1][...]
    state[...] = jnp.zeros_like(state)

    def forward(j, carry):
        d = j ^ chip
        for h in range(half):
            state[h, 0] = fine(store[d, h, 0].astype(F32), state[h, 0]) + store[d, h, 1].astype(F32)
        return carry

    def backward(i, carry):
        d = (chips - 1 - i) ^ chip
        for h in range(half):
            state[h, 1] = fine(state[h, 1], store[d, h, 0].astype(F32)) + store[d, h, 1].astype(F32)
        return carry

    lax.fori_loop(0, chip, forward, 0)
    lax.fori_loop(0, chips - 1 - chip, backward, 0)
    for h in range(half):
        mine = [keep_ref[h, i].astype(F32) for i in range(3)]
        other = [recv_ref[h, i].astype(F32) for i in range(3)]
        early = [jnp.where(first, a, b) for a, b in zip(mine, other)]
        late = [jnp.where(first, b, a) for a, b in zip(mine, other)]
        enter = state[h, 0]
        leave = state[h, 1]
        middle = fine(early[0], enter) + early[1]
        inner = fine(leave, late[0]) + late[2]
        own_ref[h, 0] = jnp.where(first, enter, middle).astype(BF16)
        own_ref[h, 1] = jnp.where(first, inner, leave).astype(BF16)
        send_ref[h, 0] = jnp.where(first, middle, enter).astype(BF16)
        send_ref[h, 1] = jnp.where(first, leave, inner).astype(BF16)


def scan_chips(keep, recv, got):
    half, _, width, _ = keep.shape
    chips = len(got) + 1
    shape = jax.ShapeDtypeStruct((half, 2, width, width), BF16)
    return pl.pallas_call(
        functools.partial(scan_kernel, chips),
        out_shape=[shape, shape],
        scratch_shapes=[
            pltpu.VMEM((chips, half, 2, width, width), BF16),
            pltpu.VMEM((half, 2, width, width), F32),
        ],
        name="scan_chips",
    )(keep, recv, *got)


def finish_kernel(
    heads, half, order_ref, w_ref, proj_ref, u_ref, wk_ref, dbt_ref, ktt_ref, logit_ref, decay_ref,
    og_ref, own_ref, recv_ref, out_ref, grad_scr, edge_scr,
):
    @pl.when(pl.program_id(0) == 0)
    def _():
        size = og_ref.shape[0]
        width = og_ref.shape[1] // heads
        if half:
            core = lax.rem(lax.axis_index("seq"), 2)
            edge_scr[pl.ds(core * half, half)] = own_ref[...]
            edge_scr[pl.ds((1 - core) * half, half)] = recv_ref[...]
        else:
            edge_scr[...] = own_ref[...]
        rows, cols = grid_ids(size)
        strength, strength_col, run_row, run_col = gates(logit_ref[...], decay_ref[...])
        every = range(heads)
        spans = [slice(h * width, (h + 1) * width) for h in every]
        last = [run_col[size - 1 : size, h : h + 1] for h in every]
        beta = [strength_col[:, h : h + 1] for h in every]
        beta_row = [strength[h : h + 1, :] for h in every]
        open_col = [jnp.exp(run_col[:, h : h + 1]) for h in every]
        fade_col = [jnp.exp(last[h] - run_col[:, h : h + 1]) for h in every]
        gap = [run_col[:, h : h + 1] - run_row[h : h + 1, :] for h in every]
        gamma = [jnp.exp(jnp.where(rows >= cols, gap[h], FAR)) for h in every]
        gamma_t = [jnp.exp(jnp.where(rows <= cols, -gap[h], FAR)) for h in every]
        query = [unit_rows(proj_ref[0, :, s]) for s in spans]
        key = [unit_rows(proj_ref[1, :, s]) for s in spans]
        query_b = [q[0].astype(BF16) for q in query]
        key_b = [k[0].astype(BF16) for k in key]
        grad = [og_ref[:, s] for s in spans]
        grad_t = [g.astype(F32).T.astype(BF16) for g in grad]
        update = [(u_ref[h] - nn(wk_ref[h], edge_scr[h, 0])).astype(BF16) for h in every]
        delta_t = [dbt_ref[h] + nn(edge_scr[h, 1], ktt_ref[h]) for h in every]
        delta = [d.T for d in delta_t]
        delta_b = [d.astype(BF16) for d in delta]
        for h in every:
            lanes = nt(jnp.concatenate([grad[h], delta_b[h]], axis=0), update[h])
            turned = nn(update[h], jnp.concatenate([grad_t[h], delta_t[h].astype(BF16)], axis=1))
            attend = (gamma[h] * lanes[:size]).astype(BF16)
            attend_t = (gamma_t[h] * turned[:, :size]).astype(BF16)
            mix = jnp.where(rows > cols, beta[h] * gamma[h] * lanes[size:], 0.0) + jnp.where(
                rows < cols, beta_row[h] * gamma_t[h] * turned[:, size:], 0.0
            )
            edge = nt(jnp.concatenate([grad[h], delta_b[h]], axis=0), edge_scr[h, 0])
            dq = open_col[h] * edge[:size] + nn(attend, key_b[h])
            dk = (
                nn(attend_t, query_b[h])
                - nn(mix.astype(BF16), key_b[h])
                + fade_col[h] * nn(update[h], edge_scr[h, 1])
                - beta[h] * open_col[h] * edge[size:]
            )
            for slot, (unit, scale), slope in ((0, query[h], dq), (1, key[h], dk)):
                along = jnp.sum(unit * slope, axis=-1, keepdims=True)
                grad_scr[slot, :, spans[h]] = (scale * (slope - unit * along)).astype(BF16)
            grad_scr[2, :, spans[h]] = (beta[h] * delta[h]).astype(BF16)

    total = nt(grad_scr[0], w_ref[0])
    for member in range(1, w_ref.shape[0]):
        total = total + nt(grad_scr[member], w_ref[member])
    out_ref[0] = total


def finish(weights, proj, u, wk, dbt, ktt, logit, decay, out_grad, own, recv, half):
    heads, size = logit.shape
    members, depth, columns = weights.shape
    width = columns // heads
    parts = lax.axis_size("head")
    step = depth // parts
    place = lax.axis_index("head")
    order = lax.rem(place + jnp.arange(parts, dtype=jnp.int32), parts)
    whole = lambda *shape: pl.BlockSpec(shape, lambda p, order: (0,) * len(shape))
    return pl.pallas_call(
        functools.partial(finish_kernel, heads, half),
        grid_spec=pltpu.PrefetchScalarGridSpec(
            num_scalar_prefetch=1,
            grid=(parts,),
            in_specs=[
                pl.BlockSpec((members, step, columns), lambda p, order: (0, order[p], 0)),
                whole(*proj.shape),
                whole(*u.shape),
                whole(*wk.shape),
                whole(*dbt.shape),
                whole(*ktt.shape),
                whole(*logit.shape),
                whole(*decay.shape),
                whole(*out_grad.shape),
                whole(*own.shape),
                whole(*recv.shape),
            ],
            out_specs=pl.BlockSpec((1, size, step), lambda p, order: (p, 0, 0)),
            scratch_shapes=[
                pltpu.VMEM((3, size, columns), BF16),
                pltpu.VMEM((heads, 2, width, width), BF16),
            ],
        ),
        out_shape=jax.ShapeDtypeStruct((parts, size, step), F32),
        name="finish",
    )(order, weights, proj, u, wk, dbt, ktt, logit, decay, out_grad, own, recv)


def swap(value, axis, count, mask):
    return lax.ppermute(value, axis, [(i, i ^ mask) for i in range(count)])


def edges_by_pairs(keep, send, count):
    chips = count // 2
    levels = chips.bit_length() - 1
    recv = swap(send, "seq", count, 1)
    pays = join_pair(keep, recv, levels)
    got = [swap(pays[d.bit_length() - 1], "seq", count, 2 * d) for d in range(1, chips)]
    own, away = scan_chips(keep, recv, got)
    return own, swap(away, "seq", count, 1)


def edges_by_gather(keep, count):
    place = lax.axis_index("seq")
    gathered = lax.all_gather(keep, "seq")
    product = functools.partial(jnp.einsum, "hij,hjk->hik", precision=HIGH)

    def take(j):
        return lax.dynamic_index_in_dim(gathered, j, 0, False).astype(F32)

    def forward(j, state):
        part = take(j)
        return product(part[:, 0], state) + part[:, 1]

    def backward(i, state):
        part = take(count - 1 - i)
        return product(state, part[:, 0]) + part[:, 2]

    vacant = jnp.zeros(keep.shape[:1] + keep.shape[2:], F32)
    enter = lax.fori_loop(0, place, forward, vacant)
    leave = lax.fori_loop(0, count - 1 - place, backward, vacant)
    own = jnp.stack([enter, leave], axis=1).astype(BF16)
    return own, own


def sum_over_heads(blocks):
    count = lax.axis_size("head")
    right = left = None
    for turn in range(count - 1):
        onward = blocks[count - 1 - turn]
        back = blocks[turn + 1]
        if turn:
            onward = onward + right.astype(F32)
            back = back + left.astype(F32)
        right = lax.ppermute(
            onward.astype(BF16), "head", [(i, i + 1) for i in range(min(turn + 1, count - 1))]
        )
        left = lax.ppermute(
            back.astype(BF16), "head", [(count - 1 - i, count - 2 - i) for i in range(min(turn + 1, count - 1))]
        )
    total = blocks[0]
    if count > 1:
        total = total + right.astype(F32) + left.astype(F32)
    return total.astype(BF16)


def on_device(tokens, qkv_weight, beta_logit, log_decay, out_grad):
    heads = beta_logit.shape[0]
    count = lax.axis_size("seq")
    paired = heads % 2 == 0 and count > 2 and count & (count - 1) == 0 and count <= 8
    half = heads // 2 if paired else 0
    proj, u, wk, dbt, ktt, keep, send = prepare(
        tokens, qkv_weight, beta_logit, log_decay, out_grad, half
    )
    if paired:
        own, recv = edges_by_pairs(keep, send, count)
    else:
        own, recv = edges_by_gather(keep, count)
    blocks = finish(
        qkv_weight, proj, u, wk, dbt, ktt, beta_logit, log_decay, out_grad, own, recv, half
    )
    return sum_over_heads(blocks)


def solution(mesh):
    return jax.shard_map(
        on_device,
        mesh=mesh,
        in_specs=(
            P("seq", None),
            P(None, None, "head"),
            P("head", "seq"),
            P("head", "seq"),
            P("seq", "head"),
        ),
        out_specs=P("seq", "head"),
        check_vma=False,
    )
```

time: 745 us -> 84 us (0.11)
  other arithmetic: 425 us -> 2.67 us
  matrix products: 130 us -> 0 us
  waiting for transfers between devices: 119 us -> 26.7 us
  local copies, waits for them, and re-layouts: 53.4 us -> 3.42 us
  Pallas kernels: 0 us -> 27.1 us
  starting transfers between devices: 0.08 us -> 23.7 us
  between operations: 13.6 us -> 0.08 us
    another operation x87 -> x0, other arithmetic: 409 us -> none  [the longest x72 406 us: block_step(): jax.scipy.linalg.solve_triangular(system, target, lower=True, unit_diagon...]
    dot_general x116 -> x0, matrix products: 117 us -> none  [the longest x100 92.4 us: product(): return jnp.dot(left, right, precision=HIGH)]
    all_gather x2 -> x0, waiting for transfers between devices: 62.6 us -> none  [prefix(): gathered = lax.all_gather(part, axis)]
    reduce_scatter x1 -> x0, waiting for transfers between devices: 56.1 us -> none  [on_device(): lax.psum_scatter(partial_sums, 'head', scatter_dimension=1, tiled=True)]
    pallas_call x0 -> x4, Pallas kernels: none -> 27.1 us  [the longest x1 11.4 us: prepare(): pl.pallas_call(functools.partial(prepare_kernel, heads, half), grid=(memb...]
    ppermute x0 -> x11, waiting for transfers between devices: none -> 26.7 us  [the longest x3 12 us: sum_over_heads(): lax.ppermute(onward.astype(BF16), 'head', [(i, i + 1) for i in range(min(...]
    ppermute x0 -> x11, starting transfers between devices: none -> 23.7 us  [the longest x3 16.2 us: sum_over_heads(): lax.ppermute(onward.astype(BF16), 'head', [(i, i + 1) for i in range(min(...]
    dot_general x4 -> x0, local copies, waits for them, and re-layouts: 17.6 us -> none  [on_device(): jnp.dot(tokens, qkv_weight[member], preferred_element_type=jnp.float32)]
  transfers between devices with their start and end apart: 3 -> 11, of which waited for: 3 -> 9; matrix products, arithmetic and copies ran while one was open for 2% -> 1% of each run, Pallas kernels for 0% -> 0%
where the time goes in v1:
time: 84 us; the launch traced here: 83.6 us
  Pallas kernels  27.1 us (32%)
  waiting for transfers between devices  26.7 us (32%)
  starting transfers between devices  23.7 us (28%)
  local copies, waits for them, and re-layouts  3.42 us (4%)
  other arithmetic  2.67 us (3%)
    ppermute x3, starting transfers between devices, sum_over_heads(): lax.ppermute(onward.astype(BF16), 'head', [(i, i + 1) for i in range(min(...  16.2 us
    ppermute x3, waiting for transfers between devices, sum_over_heads(): lax.ppermute(onward.astype(BF16), 'head', [(i, i + 1) for i in range(min(...  12 us
    pallas_call x1, Pallas kernels, prepare(): pl.pallas_call(functools.partial(prepare_kernel, heads, half), grid=(memb...  11.4 us
    ppermute x5, waiting for transfers between devices, swap(): return lax.ppermute(value, axis, [(i, i ^ mask) for i in range(count)])  10.3 us
    pallas_call x1, Pallas kernels, finish(): pl.pallas_call(functools.partial(finish_kernel, heads, half), grid_spec=p...  10.2 us
    ppermute x5, starting transfers between devices, swap(): return lax.ppermute(value, axis, [(i, i ^ mask) for i in range(count)])  4.87 us
    ppermute x3, waiting for transfers between devices, sum_over_heads(): lax.ppermute(back.astype(BF16), 'head', [(count - 1 - i, count - 2 - i) f...  4.41 us
    pallas_call x1, Pallas kernels, scan_chips(): pl.pallas_call(functools.partial(scan_kernel, chips), out_shape=[shape, s...  3.16 us
  transfers between devices with their start and end apart: 11, of which 9 were waited for; matrix products, arithmetic and copies ran while one was open for 1% of the time, Pallas kernels for 0%

profile of v1, /device:TPU:0, one launch (start us, length us, event | category | flops | bytes accessed | tf_op | source)
XLA Modules:
  0.0 83.6 jit_solution(10740362981438605974)
XLA Ops:
  0.0 11.4 %prepare.1 = (f32[2,256,512]{2,1,0:T(8,128)}, f32[4,256,128]{2,1,0:T(8,128)}, bf16[4,256,128]{2,1,0:T(8,128)(2,1)}, f32[4,128,256]{2,1,0:T(8,128)}, bf16[4,128,2...) custom-call(bf16[256,2048]{1,0:T(8,128)(2,1)} %tok_ref.1, ...), custom_call_target="tpu_custom_call" | custom-call | tf_op jit(solution)/shard_map/prepare/pallas_call | solution.py:161
  11.4 0.5 collective-permute-start
  11.9 1.3 %collective-permute-done.recv_ref = bf16[2,3,128,128]{3,2,1,0:T(8,128)(2,1)S(1)} collective-permute-done((bf16[2,3,128,128]{3,2,1,0:T(8,128)(2,1)}, bf16[2,3,128,128]{3,2,1,0:T(8,128)(2,1)S(1)}, u32[]{:S(2)}, u32[]{:S(2)}) %collective-permute-start) | collective-permute-done | bytes 196640 | tf_op jit(solution)/shard_map/ppermute | solution.py:379
  13.2 0.0 copy-start.1
  13.2 0.7 copy-done.1
  13.9 2.2 %join_pair.1 = (bf16[2,2,128,128]{3,2,1,0:T(8,128)(2,1)}, bf16[2,2,128,128]{3,2,1,0:T(8,128)(2,1)}) custom-call(bf16[2,3,128,128]{3,2,1,0:T(8,128)(2,1)} %get-tuple-element.21.keep_ref, bf16[2,3,128,128]{3,2,1,0:T(8,128)(2,1)} %copy-done.1), custom_call_target="tpu_custom_call" | custom-call | tf_op jit(solution)/shard_map/join_pair/pallas_call | solution.py:218
  16.1 2.8 %collective-permute-start.1 = (bf16[2,2,128,128]{3,2,1,0:T(8,128)(2,1)}, bf16[2,2,128,128]{3,2,1,0:T(8,128)(2,1)S(1)}, u32[]{:S(2)}, u32[]{:S(2)}) collective-permute-start(bf16[2,2,128,128]{3,2,1,0:T(8,128)(2,1)} %get-tuple-element.23), channel_id=1, source_target_pairs={{0,8},{4,12},{8,0},{12,4},{16,24},{20,28},{24,16},{28,20},{1,9},{5... | collective-permute-start | bytes 393224 | tf_op jit(solution)/shard_map/ppermute | solution.py:379
  19.0 1.5 %collective-permute-start.3 = (bf16[2,2,128,128]{3,2,1,0:T(8,128)(2,1)}, bf16[2,2,128,128]{3,2,1,0:T(8,128)(2,1)S(1)}, u32[]{:S(2)}, u32[]{:S(2)}) collective-permute-start(bf16[2,2,128,128]{3,2,1,0:T(8,128)(2,1)} %get-tuple-element.24), channel_id=1, source_target_pairs={{0,24},{4,28},{8,16},{12,20},{16,8},{20,12},{24,0},{28,4},{1,25},{... | collective-permute-start | bytes 393224 | tf_op jit(solution)/shard_map/ppermute | solution.py:379
  20.5 0.0 collective-permute-start.2
  20.5 2.9 %collective-permute-done.1.refs_0_ = bf16[2,2,128,128]{3,2,1,0:T(8,128)(2,1)S(1)} collective-permute-done((bf16[2,2,128,128]{3,2,1,0:T(8,128)(2,1)}, bf16[2,2,128,128]{3,2,1,0:T(8,128)(2,1)S(1)}, u32[]{:S(2)}, u32[]{:S(2)}) %collective-permute-start.1) | collective-permute-done | bytes 131104 | tf_op jit(solution)/shard_map/ppermute | solution.py:379
  23.3 0.0 copy-start.3
  23.4 3.7 %collective-permute-done.3.refs_2_ = bf16[2,2,128,128]{3,2,1,0:T(8,128)(2,1)S(1)} collective-permute-done((bf16[2,2,128,128]{3,2,1,0:T(8,128)(2,1)}, bf16[2,2,128,128]{3,2,1,0:T(8,128)(2,1)S(1)}, u32[]{:S(2)}, u32[]{:S(2)}) %collective-permute-start.3) | collective-permute-done | bytes 131104 | tf_op jit(solution)/shard_map/ppermute | solution.py:379
  27.1 0.0 copy-start.4
  27.1 1.4 %collective-permute-done.2.refs_1_ = bf16[2,2,128,128]{3,2,1,0:T(8,128)(2,1)S(1)} collective-permute-done((bf16[2,2,128,128]{3,2,1,0:T(8,128)(2,1)}, bf16[2,2,128,128]{3,2,1,0:T(8,128)(2,1)S(1)}, u32[]{:S(2)}, u32[]{:S(2)}) %collective-permute-start.2) | collective-permute-done | bytes 131104 | tf_op jit(solution)/shard_map/ppermute | solution.py:379
  28.5 0.0 copy-done.3
  28.5 0.0 copy-done.4
  28.5 0.0 copy-start.5
  28.5 0.7 copy-done.5
  29.1 3.2 %scan_chips.1 = (bf16[2,2,128,128]{3,2,1,0:T(8,128)(2,1)}, bf16[2,2,128,128]{3,2,1,0:T(8,128)(2,1)}) custom-call(bf16[2,3,128,128]{3,2,1,0:T(8,128)(2,1)} %get-tuple-element.21.keep_ref, bf16[2,3,128,128]{3,2,1,0:T(8,128)(2,1)} %copy-done.1, bf16[2,2,128,128]{3,2,1,0:T(8,128)(2,1)} %copy-done.3, bf16[2,2,128,128]{3,2,1,0:T(8,128)(2,1)} %copy-done.5, ...), custom_call_target="tpu_custom_call" | custom-call | tf_op jit(solution)/shard_map/scan_chips/pallas_call | solution.py:266
  32.3 0.0 collective-permute-start.4
  32.3 0.5 compare_select_fusion.order_ref
  32.8 1.0 %collective-permute-done.4.recv_ref = bf16[2,2,128,128]{3,2,1,0:T(8,128)(2,1)S(1)} collective-permute-done((bf16[2,2,128,128]{3,2,1,0:T(8,128)(2,1)}, bf16[2,2,128,128]{3,2,1,0:T(8,128)(2,1)S(1)}, u32[]{:S(2)}, u32[]{:S(2)}) %collective-permute-start.4) | collective-permute-done | bytes 131104 | tf_op jit(solution)/shard_map/ppermute | solution.py:379
  33.8 0.0 copy-start.2
  33.8 0.7 copy-done.2
  34.5 10.2 %finish.1 = f32[4,256,512]{2,1,0:T(8,128)} custom-call(s32[4]{0:T(128)} %compare_select_fusion.order_ref, bf16[3,2048,512]{2,1,0:T(8,128)(2,1)} %w_ref.3, f32[2,256,512]{2,1,0:T(8,128)} %get-tuple-element.16.proj_ref, f32[4,256,128]{2,1,0:T(8,128)} %get-tuple-element.17.u_ref, bf16[4,256,128]{2,1,0:T(8,128)(2,1)} %get-tuple-element.18.wk_ref, ...), custom_call_target="tpu_custom_call" | custom-call | tf_op jit(solution)/shard_map/finish/pallas_call | solution.py:349
  44.8 0.0 copy-start
  44.8 1.4 %fusion.4 = (bf16[256,512]{1,0:T(8,128)(2,1)S(1)}, bf16[256,512]{1,0:T(8,128)(2,1)S(1)}) fusion(f32[4,256,512]{2,1,0:T(8,128)} %finish.1), kind=kLoop, calls=%fused_computation.12 | loop fusion | bytes 1048576 | tf_op jit(solution)/shard_map/convert_element_type | solution.py:425
  46.2 3.5 %collective-permute-start.5 = (bf16[256,512]{1,0:T(8,128)(2,1)S(1)}, bf16[256,512]{1,0:T(8,128)(2,1)S(1)}, u32[]{:S(2)}, u32[]{:S(2)}) collective-permute-start(bf16[256,512]{1,0:T(8,128)(2,1)S(1)} %get-tuple-element.31), channel_id=1, source_target_pairs={{0,1},{4,5},{8,9},{12,13},{16,17},{20,21},{24,25},{28,29}} | collective-permute-start | bytes 786440 | tf_op jit(solution)/shard_map/ppermute | solution.py:424
  49.7 0.7 collective-permute-start.8
  50.4 5.2 %collective-permute-done.5 = bf16[256,512]{1,0:T(8,128)(2,1)S(1)} collective-permute-done((bf16[256,512]{1,0:T(8,128)(2,1)S(1)}, bf16[256,512]{1,0:T(8,128)(2,1)S(1)}, u32[]{:S(2)}, u32[]{:S(2)}) %collective-permute-start.5) | collective-permute-done | bytes 262176 | tf_op jit(solution)/shard_map/ppermute | solution.py:424
  55.5 0.0 collective-permute-done.8
  55.5 1.2 %add_convert_fusion.3 = (bf16[256,512]{1,0:T(8,128)(2,1)S(1)}, bf16[256,512]{1,0:T(8,128)(2,1)S(1)}) fusion(bf16[256,512]{1,0:T(8,128)(2,1)S(1)} %collective-permute-done.5, f32[4,256,512]{2,1,0:T(8,128)} %finish.1, bf16[256,512]{1,0:T(8,128)(2,1)S(1)} %collective-permute-done.8), kind=kLoop, calls=%fused_computation.10 | loop fusion | flops 786432 | bytes 1572864 | tf_op jit(solution)/shard_map/convert_element_type | solution.py:425
  56.7 4.4 %collective-permute-start.6 = (bf16[256,512]{1,0:T(8,128)(2,1)S(1)}, bf16[256,512]{1,0:T(8,128)(2,1)S(1)}, u32[]{:S(2)}, u32[]{:S(2)}) collective-permute-start(bf16[256,512]{1,0:T(8,128)(2,1)S(1)} %get-tuple-element.29), channel_id=1, source_target_pairs={{0,1},{1,2},{4,5},{5,6},{8,9},{9,10},{12,13},{13,14},{16,17},{17,1... | collective-permute-start | bytes 786440 | tf_op jit(solution)/shard_map/ppermute | solution.py:424
  61.1 0.7 collective-permute-start.9
  61.8 4.3 %collective-permute-done.6 = bf16[256,512]{1,0:T(8,128)(2,1)S(1)} collective-permute-done((bf16[256,512]{1,0:T(8,128)(2,1)S(1)}, bf16[256,512]{1,0:T(8,128)(2,1)S(1)}, u32[]{:S(2)}, u32[]{:S(2)}) %collective-permute-start.6) | collective-permute-done | bytes 262176 | tf_op jit(solution)/shard_map/ppermute | solution.py:424
  66.1 0.0 collective-permute-done.9
  66.1 0.0 copy-done
  66.1 0.2 add_convert_fusion.2
  66.2 8.3 %collective-permute-start.7 = (bf16[256,512]{1,0:T(8,128)(2,1)S(1)}, bf16[256,512]{1,0:T(8,128)(2,1)S(1)}, u32[]{:S(2)}, u32[]{:S(2)}) collective-permute-start(bf16[256,512]{1,0:T(8,128)(2,1)S(1)} %get-tuple-element.27), channel_id=1, source_target_pairs={{0,1},{1,2},{2,3},{4,5},{5,6},{6,7},{8,9},{9,10},{10,11},{12,13},{... | collective-permute-start | bytes 786440 | tf_op jit(solution)/shard_map/ppermute | solution.py:424
  74.5 1.3 %collective-permute-start.10 = (bf16[256,512]{1,0:T(8,128)(2,1)S(1)}, bf16[256,512]{1,0:T(8,128)(2,1)S(1)}, u32[]{:S(2)}, u32[]{:S(2)}) collective-permute-start(bf16[256,512]{1,0:T(8,128)(2,1)S(1)} %get-tuple-element.28), channel_id=1, source_target_pairs={{3,2},{2,1},{1,0},{7,6},{6,5},{5,4},{11,10},{10,9},{9,8},{15,14},{... | collective-permute-start | bytes 786440 | tf_op jit(solution)/shard_map/ppermute | solution.py:427
  75.8 2.6 %collective-permute-done.7 = bf16[256,512]{1,0:T(8,128)(2,1)S(1)} collective-permute-done((bf16[256,512]{1,0:T(8,128)(2,1)S(1)}, bf16[256,512]{1,0:T(8,128)(2,1)S(1)}, u32[]{:S(2)}, u32[]{:S(2)}) %collective-permute-start.7) | collective-permute-done | bytes 262176 | tf_op jit(solution)/shard_map/ppermute | solution.py:424
  78.4 4.4 %collective-permute-done.10 = bf16[256,512]{1,0:T(8,128)(2,1)S(1)} collective-permute-done((bf16[256,512]{1,0:T(8,128)(2,1)S(1)}, bf16[256,512]{1,0:T(8,128)(2,1)S(1)}, u32[]{:S(2)}, u32[]{:S(2)}) %collective-permute-start.10) | collective-permute-done | bytes 262176 | tf_op jit(solution)/shard_map/ppermute | solution.py:427
  82.8 0.8 fusion.2
Async XLA Ops:
  11.4 1.8 %collective-permute-start = (bf16[2,3,128,128]{3,2,1,0:T(8,128)(2,1)}, bf16[2,3,128,128]{3,2,1,0:T(8,128)(2,1)S(1)}, u32[]{:S(2)}, u32[]{:S(2)}) collective-permute-start(bf16[2,3,128,128]{3,2,1,0:T(8,128)(2,1)} %get-tuple-element.22), channel_id=1, source_target_pairs={{0,4},{4,0},{8,12},{12,8},{16,20},{20,16},{24,28},{28,24},{1,5},{5... | collective-permute-start | bytes 589832 | tf_op jit(solution)/shard_map/ppermute | solution.py:379
  13.2 0.7 copy-start.1
  16.1 7.2 %collective-permute-start.1 = (bf16[2,2,128,128]{3,2,1,0:T(8,128)(2,1)}, bf16[2,2,128,128]{3,2,1,0:T(8,128)(2,1)S(1)}, u32[]{:S(2)}, u32[]{:S(2)}) collective-permute-start(bf16[2,2,128,128]{3,2,1,0:T(8,128)(2,1)} %get-tuple-element.23), channel_id=1, source_target_pairs={{0,8},{4,12},{8,0},{12,4},{16,24},{20,28},{24,16},{28,20},{1,9},{5... | collective-permute-start | bytes 393224 | tf_op jit(solution)/shard_map/ppermute | solution.py:379
  19.0 8.1 %collective-permute-start.3 = (bf16[2,2,128,128]{3,2,1,0:T(8,128)(2,1)}, bf16[2,2,128,128]{3,2,1,0:T(8,128)(2,1)S(1)}, u32[]{:S(2)}, u32[]{:S(2)}) collective-permute-start(bf16[2,2,128,128]{3,2,1,0:T(8,128)(2,1)} %get-tuple-element.24), channel_id=1, source_target_pairs={{0,24},{4,28},{8,16},{12,20},{16,8},{20,12},{24,0},{28,4},{1,25},{... | collective-permute-start | bytes 393224 | tf_op jit(solution)/shard_map/ppermute | solution.py:379
  20.5 8.0 %collective-permute-start.2 = (bf16[2,2,128,128]{3,2,1,0:T(8,128)(2,1)}, bf16[2,2,128,128]{3,2,1,0:T(8,128)(2,1)S(1)}, u32[]{:S(2)}, u32[]{:S(2)}) collective-permute-start(bf16[2,2,128,128]{3,2,1,0:T(8,128)(2,1)} %get-tuple-element.24), channel_id=1, source_target_pairs={{0,16},{4,20},{8,24},{12,28},{16,0},{20,4},{24,8},{28,12},{1,17},{... | collective-permute-start | bytes 393224 | tf_op jit(solution)/shard_map/ppermute | solution.py:379
  23.3 5.1 %copy-start.3 = (bf16[2,2,128,128]{3,2,1,0:T(8,128)(2,1)}, bf16[2,2,128,128]{3,2,1,0:T(8,128)(2,1)S(1)}, u32[]{:S(2)}) copy-start(bf16[2,2,128,128]{3,2,1,0:T(8,128)(2,1)S(1)} %collective-permute-done.1.refs_0_) | copy-start | bytes 393220
  27.1 1.4 %copy-start.4 = (bf16[2,2,128,128]{3,2,1,0:T(8,128)(2,1)}, bf16[2,2,128,128]{3,2,1,0:T(8,128)(2,1)S(1)}, u32[]{:S(2)}) copy-start(bf16[2,2,128,128]{3,2,1,0:T(8,128)(2,1)S(1)} %collective-permute-done.3.refs_2_) | copy-start | bytes 393220
  28.5 0.7 copy-start.5
  32.3 1.6 %collective-permute-start.4 = (bf16[2,2,128,128]{3,2,1,0:T(8,128)(2,1)}, bf16[2,2,128,128]{3,2,1,0:T(8,128)(2,1)S(1)}, u32[]{:S(2)}, u32[]{:S(2)}) collective-permute-start(bf16[2,2,128,128]{3,2,1,0:T(8,128)(2,1)} %get-tuple-element.26), channel_id=1, source_target_pairs={{0,4},{4,0},{8,12},{12,8},{16,20},{20,16},{24,28},{28,24},{1,5},{5... | collective-permute-start | bytes 393224 | tf_op jit(solution)/shard_map/ppermute | solution.py:379
  33.8 0.7 copy-start.2
  44.8 21.3 %copy-start = (f32[4,256,512]{2,1,0:T(8,128)S(1)}, f32[4,256,512]{2,1,0:T(8,128)}, u32[]{:S(2)}) copy-start(f32[4,256,512]{2,1,0:T(8,128)} %finish.1) | copy-start | bytes 6291460
  46.2 9.3 %collective-permute-start.5 = (bf16[256,512]{1,0:T(8,128)(2,1)S(1)}, bf16[256,512]{1,0:T(8,128)(2,1)S(1)}, u32[]{:S(2)}, u32[]{:S(2)}) collective-permute-start(bf16[256,512]{1,0:T(8,128)(2,1)S(1)} %get-tuple-element.31), channel_id=1, source_target_pairs={{0,1},{4,5},{8,9},{12,13},{16,17},{20,21},{24,25},{28,29}} | collective-permute-start | bytes 786440 | tf_op jit(solution)/shard_map/ppermute | solution.py:424
  49.7 5.8 %collective-permute-start.8 = (bf16[256,512]{1,0:T(8,128)(2,1)S(1)}, bf16[256,512]{1,0:T(8,128)(2,1)S(1)}, u32[]{:S(2)}, u32[]{:S(2)}) collective-permute-start(bf16[256,512]{1,0:T(8,128)(2,1)S(1)} %get-tuple-element.32), channel_id=1, source_target_pairs={{3,2},{7,6},{11,10},{15,14},{19,18},{23,22},{27,26},{31,30}} | collective-permute-start | bytes 786440 | tf_op jit(solution)/shard_map/ppermute | solution.py:427
  56.7 9.4 %collective-permute-start.6 = (bf16[256,512]{1,0:T(8,128)(2,1)S(1)}, bf16[256,512]{1,0:T(8,128)(2,1)S(1)}, u32[]{:S(2)}, u32[]{:S(2)}) collective-permute-start(bf16[256,512]{1,0:T(8,128)(2,1)S(1)} %get-tuple-element.29), channel_id=1, source_target_pairs={{0,1},{1,2},{4,5},{5,6},{8,9},{9,10},{12,13},{13,14},{16,17},{17,1... | collective-permute-start | bytes 786440 | tf_op jit(solution)/shard_map/ppermute | solution.py:424
  61.1 5.0 %collective-permute-start.9 = (bf16[256,512]{1,0:T(8,128)(2,1)S(1)}, bf16[256,512]{1,0:T(8,128)(2,1)S(1)}, u32[]{:S(2)}, u32[]{:S(2)}) collective-permute-start(bf16[256,512]{1,0:T(8,128)(2,1)S(1)} %get-tuple-element.30), channel_id=1, source_target_pairs={{3,2},{2,1},{7,6},{6,5},{11,10},{10,9},{15,14},{14,13},{19,18},{18... | collective-permute-start | bytes 786440 | tf_op jit(solution)/shard_map/ppermute | solution.py:427
  66.2 12.2 %collective-permute-start.7 = (bf16[256,512]{1,0:T(8,128)(2,1)S(1)}, bf16[256,512]{1,0:T(8,128)(2,1)S(1)}, u32[]{:S(2)}, u32[]{:S(2)}) collective-permute-start(bf16[256,512]{1,0:T(8,128)(2,1)S(1)} %get-tuple-element.27), channel_id=1, source_target_pairs={{0,1},{1,2},{2,3},{4,5},{5,6},{6,7},{8,9},{9,10},{10,11},{12,13},{... | collective-permute-start | bytes 786440 | tf_op jit(solution)/shard_map/ppermute | solution.py:424
  74.5 8.3 %collective-permute-start.10 = (bf16[256,512]{1,0:T(8,128)(2,1)S(1)}, bf16[256,512]{1,0:T(8,128)(2,1)S(1)}, u32[]{:S(2)}, u32[]{:S(2)}) collective-permute-start(bf16[256,512]{1,0:T(8,128)(2,1)S(1)} %get-tuple-element.28), channel_id=1, source_target_pairs={{3,2},{2,1},{1,0},{7,6},{6,5},{5,4},{11,10},{10,9},{9,8},{15,14},{... | collective-permute-start | bytes 786440 | tf_op jit(solution)/shard_map/ppermute | solution.py:427

commit v2 on v0

v2 whole, which is shorter than its diff:
```python
import functools

import jax
import jax.numpy as jnp
from jax import lax
from jax.experimental import pallas as pl
from jax.experimental.pallas import tpu as pltpu
from jax.sharding import PartitionSpec as P

F32 = jnp.float32
BF16 = jnp.bfloat16
HIGH = lax.Precision.HIGHEST
FAR = -1e30


def nn(a, b):
    return lax.dot_general(a, b, (((1,), (0,)), ((), ())), preferred_element_type=F32)


def nt(a, b):
    return lax.dot_general(a, b, (((1,), (1,)), ((), ())), preferred_element_type=F32)


def fine(a, b, dims=(1, 0)):
    return lax.dot_general(
        a, b, (((dims[0],), (dims[1],)), ((), ())), precision=HIGH, preferred_element_type=F32
    )


def grid_ids(size):
    rows = lax.broadcasted_iota(jnp.int32, (size, size), 0)
    cols = lax.broadcasted_iota(jnp.int32, (size, size), 1)
    return rows, cols


def exact_terms(value):
    high = value.astype(BF16)
    left = value - high.astype(F32)
    mid = left.astype(BF16)
    return high, mid, (left - mid.astype(F32)).astype(BF16)


def gates(logit, decay):
    heads, size = decay.shape
    rows, cols = grid_ids(size)
    upper = jnp.where(rows <= cols, 1.0, 0.0).astype(BF16)
    high, mid, low = exact_terms(decay)
    run = nn(high, upper) + nn(mid, upper) + nn(low, upper)
    lanes = [run, 1.0 / (1.0 + jnp.exp(-logit))]
    spare = -2 * heads % 8
    if spare:
        lanes.append(jnp.zeros((spare, size), F32))
    lanes = jnp.concatenate(lanes, axis=0)
    return lanes, lanes.T


def unit_rows(tensor):
    scale = lax.rsqrt(jnp.sum(tensor * tensor, axis=-1, keepdims=True) + 1e-06)
    return tensor * scale, scale


def unit_lower_inverse(couplings):
    size = couplings[0].shape[0]
    base = size // 4
    lane_block = lax.broadcasted_iota(jnp.int32, (base, size), 1) // base
    on = [lane_block == b for b in range(4)]
    odd = lane_block % 2 == 1
    masks = [jnp.where(o, 1.0, 0.0).astype(BF16) for o in on]
    none = jnp.zeros((base, size), BF16)

    def strip(a, b):
        return a[b * base : (b + 1) * base]

    def spread(x):
        return jnp.concatenate([x * m for m in masks], axis=0)

    flat = [sum(jnp.where(on[b], strip(a, b), 0.0) for b in range(4)) for a in couplings]
    rest = [-x for x in flat]
    power = flat
    reach = 1
    while 2 * reach < base:
        narrow = [p.astype(BF16) for p in power]
        if reach == 1:
            power = [nn(p, spread(p)) for p in narrow]
        else:
            both = [
                nn(jnp.concatenate([n.astype(BF16), p], axis=0), spread(p))
                for n, p in zip(rest, narrow)
            ]
            rest = [n + p + x[:base] for n, p, x in zip(rest, power, both)]
            power = [x[base:] for x in both]
        reach *= 2
    if reach > 1:
        narrow = [p.astype(BF16) for p in power]
        rest = [n + p + nn(n.astype(BF16), spread(b)) for n, p, b in zip(rest, power, narrow)]

    outer = [jnp.where(on[0], strip(a, 1), 0.0) + jnp.where(on[2], strip(a, 3), 0.0) for a in couplings]
    wide = [n.astype(BF16) for n in rest]
    half = [g + nn(g.astype(BF16), spread(n)) for g, n in zip(outer, wide)]
    half_b = [y.astype(BF16) for y in half]
    late = [jnp.where(odd, n, 0.0) for n in rest]
    cross = [
        y + nn(l.astype(BF16), jnp.concatenate([none, b * masks[0], none, b * masks[2]], axis=0))
        for y, l, b in zip(half, late, half_b)
    ]
    below = [l - z for l, z in zip(late, cross)]
    above = [jnp.where(odd, 0.0, n) for n in rest]
    mid = size // 2
    early = [jnp.concatenate([t[:, :mid], b[:, :mid]], axis=0).astype(BF16) for t, b in zip(above, below)]
    later = [jnp.concatenate([t[:, mid:], b[:, mid:]], axis=0).astype(BF16) for t, b in zip(above, below)]
    corner = [a[mid:, :mid] for a in couplings]
    half = [c + nn(c.astype(BF16), e) for c, e in zip(corner, early)]
    cross = [y + nn(l, y.astype(BF16)) for y, l in zip(half, later)]
    blank = jnp.zeros((mid, mid), BF16)
    return [
        jnp.concatenate(
            [
                jnp.concatenate([e, blank], axis=1),
                jnp.concatenate([(-z).astype(BF16), l], axis=1),
            ],
            axis=0,
        )
        for e, z, l in zip(early, cross, later)
    ]


def prepare_kernel(
    half, pieces, tok_hbm, w_hbm, logit_ref, decay_ref, og_ref,
    unit_ref, scale_ref, lane_ref, col_ref, u_ref, wk_ref, dbt_ref, ktt_ref, gt_ref, keep_ref, send_ref,
    tok_scr, w_scr, value_scr, pay_scr, tok_sem, w_sem,
):
    heads, size = decay_ref.shape
    members, depth, columns = w_scr.shape
    width = columns // heads
    chunk = depth // pieces
    members_in_turn = (1, 2, 0)

    def part(i):
        return pl.ds(i * chunk, chunk)

    tok_copies = [
        pltpu.make_async_copy(tok_hbm.at[:, part(i)], tok_scr.at[:, part(i)], tok_sem.at[i])
        for i in range(pieces)
    ]
    w_copies = [
        [
            pltpu.make_async_copy(w_hbm.at[p, part(i)], w_scr.at[p, part(i)], w_sem.at[p, i])
            for i in range(pieces)
        ]
        for p in range(members)
    ]
    for turn, p in enumerate(members_in_turn):
        for i in range(pieces):
            if turn == 0:
                tok_copies[i].start()
            w_copies[p][i].start()

    lanes, cols_of = gates(logit_ref[...], decay_ref[...])
    lane_ref[...] = lanes
    col_ref[...] = cols_of
    every = range(heads)
    spans = [slice(h * width, (h + 1) * width) for h in every]
    for h in every:
        gt_ref[h] = og_ref[:, spans[h]].astype(F32).T.astype(BF16)

    for turn, p in enumerate(members_in_turn):
        total = None
        for i in range(pieces):
            if turn == 0:
                tok_copies[i].wait()
            w_copies[p][i].wait()
            here = slice(i * chunk, (i + 1) * chunk)
            result = nn(tok_scr[:, here], w_scr[p, here])
            total = result if total is None else total + result
        if p == 2:
            value_scr[...] = total
        else:
            for h in every:
                unit, scale = unit_rows(total[:, spans[h]])
                unit_ref[p, :, spans[h]] = unit
                scale_ref[:, p * heads + h : p * heads + h + 1] = scale

    rows, cols = grid_ids(size)
    causal = rows >= cols
    strict = rows > cols
    run_col = [cols_of[:, h : h + 1] for h in every]
    run_row = [lanes[h : h + 1, :] for h in every]
    beta = [cols_of[:, heads + h : heads + h + 1] for h in every]
    keys = [unit_ref[1, :, s] for s in spans]
    key_b = [k.astype(BF16) for k in keys]
    gamma = [jnp.exp(jnp.where(causal, run_col[h] - run_row[h], FAR)) for h in every]
    couplings = [
        jnp.where(strict, beta[h] * gamma[h] * nt(key_b[h], key_b[h]), 0.0) for h in every
    ]
    queries = [unit_ref[0, :, s] for s in spans]
    scores = [(gamma[h] * nt(queries[h].astype(BF16), key_b[h])).astype(BF16) for h in every]
    inverse = unit_lower_inverse(couplings)
    last = [run_col[h][size - 1 : size, :] for h in every]
    open_col = [jnp.exp(run_col[h]) for h in every]
    fade_row = [jnp.exp(last[h] - run_row[h]) for h in every]
    write_key = [beta[h] * open_col[h] * keys[h] for h in every]
    right = [
        jnp.concatenate([beta[h] * value_scr[:, spans[h]], write_key[h]], axis=1) for h in every
    ]
    solved = [right[h] + nn(inverse[h], right[h].astype(BF16)) for h in every]
    fade_t = [keys[h].T * fade_row[h] for h in every]
    left = [jnp.concatenate([nn(gt_ref[h], scores[h]), fade_t[h]], axis=0) for h in every]
    back = [left[h] + nn(left[h].astype(BF16), inverse[h]) for h in every]
    e_rows, e_cols = grid_ids(width)
    for h in every:
        fade_hi = fade_t[h].astype(BF16)
        fade_lo = (fade_t[h] - fade_hi.astype(F32)).astype(BF16)
        solved_hi = solved[h].astype(BF16)
        solved_lo = (solved[h][:, :width] - solved_hi[:, :width].astype(F32)).astype(BF16)
        state = nn(fade_hi, solved_hi)
        fill = state[:, :width] + nn(fade_lo, solved_hi[:, :width]) + nn(fade_hi, solved_lo)
        unit = jnp.where(e_rows == e_cols, jnp.exp(last[h]), 0.0)
        seed = nn(gt_ref[h], (open_col[h] * queries[h]).astype(BF16)) - nn(
            back[h][:width].astype(BF16), write_key[h].astype(BF16)
        )
        pay_scr[h, 0] = (unit - state[:, width:]).astype(BF16)
        pay_scr[h, 1] = fill.astype(BF16)
        pay_scr[h, 2] = seed.astype(BF16)
        u_ref[h] = solved[h][:, :width]
        wk_ref[h] = solved_hi[:, width:]
        dbt_ref[h] = back[h][:width]
        ktt_ref[h] = back[h][width:].astype(BF16)
    if half:
        core = lax.rem(lax.axis_index("seq"), 2)
        keep_ref[...] = pay_scr[pl.ds(core * half, half)]
        send_ref[...] = pay_scr[pl.ds((1 - core) * half, half)]
    else:
        keep_ref[...] = pay_scr[...]
        send_ref[...] = pay_scr[...]


def here():
    return pl.BlockSpec(memory_space=pltpu.VMEM)


def away():
    return pl.BlockSpec(memory_space=pl.ANY)


def limit(mebibytes):
    return pltpu.CompilerParams(vmem_limit_bytes=mebibytes * 2**20)


def prepare(tokens, weights, logit, decay, out_grad, half):
    heads, size = logit.shape
    members, depth, columns = weights.shape
    width = columns // heads
    part = half or heads
    pieces = 4 if depth % 512 == 0 else 1
    gate_rows = 2 * heads + -2 * heads % 8
    shapes = [
        ((2, size, columns), F32),
        ((size, 2 * heads), F32),
        ((gate_rows, size), F32),
        ((size, gate_rows), F32),
        ((heads, size, width), F32),
        ((heads, size, width), BF16),
        ((heads, width, size), F32),
        ((heads, width, size), BF16),
        ((heads, width, size), BF16),
        ((part, 3, width, width), BF16),
        ((part, 3, width, width), BF16),
    ]
    return pl.pallas_call(
        functools.partial(prepare_kernel, half, pieces),
        in_specs=[away(), away(), here(), here(), here()],
        out_specs=[here()] * len(shapes),
        out_shape=[jax.ShapeDtypeStruct(*s) for s in shapes],
        scratch_shapes=[
            pltpu.VMEM((size, depth), BF16),
            pltpu.VMEM((members, depth, columns), BF16),
            pltpu.VMEM((size, columns), F32),
            pltpu.VMEM((heads, 3, width, width), BF16),
            pltpu.SemaphoreType.DMA((pieces,)),
            pltpu.SemaphoreType.DMA((members, pieces)),
        ],
        compiler_params=limit(36),
        name="prepare",
    )(tokens, weights, logit, decay, out_grad)


def weigh_kernel(heads, lane_ref, col_ref, gamma_ref, turned_ref, strong_ref, strong_t_ref):
    size = lane_ref.shape[1]
    rows, cols = grid_ids(size)
    for h in range(heads):
        gap = col_ref[:, h : h + 1] - lane_ref[h : h + 1, :]
        gamma = jnp.exp(jnp.where(rows >= cols, gap, FAR))
        turned = jnp.exp(jnp.where(rows <= cols, -gap, FAR))
        gamma_ref[h] = gamma
        turned_ref[h] = turned
        beta = col_ref[:, heads + h : heads + h + 1]
        beta_row = lane_ref[heads + h : heads + h + 1, :]
        strong_ref[h] = jnp.where(rows > cols, beta * gamma, 0.0)
        strong_t_ref[h] = jnp.where(rows < cols, beta_row * turned, 0.0)


def weigh(lanes, cols, heads):
    size = lanes.shape[1]
    shape = jax.ShapeDtypeStruct((heads, size, size), F32)
    return pl.pallas_call(
        functools.partial(weigh_kernel, heads),
        in_specs=[here()] * 2,
        out_specs=[here()] * 4,
        out_shape=[shape] * 4,
        compiler_params=limit(8),
        name="weigh",
    )(lanes, cols)


def pair_kernel(levels, keep_ref, recv_ref, *pay_refs):
    place = lax.axis_index("seq")
    first = lax.rem(place, 2) == 0
    chip = place // 2

    def join(early, late):
        width = early.shape[-1]
        for h in range(keep_ref.shape[0]):
            ahead = nn(late[h, 0], jnp.concatenate([early[h, 1], early[h, 0]], axis=1))
            up = ahead[:, :width] + late[h, 1].astype(F32)
            down = nn(late[h, 2], early[h, 0]) + early[h, 2].astype(F32)
            joint = ahead[:, width:].astype(BF16)
            for level in range(levels):
                upward = lax.rem(chip // (1 << level), 2) == 0
                pay_refs[level][h, 0] = joint
                pay_refs[level][h, 1] = jnp.where(upward, up, down).astype(BF16)

    @pl.when(first)
    def _():
        join(keep_ref, recv_ref)

    @pl.when(jnp.logical_not(first))
    def _():
        join(recv_ref, keep_ref)


def join_pair(keep, recv, levels):
    half, _, width, _ = keep.shape
    shape = jax.ShapeDtypeStruct((half, 2, width, width), BF16)
    return pl.pallas_call(
        functools.partial(pair_kernel, levels),
        in_specs=[here()] * 2,
        out_specs=[here()] * levels,
        out_shape=[shape] * levels,
        compiler_params=limit(8),
        name="join_pair",
    )(keep, recv)


def two_terms(value):
    high = value.astype(BF16)
    return high, (value - high.astype(F32)).astype(BF16)


def scan_kernel(keep_ref, recv_ref, near_ref, far_ref, cross_ref, own_ref, send_ref, enter, leave):
    place = lax.axis_index("seq")
    first = lax.rem(place, 2) == 0
    chip = place // 2
    low = lax.rem(chip, 2) == 1
    high = chip // 2 == 1
    every = range(keep_ref.shape[0])

    def pairs(one, two):
        for h in every:

            @pl.when(high)
            def _():
                enter[h] = nn(two[h, 0], one[h, 1]) + two[h, 1].astype(F32)
                leave[h] = jnp.zeros_like(leave[h])

            @pl.when(jnp.logical_not(high))
            def _():
                leave[h] = nn(two[h, 1], one[h, 0]) + one[h, 1].astype(F32)
                enter[h] = jnp.zeros_like(enter[h])

    @pl.when(low)
    def _():
        pairs(cross_ref, far_ref)
        for h in every:
            top, rest = two_terms(enter[h])
            enter[h] = nn(near_ref[h, 0], top) + nn(near_ref[h, 0], rest) + near_ref[h, 1].astype(F32)

    @pl.when(jnp.logical_not(low))
    def _():
        pairs(far_ref, cross_ref)
        for h in every:
            top, rest = two_terms(leave[h])
            leave[h] = nn(top, near_ref[h, 0]) + nn(rest, near_ref[h, 0]) + near_ref[h, 1].astype(F32)

    def within(early, late, early_out, late_out):
        for h in every:
            top, rest = two_terms(enter[h])
            back, tail = two_terms(leave[h])
            middle = nn(early[h, 0], top) + nn(early[h, 0], rest) + early[h, 1].astype(F32)
            inner = nn(back, late[h, 0]) + nn(tail, late[h, 0]) + late[h, 2].astype(F32)
            early_out[h, 0] = top
            early_out[h, 1] = inner.astype(BF16)
            late_out[h, 0] = middle.astype(BF16)
            late_out[h, 1] = back

    @pl.when(first)
    def _():
        within(keep_ref, recv_ref, own_ref, send_ref)

    @pl.when(jnp.logical_not(first))
    def _():
        within(recv_ref, keep_ref, send_ref, own_ref)


def scan_chips(keep, recv, near, far, cross):
    half, _, width, _ = keep.shape
    shape = jax.ShapeDtypeStruct((half, 2, width, width), BF16)
    return pl.pallas_call(
        scan_kernel,
        in_specs=[here()] * 5,
        out_specs=[here()] * 2,
        out_shape=[shape] * 2,
        scratch_shapes=[pltpu.VMEM((half, width, width), F32)] * 2,
        compiler_params=limit(8),
        name="scan_chips",
    )(keep, recv, near, far, cross)


def part_at(slot, count):
    place = lax.axis_index("head")
    if count != 4:
        return lax.rem(place + slot + 1, count)
    if slot == 0:
        return 3 - place
    if slot == 3:
        return place
    low, high = ((2, 0), (3, 1)) if slot == 1 else ((1, 3), (0, 2))
    ends = jnp.where(place == 0, low[0], low[1])
    return jnp.where(place < 2, ends, jnp.where(place == 2, high[0], high[1]))


def fetch(w_hbm, w_scr, sem, slot, count):
    step = w_hbm.shape[1] // count
    start = pl.multiple_of(part_at(slot, count) * step, step)
    return pltpu.make_async_copy(w_hbm.at[:, pl.ds(start, step)], w_scr, sem)


def grads_kernel(
    half, count, w_hbm, unit_ref, scale_ref, col_ref, u_ref, wk_ref, dbt_ref, ktt_ref, gt_ref, og_ref,
    gamma_ref, turned_ref, strong_ref, strong_t_ref, own_ref, recv_ref,
    grad_ref, out_ref, w_scr, edge_scr, sem,
):
    heads, size, width = u_ref.shape
    copy = fetch(w_hbm, w_scr, sem, 0, count)
    copy.start()
    if half:
        core = lax.rem(lax.axis_index("seq"), 2)
        edge_scr[pl.ds(core * half, half)] = own_ref[...]
        edge_scr[pl.ds((1 - core) * half, half)] = recv_ref[...]
    else:
        edge_scr[...] = own_ref[...]
    every = range(heads)
    spans = [slice(h * width, (h + 1) * width) for h in every]
    run_col = [col_ref[:, h : h + 1] for h in every]
    beta = [col_ref[:, heads + h : heads + h + 1] for h in every]
    open_col = [jnp.exp(run_col[h]) for h in every]
    fade_col = [jnp.exp(run_col[h][size - 1 : size, :] - run_col[h]) for h in every]
    update = [(u_ref[h] - nn(wk_ref[h], edge_scr[h, 0])).astype(BF16) for h in every]
    delta_t = [dbt_ref[h] + nn(edge_scr[h, 1], ktt_ref[h]) for h in every]
    delta = [d.T for d in delta_t]
    for h in every:
        span = spans[h]
        rows = jnp.concatenate([og_ref[:, span], delta[h].astype(BF16)], axis=0)
        lanes = nt(rows, update[h])
        turned = nn(update[h], jnp.concatenate([gt_ref[h], delta_t[h].astype(BF16)], axis=1))
        attend = (gamma_ref[h] * lanes[:size]).astype(BF16)
        attend_t = (turned_ref[h] * turned[:, :size]).astype(BF16)
        mix = (strong_ref[h] * lanes[size:] + strong_t_ref[h] * turned[:, size:]).astype(BF16)
        edge = nt(rows, edge_scr[h, 0])
        query = unit_ref[0, :, span]
        key = unit_ref[1, :, span]
        key_b = key.astype(BF16)
        dq = open_col[h] * edge[:size] + nn(attend, key_b)
        dk = (
            nn(attend_t, query.astype(BF16))
            - nn(mix, key_b)
            + fade_col[h] * nn(update[h], edge_scr[h, 1])
            - beta[h] * open_col[h] * edge[size:]
        )
        for slot, unit, slope in ((0, query, dq), (1, key, dk)):
            scale = scale_ref[:, slot * heads + h : slot * heads + h + 1]
            along = jnp.sum(unit * slope, axis=-1, keepdims=True)
            grad_ref[slot, :, span] = (scale * (slope - unit * along)).astype(BF16)
        grad_ref[2, :, span] = (beta[h] * delta[h]).astype(BF16)
    copy.wait()
    out_ref[...] = spread_grads(grad_ref, w_scr).astype(out_ref.dtype)


def spread_grads(grad_ref, w_ref):
    total = nt(grad_ref[0], w_ref[0])
    for member in range(1, grad_ref.shape[0]):
        total = total + nt(grad_ref[member], w_ref[member])
    return total


def grads(weights, prepared, out_grad, weighed, own, recv, half):
    unit, scale, col, u, wk, dbt, ktt, gt = prepared
    heads, size, width = u.shape
    members, depth, columns = weights.shape
    count = lax.axis_size("head")
    step = depth // count
    return pl.pallas_call(
        functools.partial(grads_kernel, half, count),
        in_specs=[away()] + [here()] * 15,
        out_specs=[here()] * 2,
        out_shape=[
            jax.ShapeDtypeStruct((members, size, columns), BF16),
            jax.ShapeDtypeStruct((size, step), BF16),
        ],
        scratch_shapes=[
            pltpu.VMEM((members, step, columns), BF16),
            pltpu.VMEM((heads, 2, width, width), BF16),
            pltpu.SemaphoreType.DMA(()),
        ],
        compiler_params=limit(24),
        name="grads",
    )(weights, unit, scale, col, u, wk, dbt, ktt, gt, out_grad, *weighed, own, recv)


def others_kernel(count, w_hbm, grad_ref, *refs):
    outs, (w_scr, sem) = refs[: count - 1], refs[count - 1 :]
    copies = [fetch(w_hbm, w_scr.at[i], sem.at[i], i + 1, count) for i in range(count - 1)]
    for copy in copies:
        copy.start()
    for i, copy in enumerate(copies):
        copy.wait()
        outs[i][...] = spread_grads(grad_ref, w_scr.at[i]).astype(outs[i].dtype)


def others(weights, grad):
    members, depth, columns = weights.shape
    size = grad.shape[1]
    count = lax.axis_size("head")
    step = depth // count
    kinds = [BF16] + [F32] * 2 if count == 4 else [BF16] * (count - 2) + [F32]
    return pl.pallas_call(
        functools.partial(others_kernel, count),
        in_specs=[away(), here()],
        out_specs=[here()] * (count - 1),
        out_shape=[jax.ShapeDtypeStruct((size, step), k) for k in kinds],
        scratch_shapes=[
            pltpu.VMEM((count - 1, members, step, columns), BF16),
            pltpu.SemaphoreType.DMA((count - 1,)),
        ],
        compiler_params=limit(24),
        name="others",
    )(weights, grad)


def swap(value, axis, count, mask):
    return lax.ppermute(value, axis, [(i, i ^ mask) for i in range(count)])


def edges_by_pairs(keep, send, count):
    recv = swap(send, "seq", count, 1)
    low, high = join_pair(keep, recv, 2)
    near = swap(low, "seq", count, 2)
    far = swap(high, "seq", count, 4)
    cross = swap(high, "seq", count, 6)
    own, other = scan_chips(keep, recv, near, far, cross)
    return own, swap(other, "seq", count, 1)


def edges_by_gather(keep, count):
    place = lax.axis_index("seq")
    gathered = lax.all_gather(keep, "seq")
    product = functools.partial(jnp.einsum, "hij,hjk->hik", precision=HIGH)

    def take(j):
        return lax.dynamic_index_in_dim(gathered, j, 0, False).astype(F32)

    def forward(j, state):
        part = take(j)
        return product(part[:, 0], state) + part[:, 1]

    def backward(i, state):
        part = take(count - 1 - i)
        return product(state, part[:, 0]) + part[:, 2]

    vacant = jnp.zeros(keep.shape[:1] + keep.shape[2:], F32)
    enter = lax.fori_loop(0, place, forward, vacant)
    leave = lax.fori_loop(0, count - 1 - place, backward, vacant)
    own = jnp.stack([enter, leave], axis=1).astype(BF16)
    return own, own


def sum_on_line(blocks):
    count = lax.axis_size("head")
    right = left = None
    for turn in range(count - 1):
        onward = blocks[count - 1 - turn]
        back = blocks[turn + 1]
        if turn:
            onward = (onward.astype(F32) + right.astype(F32)).astype(BF16)
            back = (back.astype(F32) + left.astype(F32)).astype(BF16)
        right = lax.ppermute(onward, "head", [(i, i + 1) for i in range(turn + 1)])
        left = lax.ppermute(back, "head", [(count - 1 - i, count - 2 - i) for i in range(turn + 1)])
    total = blocks[0]
    if count > 1:
        total = total + right.astype(F32) + left.astype(F32)
    return total.astype(BF16)


def sum_of_four(end, first, joint, own):
    outer = lax.ppermute(end, "head", [(0, 1), (3, 2)])
    inner = lax.ppermute(end, "head", [(1, 2), (2, 1)])
    ring = lax.ppermute(first, "head", [(0, 2), (2, 3), (3, 1), (1, 0)])
    joint = (joint + outer.astype(F32)).astype(BF16)
    joint = lax.ppermute(joint, "head", [(0, 1), (1, 3), (3, 2), (2, 0)])
    total = own + inner.astype(F32) + ring.astype(F32) + joint.astype(F32)
    return total.astype(BF16)


def on_device(tokens, qkv_weight, beta_logit, log_decay, out_grad):
    heads = beta_logit.shape[0]
    count = lax.axis_size("seq")
    paired = heads % 2 == 0 and count == 8
    half = heads // 2 if paired else 0
    unit, scale, lanes, col, u, wk, dbt, ktt, gt, keep, send = prepare(
        tokens, qkv_weight, beta_logit, log_decay, out_grad, half
    )
    if paired:
        own, recv = edges_by_pairs(keep, send, count)
    else:
        own, recv = edges_by_gather(keep, count)
    weighed = weigh(lanes, col, heads)
    prepared = (unit, scale, col, u, wk, dbt, ktt, gt)
    grad, end = grads(qkv_weight, prepared, out_grad, weighed, own, recv, half)
    rest = others(qkv_weight, grad)
    if lax.axis_size("head") == 4:
        return sum_of_four(end, *rest)
    return sum_on_line([rest[-1], end, *rest[:-1]])


def solution(mesh):
    return jax.shard_map(
        on_device,
        mesh=mesh,
        in_specs=(
            P("seq", None),
            P(None, None, "head"),
            P("head", "seq"),
            P("head", "seq"),
            P("seq", "head"),
        ),
        out_specs=P("seq", "head"),
        check_vma=False,
    )
```

time: 745 us -> 58.5 us (0.08)
  other arithmetic: 425 us -> 0.91 us
  matrix products: 130 us -> 0 us
  waiting for transfers between devices: 119 us -> 22.2 us
  local copies, waits for them, and re-layouts: 53.4 us -> 6.33 us
  Pallas kernels: 0 us -> 14.8 us
  starting transfers between devices: 0.08 us -> 13.9 us
  between operations: 13.6 us -> 0.09 us
    another operation x87 -> x0, other arithmetic: 409 us -> none  [the longest x72 406 us: block_step(): jax.scipy.linalg.solve_triangular(system, target, lower=True, unit_diagon...]
    dot_general x116 -> x0, matrix products: 117 us -> none  [the longest x100 92.4 us: product(): return jnp.dot(left, right, precision=HIGH)]
    all_gather x2 -> x0, waiting for transfers between devices: 62.6 us -> none  [prefix(): gathered = lax.all_gather(part, axis)]
    reduce_scatter x1 -> x0, waiting for transfers between devices: 56.1 us -> none  [on_device(): lax.psum_scatter(partial_sums, 'head', scatter_dimension=1, tiled=True)]
    ppermute x0 -> x9, waiting for transfers between devices: none -> 22.2 us  [the longest x5 9.58 us: swap(): return lax.ppermute(value, axis, [(i, i ^ mask) for i in range(count)])]
    dot_general x4 -> x0, local copies, waits for them, and re-layouts: 17.6 us -> none  [on_device(): jnp.dot(tokens, qkv_weight[member], preferred_element_type=jnp.float32)]
    pallas_call x0 -> x6, Pallas kernels: none -> 14.8 us  [the longest x1 7.17 us: prepare(): pl.pallas_call(functools.partial(prepare_kernel, half, pieces), in_specs=...]
    ppermute x0 -> x9, starting transfers between devices: none -> 13.9 us  [the longest x5 5.07 us: swap(): return lax.ppermute(value, axis, [(i, i ^ mask) for i in range(count)])]
  transfers between devices with their start and end apart: 3 -> 9, of which waited for: 3 -> 8; matrix products, arithmetic and copies ran while one was open for 2% -> 0% of each run, Pallas kernels for 0% -> 5%
where the time goes in v2:
time: 58.5 us; the launch traced here: 58.2 us
  waiting for transfers between devices  22.2 us (38%)
  Pallas kernels  14.8 us (25%)
  starting transfers between devices  13.9 us (24%)
  local copies, waits for them, and re-layouts  6.33 us (11%)
  other arithmetic  0.91 us (2%)
    ppermute x5, waiting for transfers between devices, swap(): return lax.ppermute(value, axis, [(i, i ^ mask) for i in range(count)])  9.58 us
    ppermute x1, waiting for transfers between devices, sum_of_four(): joint = lax.ppermute(joint, 'head', [(0, 1), (1, 3), (3, 2), (2, 0)])  8.02 us
    pallas_call x1, Pallas kernels, prepare(): pl.pallas_call(functools.partial(prepare_kernel, half, pieces), in_specs=...  7.17 us
    unnamed x12, local copies, waits for them, and re-layouts  6.33 us
    ppermute x5, starting transfers between devices, swap(): return lax.ppermute(value, axis, [(i, i ^ mask) for i in range(count)])  5.07 us
    pallas_call x1, Pallas kernels, grads(): pl.pallas_call(functools.partial(grads_kernel, half, count), in_specs=[aw...  3.93 us
    ppermute x1, starting transfers between devices, sum_of_four(): outer = lax.ppermute(end, 'head', [(0, 1), (3, 2)])  3.49 us
    ppermute x1, waiting for transfers between devices, sum_of_four(): ring = lax.ppermute(first, 'head', [(0, 2), (2, 3), (3, 1), (1, 0)])  3.05 us
  transfers between devices with their start and end apart: 9, of which 8 were waited for; matrix products, arithmetic and copies ran while one was open for 0% of the time, Pallas kernels for 5%

profile of v2, /device:TPU:0, one launch (start us, length us, event | category | flops | bytes accessed | tf_op | source)
XLA Modules:
  0.0 58.2 jit_solution(12462024374639910724)
XLA Ops:
  0.0 0.0 copy-start
  0.0 2.8 %copy-done = bf16[3,2048,512]{2,1,0:T(8,128)(2,1)S(1)} copy-done((bf16[3,2048,512]{2,1,0:T(8,128)(2,1)S(1)}, bf16[3,2048,512]{2,1,0:T(8,128)(2,1)}, u32[]{:S(2)}) %copy-start) | copy-done | bytes 6291480
  2.8 0.0 copy-start.2
  2.8 0.9 %copy-done.2 = bf16[256,512]{1,0:T(8,128)(2,1)S(1)} copy-done((bf16[256,512]{1,0:T(8,128)(2,1)S(1)}, bf16[256,512]{1,0:T(8,128)(2,1)}, u32[]{:S(2)}) %copy-start.2) | copy-done | bytes 262168
  3.7 0.0 copy-start.3
  3.7 1.2 %copy-done.3 = bf16[256,2048]{1,0:T(8,128)(2,1)S(1)} copy-done((bf16[256,2048]{1,0:T(8,128)(2,1)S(1)}, bf16[256,2048]{1,0:T(8,128)(2,1)}, u32[]{:S(2)}) %copy-start.3) | copy-done | bytes 1048600
  5.0 0.0 copy-start.4
  5.0 0.7 %copy-done.4 = f32[4,256]{1,0:T(4,128)S(1)} copy-done((f32[4,256]{1,0:T(4,128)S(1)}, f32[4,256]{1,0:T(4,128)}, u32[]{:S(2)}) %copy-start.4) | copy-done | bytes 4120
  5.6 0.0 copy-start.5
  5.7 0.7 %copy-done.5 = f32[4,256]{1,0:T(4,128)S(1)} copy-done((f32[4,256]{1,0:T(4,128)S(1)}, f32[4,256]{1,0:T(4,128)}, u32[]{:S(2)}) %copy-start.5) | copy-done | bytes 4120
  6.3 0.0 copy-start.1
  6.3 7.2 %prepare.1 = (f32[2,256,512]{2,1,0:T(8,128)S(1)}, f32[256,8]{1,0:T(8,128)S(1)}, f32[8,256]{1,0:T(8,128)S(1)}, f32[256,8]{1,0:T(8,128)S(1)}, f32[4,256,128]{2,1,0...) custom-call(bf16[256,2048]{1,0:T(8,128)(2,1)S(1)} %copy-done.3, ...), custom_call_target="tpu_custom_call" | custom-call | tf_op jit(solution)/shard_map/prepare/pallas_call | solution.py:269
  13.5 0.6 collective-permute-start
  14.1 1.1 %collective-permute-done.recv_ref = bf16[2,3,128,128]{3,2,1,0:T(8,128)(2,1)S(1)} collective-permute-done((bf16[2,3,128,128]{3,2,1,0:T(8,128)(2,1)S(1)}, bf16[2,3,128,128]{3,2,1,0:T(8,128)(2,1)S(1)}, u32[]{:S(2)}, u32[]{:S(2)}) %collective-permute-start) | collective-permute-done | bytes 196640 | tf_op jit(solution)/shard_map/ppermute | solution.py:560
  15.2 0.2 join_pair.1
  15.4 2.9 %collective-permute-start.1 = (bf16[2,2,128,128]{3,2,1,0:T(8,128)(2,1)S(1)}, bf16[2,2,128,128]{3,2,1,0:T(8,128)(2,1)S(1)}, u32[]{:S(2)}, u32[]{:S(2)}) collective-permute-start(bf16[2,2,128,128]{3,2,1,0:T(8,128)(2,1)S(1)} %get-tuple-element.44), channel_id=1, source_target_pairs={{0,8},{4,12},{8,0},{12,4},{16,24},{20,28},{24,16},{28,20},{1,9},{5... | collective-permute-start | bytes 393224 | tf_op jit(solution)/shard_map/ppermute | solution.py:560
  18.3 1.5 %collective-permute-start.3 = (bf16[2,2,128,128]{3,2,1,0:T(8,128)(2,1)S(1)}, bf16[2,2,128,128]{3,2,1,0:T(8,128)(2,1)S(1)}, u32[]{:S(2)}, u32[]{:S(2)}) collective-permute-start(bf16[2,2,128,128]{3,2,1,0:T(8,128)(2,1)S(1)} %get-tuple-element.45), channel_id=1, source_target_pairs={{0,24},{4,28},{8,16},{12,20},{16,8},{20,12},{24,0},{28,4},{1,25},{... | collective-permute-start | bytes 393224 | tf_op jit(solution)/shard_map/ppermute | solution.py:560
  19.7 0.1 collective-permute-start.2
  19.8 2.7 %collective-permute-done.1.near_ref = bf16[2,2,128,128]{3,2,1,0:T(8,128)(2,1)S(1)} collective-permute-done((bf16[2,2,128,128]{3,2,1,0:T(8,128)(2,1)S(1)}, bf16[2,2,128,128]{3,2,1,0:T(8,128)(2,1)S(1)}, u32[]{:S(2)}, u32[]{:S(2)}) %collective-permute-start.1) | collective-permute-done | bytes 131104 | tf_op jit(solution)/shard_map/ppermute | solution.py:560
  22.5 3.7 %collective-permute-done.3.cross_ref = bf16[2,2,128,128]{3,2,1,0:T(8,128)(2,1)S(1)} collective-permute-done((bf16[2,2,128,128]{3,2,1,0:T(8,128)(2,1)S(1)}, bf16[2,2,128,128]{3,2,1,0:T(8,128)(2,1)S(1)}, u32[]{:S(2)}, u32[]{:S(2)}) %collective-permute-start.3) | collective-permute-done | bytes 131104 | tf_op jit(solution)/shard_map/ppermute | solution.py:560
  26.2 1.4 %collective-permute-done.2.far_ref = bf16[2,2,128,128]{3,2,1,0:T(8,128)(2,1)S(1)} collective-permute-done((bf16[2,2,128,128]{3,2,1,0:T(8,128)(2,1)S(1)}, bf16[2,2,128,128]{3,2,1,0:T(8,128)(2,1)S(1)}, u32[]{:S(2)}, u32[]{:S(2)}) %collective-permute-start.2) | collective-permute-done | bytes 131104 | tf_op jit(solution)/shard_map/ppermute | solution.py:560
  27.5 0.7 %scan_chips.1 = (bf16[2,2,128,128]{3,2,1,0:T(8,128)(2,1)S(1)}, bf16[2,2,128,128]{3,2,1,0:T(8,128)(2,1)S(1)}) custom-call(bf16[2,3,128,128]{3,2,1,0:T(8,128)(2,1)S(1)} %get-tuple-element.42.keep_ref, bf16[2,3,128,128]{3,2,1,0:T(8,128)(2,1)S(1)} %collective-permute-done.recv_ref, bf16[2,2,128,128]{3,2,1,0:T(8,128)(2,1)S(1)} %collective-permute-done.1.near_ref, ...), custom_call_target="tpu_custom_call" | custom-call | tf_op jit(solution)/shard_map/scan_chips/pallas_call | solution.py:417
  28.2 0.1 collective-permute-start.4
  28.3 0.5 weigh.1
  28.8 0.8 %collective-permute-done.4.recv_ref = bf16[2,2,128,128]{3,2,1,0:T(8,128)(2,1)S(1)} collective-permute-done((bf16[2,2,128,128]{3,2,1,0:T(8,128)(2,1)S(1)}, bf16[2,2,128,128]{3,2,1,0:T(8,128)(2,1)S(1)}, u32[]{:S(2)}, u32[]{:S(2)}) %collective-permute-start.4) | collective-permute-done | bytes 131104 | tf_op jit(solution)/shard_map/ppermute | solution.py:560
  29.6 0.0 copy-done.1
  29.6 3.9 %grads.1 = (bf16[3,256,512]{2,1,0:T(8,128)(2,1)S(1)}, bf16[256,512]{1,0:T(8,128)(2,1)S(1)}) custom-call(bf16[3,2048,512]{2,1,0:T(8,128)(2,1)S(1)} %copy-done.1, f32[2,256,512]{2,1,0:T(8,128)S(1)} %get-tuple-element.29.unit_ref, f32[256,8]{1,0:T(8,128)S(1)} %get-tuple-element.30.scale_ref, f32[256,8]{1,0:T(8,128)S(1)} %get-tuple-element.31.col_ref, ...), custom_call_target="tpu_custom_call" | custom-call | tf_op jit(solution)/shard_map/grads/pallas_call | solution.py:511
  33.6 3.5 %collective-permute-start.7 = (bf16[256,512]{1,0:T(8,128)(2,1)S(1)}, bf16[256,512]{1,0:T(8,128)(2,1)S(1)}, u32[]{:S(2)}, u32[]{:S(2)}) collective-permute-start(bf16[256,512]{1,0:T(8,128)(2,1)S(1)} %get-tuple-element.50), channel_id=1, source_target_pairs={{0,1},{3,2},{4,5},{7,6},{8,9},{11,10},{12,13},{15,14},{16,17},{19,... | collective-permute-start | bytes 786440 | tf_op jit(solution)/shard_map/ppermute | solution.py:614
  37.1 0.7 %collective-permute-start.5 = (bf16[256,512]{1,0:T(8,128)(2,1)S(1)}, bf16[256,512]{1,0:T(8,128)(2,1)S(1)}, u32[]{:S(2)}, u32[]{:S(2)}) collective-permute-start(bf16[256,512]{1,0:T(8,128)(2,1)S(1)} %get-tuple-element.50), channel_id=1, source_target_pairs={{1,2},{2,1},{5,6},{6,5},{9,10},{10,9},{13,14},{14,13},{17,18},{18,... | collective-permute-start | bytes 786440 | tf_op jit(solution)/shard_map/ppermute | solution.py:615
  37.8 2.3 %others.1 = (bf16[256,512]{1,0:T(8,128)(2,1)S(1)}, f32[256,512]{1,0:T(8,128)S(1)}, f32[256,512]{1,0:T(8,128)S(1)}) custom-call(bf16[3,2048,512]{2,1,0:T(8,128)(2,1)S(1)} %copy-done.1, bf16[3,256,512]{2,1,0:T(8,128)(2,1)S(1)} %get-tuple-element.48.grad_ref), custom_call_target="tpu_custom_call" | custom-call | tf_op jit(solution)/shard_map/others/pallas_call | solution.py:545
  40.0 2.1 %collective-permute-start.6 = (bf16[256,512]{1,0:T(8,128)(2,1)S(1)}, bf16[256,512]{1,0:T(8,128)(2,1)S(1)}, u32[]{:S(2)}, u32[]{:S(2)}) collective-permute-start(bf16[256,512]{1,0:T(8,128)(2,1)S(1)} %get-tuple-element.51), channel_id=1, source_target_pairs={{0,2},{2,3},{3,1},{1,0},{4,6},{6,7},{7,5},{5,4},{8,10},{10,11},{11... | collective-permute-start | bytes 786440 | tf_op jit(solution)/shard_map/ppermute | solution.py:616
  42.2 1.5 %collective-permute-done.7 = bf16[256,512]{1,0:T(8,128)(2,1)S(1)} collective-permute-done((bf16[256,512]{1,0:T(8,128)(2,1)S(1)}, bf16[256,512]{1,0:T(8,128)(2,1)S(1)}, u32[]{:S(2)}, u32[]{:S(2)}) %collective-permute-start.7) | collective-permute-done | bytes 262176 | tf_op jit(solution)/shard_map/ppermute | solution.py:614
  43.7 0.1 add_convert_fusion.1
  43.8 2.5 %collective-permute-start.8 = (bf16[256,512]{1,0:T(8,128)(2,1)S(1)}, bf16[256,512]{1,0:T(8,128)(2,1)S(1)}, u32[]{:S(2)}, u32[]{:S(2)}) collective-permute-start(bf16[256,512]{1,0:T(8,128)(2,1)S(1)} %add_convert_fusion.1), channel_id=1, source_target_pairs={{0,1},{1,3},{3,2},{2,0},{4,5},{5,7},{7,6},{6,4},{8,9},{9,11},{11,1... | collective-permute-start | bytes 786440 | tf_op jit(solution)/shard_map/ppermute | solution.py:618
  46.3 0.0 collective-permute-done.5
  46.3 3.1 %collective-permute-done.6 = bf16[256,512]{1,0:T(8,128)(2,1)S(1)} collective-permute-done((bf16[256,512]{1,0:T(8,128)(2,1)S(1)}, bf16[256,512]{1,0:T(8,128)(2,1)S(1)}, u32[]{:S(2)}, u32[]{:S(2)}) %collective-permute-start.6) | collective-permute-done | bytes 262176 | tf_op jit(solution)/shard_map/ppermute | solution.py:616
  49.3 8.0 %collective-permute-done.8 = bf16[256,512]{1,0:T(8,128)(2,1)S(1)} collective-permute-done((bf16[256,512]{1,0:T(8,128)(2,1)S(1)}, bf16[256,512]{1,0:T(8,128)(2,1)S(1)}, u32[]{:S(2)}, u32[]{:S(2)}) %collective-permute-start.8) | collective-permute-done | bytes 262176 | tf_op jit(solution)/shard_map/ppermute | solution.py:618
  57.4 0.8 %add_convert_fusion = bf16[256,512]{1,0:T(8,128)(2,1)} fusion(bf16[256,512]{1,0:T(8,128)(2,1)S(1)} %collective-permute-done.8, bf16[256,512]{1,0:T(8,128)(2,1)S(1)} %collective-permute-done.6, f32[256,512]{1,0:T(8,128)S(1)} %get-tuple-element.49, bf16[256,512]{1,0:T(8,128)(2,1)S(1)} %collective-permute-done.5), kind=kLoop, calls=%fused_computation | loop fusion | flops 917504 | bytes 1572864 | tf_op jit(solution)/shard_map/convert_element_type | solution.py:620
Async XLA Ops:
  0.0 2.8 %copy-start = (bf16[3,2048,512]{2,1,0:T(8,128)(2,1)S(1)}, bf16[3,2048,512]{2,1,0:T(8,128)(2,1)}, u32[]{:S(2)}) copy-start(bf16[3,2048,512]{2,1,0:T(8,128)(2,1)} %w_hbm.5) | copy-start | bytes 18874372
  2.8 0.9 %copy-start.2 = (bf16[256,512]{1,0:T(8,128)(2,1)S(1)}, bf16[256,512]{1,0:T(8,128)(2,1)}, u32[]{:S(2)}) copy-start(bf16[256,512]{1,0:T(8,128)(2,1)} %og_ref.3) | copy-start | bytes 786436
  3.7 1.2 %copy-start.3 = (bf16[256,2048]{1,0:T(8,128)(2,1)S(1)}, bf16[256,2048]{1,0:T(8,128)(2,1)}, u32[]{:S(2)}) copy-start(bf16[256,2048]{1,0:T(8,128)(2,1)} %tok_hbm.1) | copy-start | bytes 3145732
  5.0 0.7 %copy-start.4 = (f32[4,256]{1,0:T(4,128)S(1)}, f32[4,256]{1,0:T(4,128)}, u32[]{:S(2)}) copy-start(f32[4,256]{1,0:T(4,128)} %logit_ref.1) | copy-start | bytes 12292
  5.6 0.7 %copy-start.5 = (f32[4,256]{1,0:T(4,128)S(1)}, f32[4,256]{1,0:T(4,128)}, u32[]{:S(2)}) copy-start(f32[4,256]{1,0:T(4,128)} %decay_ref.1) | copy-start | bytes 12292
  6.3 23.3 %copy-start.1 = (bf16[3,2048,512]{2,1,0:T(8,128)(2,1)S(1)}, bf16[3,2048,512]{2,1,0:T(8,128)(2,1)}, u32[]{:S(2)}) copy-start(bf16[3,2048,512]{2,1,0:T(8,128)(2,1)} %w_hbm.5) | copy-start | bytes 18874372
  13.5 1.6 %collective-permute-start = (bf16[2,3,128,128]{3,2,1,0:T(8,128)(2,1)S(1)}, bf16[2,3,128,128]{3,2,1,0:T(8,128)(2,1)S(1)}, u32[]{:S(2)}, u32[]{:S(2)}) collective-permute-start(bf16[2,3,128,128]{3,2,1,0:T(8,128)(2,1)S(1)} %get-tuple-element.43), channel_id=1, source_target_pairs={{0,4},{4,0},{8,12},{12,8},{16,20},{20,16},{24,28},{28,24},{1,5},{5... | collective-permute-start | bytes 589832 | tf_op jit(solution)/shard_map/ppermute | solution.py:560
  15.4 7.1 %collective-permute-start.1 = (bf16[2,2,128,128]{3,2,1,0:T(8,128)(2,1)S(1)}, bf16[2,2,128,128]{3,2,1,0:T(8,128)(2,1)S(1)}, u32[]{:S(2)}, u32[]{:S(2)}) collective-permute-start(bf16[2,2,128,128]{3,2,1,0:T(8,128)(2,1)S(1)} %get-tuple-element.44), channel_id=1, source_target_pairs={{0,8},{4,12},{8,0},{12,4},{16,24},{20,28},{24,16},{28,20},{1,9},{5... | collective-permute-start | bytes 393224 | tf_op jit(solution)/shard_map/ppermute | solution.py:560
  18.3 7.9 %collective-permute-start.3 = (bf16[2,2,128,128]{3,2,1,0:T(8,128)(2,1)S(1)}, bf16[2,2,128,128]{3,2,1,0:T(8,128)(2,1)S(1)}, u32[]{:S(2)}, u32[]{:S(2)}) collective-permute-start(bf16[2,2,128,128]{3,2,1,0:T(8,128)(2,1)S(1)} %get-tuple-element.45), channel_id=1, source_target_pairs={{0,24},{4,28},{8,16},{12,20},{16,8},{20,12},{24,0},{28,4},{1,25},{... | collective-permute-start | bytes 393224 | tf_op jit(solution)/shard_map/ppermute | solution.py:560
  19.7 7.8 %collective-permute-start.2 = (bf16[2,2,128,128]{3,2,1,0:T(8,128)(2,1)S(1)}, bf16[2,2,128,128]{3,2,1,0:T(8,128)(2,1)S(1)}, u32[]{:S(2)}, u32[]{:S(2)}) collective-permute-start(bf16[2,2,128,128]{3,2,1,0:T(8,128)(2,1)S(1)} %get-tuple-element.45), channel_id=1, source_target_pairs={{0,16},{4,20},{8,24},{12,28},{16,0},{20,4},{24,8},{28,12},{1,17},{... | collective-permute-start | bytes 393224 | tf_op jit(solution)/shard_map/ppermute | solution.py:560
  28.2 1.4 %collective-permute-start.4 = (bf16[2,2,128,128]{3,2,1,0:T(8,128)(2,1)S(1)}, bf16[2,2,128,128]{3,2,1,0:T(8,128)(2,1)S(1)}, u32[]{:S(2)}, u32[]{:S(2)}) collective-permute-start(bf16[2,2,128,128]{3,2,1,0:T(8,128)(2,1)S(1)} %get-tuple-element.47), channel_id=1, source_target_pairs={{0,4},{4,0},{8,12},{12,8},{16,20},{20,16},{24,28},{28,24},{1,5},{5... | collective-permute-start | bytes 393224 | tf_op jit(solution)/shard_map/ppermute | solution.py:560
  33.6 10.1 %collective-permute-start.7 = (bf16[256,512]{1,0:T(8,128)(2,1)S(1)}, bf16[256,512]{1,0:T(8,128)(2,1)S(1)}, u32[]{:S(2)}, u32[]{:S(2)}) collective-permute-start(bf16[256,512]{1,0:T(8,128)(2,1)S(1)} %get-tuple-element.50), channel_id=1, source_target_pairs={{0,1},{3,2},{4,5},{7,6},{8,9},{11,10},{12,13},{15,14},{16,17},{19,... | collective-permute-start | bytes 786440 | tf_op jit(solution)/shard_map/ppermute | solution.py:614
  37.1 9.2 %collective-permute-start.5 = (bf16[256,512]{1,0:T(8,128)(2,1)S(1)}, bf16[256,512]{1,0:T(8,128)(2,1)S(1)}, u32[]{:S(2)}, u32[]{:S(2)}) collective-permute-start(bf16[256,512]{1,0:T(8,128)(2,1)S(1)} %get-tuple-element.50), channel_id=1, source_target_pairs={{1,2},{2,1},{5,6},{6,5},{9,10},{10,9},{13,14},{14,13},{17,18},{18,... | collective-permute-start | bytes 786440 | tf_op jit(solution)/shard_map/ppermute | solution.py:615
  40.0 9.3 %collective-permute-start.6 = (bf16[256,512]{1,0:T(8,128)(2,1)S(1)}, bf16[256,512]{1,0:T(8,128)(2,1)S(1)}, u32[]{:S(2)}, u32[]{:S(2)}) collective-permute-start(bf16[256,512]{1,0:T(8,128)(2,1)S(1)} %get-tuple-element.51), channel_id=1, source_target_pairs={{0,2},{2,3},{3,1},{1,0},{4,6},{6,7},{7,5},{5,4},{8,10},{10,11},{11... | collective-permute-start | bytes 786440 | tf_op jit(solution)/shard_map/ppermute | solution.py:616
  43.8 13.6 %collective-permute-start.8 = (bf16[256,512]{1,0:T(8,128)(2,1)S(1)}, bf16[256,512]{1,0:T(8,128)(2,1)S(1)}, u32[]{:S(2)}, u32[]{:S(2)}) collective-permute-start(bf16[256,512]{1,0:T(8,128)(2,1)S(1)} %add_convert_fusion.1), channel_id=1, source_target_pairs={{0,1},{1,3},{3,2},{2,0},{4,5},{5,7},{7,6},{6,4},{8,9},{9,11},{11,1... | collective-permute-start | bytes 786440 | tf_op jit(solution)/shard_map/ppermute | solution.py:618

commit v3 on v2

--- a/solution.py
+++ b/solution.py
@@ -125,12 +125,13 @@
 
 
 def prepare_kernel(
-    half, pieces, tok_hbm, w_hbm, logit_ref, decay_ref, og_ref,
-    unit_ref, scale_ref, lane_ref, col_ref, u_ref, wk_ref, dbt_ref, ktt_ref, gt_ref, keep_ref, send_ref,
-    tok_scr, w_scr, value_scr, pay_scr, tok_sem, w_sem,
+    half, pieces, tok_hbm, w_hbm, logit_hbm, decay_hbm, og_hbm,
+    w_ref, og_ref, unit_ref, scale_ref, lane_ref, col_ref, u_ref, wk_ref, dbt_ref, ktt_ref, gt_ref,
+    keep_ref, send_ref,
+    tok_scr, logit_ref, decay_ref, value_scr, pay_scr, tok_sem, w_sem, more_sem,
 ):
     heads, size = decay_ref.shape
-    members, depth, columns = w_scr.shape
+    members, depth, columns = w_ref.shape
     width = columns // heads
     chunk = depth // pieces
     members_in_turn = (1, 2, 0)
@@ -144,25 +145,30 @@
     ]
     w_copies = [
         [
-            pltpu.make_async_copy(w_hbm.at[p, part(i)], w_scr.at[p, part(i)], w_sem.at[p, i])
+            pltpu.make_async_copy(w_hbm.at[p, part(i)], w_ref.at[p, part(i)], w_sem.at[p, i])
             for i in range(pieces)
         ]
         for p in range(members)
     ]
+    small = [(logit_hbm, logit_ref), (decay_hbm, decay_ref), (og_hbm, og_ref)]
+    small = [pltpu.make_async_copy(a, b, more_sem.at[i]) for i, (a, b) in enumerate(small)]
+    for copy in small[:2]:
+        copy.start()
     for turn, p in enumerate(members_in_turn):
         for i in range(pieces):
             if turn == 0:
                 tok_copies[i].start()
             w_copies[p][i].start()
+            if turn == 0 and i == 0:
+                small[2].start()
+    for copy in small[:2]:
+        copy.wait()
 
     lanes, cols_of = gates(logit_ref[...], decay_ref[...])
     lane_ref[...] = lanes
     col_ref[...] = cols_of
     every = range(heads)
     spans = [slice(h * width, (h + 1) * width) for h in every]
-    for h in every:
-        gt_ref[h] = og_ref[:, spans[h]].astype(F32).T.astype(BF16)
-
     for turn, p in enumerate(members_in_turn):
         total = None
         for i in range(pieces):
@@ -170,7 +176,7 @@
                 tok_copies[i].wait()
             w_copies[p][i].wait()
             here = slice(i * chunk, (i + 1) * chunk)
-            result = nn(tok_scr[:, here], w_scr[p, here])
+            result = nn(tok_scr[:, here], w_ref[p, here])
             total = result if total is None else total + result
         if p == 2:
             value_scr[...] = total
@@ -180,6 +186,9 @@
                 unit_ref[p, :, spans[h]] = unit
                 scale_ref[:, p * heads + h : p * heads + h + 1] = scale
 
+    small[2].wait()
+    for h in every:
+        gt_ref[h] = og_ref[:, spans[h]].astype(F32).T.astype(BF16)
     rows, cols = grid_ids(size)
     causal = rows >= cols
     strict = rows > cols
@@ -239,7 +248,7 @@
 
 
 def away():
-    return pl.BlockSpec(memory_space=pl.ANY)
+    return pl.BlockSpec(memory_space=pltpu.HBM)
 
 
 def limit(mebibytes):
@@ -254,6 +263,8 @@
     pieces = 4 if depth % 512 == 0 else 1
     gate_rows = 2 * heads + -2 * heads % 8
     shapes = [
+        ((members, depth, columns), BF16),
+        ((size, columns), BF16),
         ((2, size, columns), F32),
         ((size, 2 * heads), F32),
         ((gate_rows, size), F32),
@@ -268,20 +279,22 @@
     ]
     return pl.pallas_call(
         functools.partial(prepare_kernel, half, pieces),
-        in_specs=[away(), away(), here(), here(), here()],
+        in_specs=[away()] * 5,
         out_specs=[here()] * len(shapes),
         out_shape=[jax.ShapeDtypeStruct(*s) for s in shapes],
         scratch_shapes=[
             pltpu.VMEM((size, depth), BF16),
-            pltpu.VMEM((members, depth, columns), BF16),
+            pltpu.VMEM((heads, size), F32),
+            pltpu.VMEM((heads, size), F32),
             pltpu.VMEM((size, columns), F32),
             pltpu.VMEM((heads, 3, width, width), BF16),
             pltpu.SemaphoreType.DMA((pieces,)),
             pltpu.SemaphoreType.DMA((members, pieces)),
+            pltpu.SemaphoreType.DMA((3,)),
         ],
-        compiler_params=limit(36),
+        compiler_params=limit(28),
         name="prepare",
-    )(tokens, weights, logit, decay, out_grad)
+    )(*(pltpu.with_memory_space_constraint(x, pltpu.HBM) for x in (tokens, weights, logit, decay, out_grad)))
 
 
 def weigh_kernel(heads, lane_ref, col_ref, gamma_ref, turned_ref, strong_ref, strong_t_ref):
@@ -312,7 +325,7 @@
     )(lanes, cols)
 
 
-def pair_kernel(levels, keep_ref, recv_ref, *pay_refs):
+def pair_kernel(keep_ref, recv_ref, pay_ref):
     place = lax.axis_index("seq")
     first = lax.rem(place, 2) == 0
     chip = place // 2
@@ -324,10 +337,9 @@
             up = ahead[:, :width] + late[h, 1].astype(F32)
             down = nn(late[h, 2], early[h, 0]) + early[h, 2].astype(F32)
             joint = ahead[:, width:].astype(BF16)
-            for level in range(levels):
-                upward = lax.rem(chip // (1 << level), 2) == 0
-                pay_refs[level][h, 0] = joint
-                pay_refs[level][h, 1] = jnp.where(upward, up, down).astype(BF16)
+            for target in range(pay_ref.shape[0]):
+                pay_ref[target, h, 0] = joint
+                pay_ref[target, h, 1] = jnp.where(chip < target, up, down).astype(BF16)
 
     @pl.when(first)
     def _():
@@ -338,14 +350,13 @@
         join(recv_ref, keep_ref)
 
 
-def join_pair(keep, recv, levels):
+def join_pair(keep, recv, chips):
     half, _, width, _ = keep.shape
-    shape = jax.ShapeDtypeStruct((half, 2, width, width), BF16)
     return pl.pallas_call(
-        functools.partial(pair_kernel, levels),
+        pair_kernel,
         in_specs=[here()] * 2,
-        out_specs=[here()] * levels,
-        out_shape=[shape] * levels,
+        out_specs=here(),
+        out_shape=jax.ShapeDtypeStruct((chips, half, 2, width, width), BF16),
         compiler_params=limit(8),
         name="join_pair",
     )(keep, recv)
@@ -356,13 +367,14 @@
     return high, (value - high.astype(F32)).astype(BF16)
 
 
-def scan_kernel(keep_ref, recv_ref, near_ref, far_ref, cross_ref, own_ref, send_ref, enter, leave):
+def scan_kernel(keep_ref, recv_ref, got_ref, own_ref, send_ref, enter, leave):
     place = lax.axis_index("seq")
     first = lax.rem(place, 2) == 0
     chip = place // 2
     low = lax.rem(chip, 2) == 1
     high = chip // 2 == 1
     every = range(keep_ref.shape[0])
+    near_ref, far_ref, cross_ref = (got_ref.at[chip ^ i] for i in (1, 2, 3))
 
     def pairs(one, two):
         for h in every:
@@ -411,18 +423,18 @@
         within(recv_ref, keep_ref, send_ref, own_ref)
 
 
-def scan_chips(keep, recv, near, far, cross):
+def scan_chips(keep, recv, got):
     half, _, width, _ = keep.shape
     shape = jax.ShapeDtypeStruct((half, 2, width, width), BF16)
     return pl.pallas_call(
         scan_kernel,
-        in_specs=[here()] * 5,
+        in_specs=[here()] * 3,
         out_specs=[here()] * 2,
         out_shape=[shape] * 2,
         scratch_shapes=[pltpu.VMEM((half, width, width), F32)] * 2,
         compiler_params=limit(8),
         name="scan_chips",
-    )(keep, recv, near, far, cross)
+    )(keep, recv, got)
 
 
 def part_at(slot, count):
@@ -438,20 +450,12 @@
     return jnp.where(place < 2, ends, jnp.where(place == 2, high[0], high[1]))
 
 
-def fetch(w_hbm, w_scr, sem, slot, count):
-    step = w_hbm.shape[1] // count
-    start = pl.multiple_of(part_at(slot, count) * step, step)
-    return pltpu.make_async_copy(w_hbm.at[:, pl.ds(start, step)], w_scr, sem)
-
-
 def grads_kernel(
-    half, count, w_hbm, unit_ref, scale_ref, col_ref, u_ref, wk_ref, dbt_ref, ktt_ref, gt_ref, og_ref,
+    half, count, w_ref, unit_ref, scale_ref, col_ref, u_ref, wk_ref, dbt_ref, ktt_ref, gt_ref, og_ref,
     gamma_ref, turned_ref, strong_ref, strong_t_ref, own_ref, recv_ref,
-    grad_ref, out_ref, w_scr, edge_scr, sem,
+    grad_ref, out_ref, edge_scr,
 ):
     heads, size, width = u_ref.shape
-    copy = fetch(w_hbm, w_scr, sem, 0, count)
-    copy.start()
     if half:
         core = lax.rem(lax.axis_index("seq"), 2)
         edge_scr[pl.ds(core * half, half)] = own_ref[...]
@@ -491,14 +495,15 @@
             along = jnp.sum(unit * slope, axis=-1, keepdims=True)
             grad_ref[slot, :, span] = (scale * (slope - unit * along)).astype(BF16)
         grad_ref[2, :, span] = (beta[h] * delta[h]).astype(BF16)
-    copy.wait()
-    out_ref[...] = spread_grads(grad_ref, w_scr).astype(out_ref.dtype)
-
-
-def spread_grads(grad_ref, w_ref):
-    total = nt(grad_ref[0], w_ref[0])
+    out_ref[...] = spread_grads(grad_ref, w_ref, 0, count).astype(out_ref.dtype)
+
+
+def spread_grads(grad_ref, w_ref, slot, count):
+    step = w_ref.shape[1] // count
+    rows = pl.ds(pl.multiple_of(part_at(slot, count) * step, step), step)
+    total = nt(grad_ref[0], w_ref[0, rows])
     for member in range(1, grad_ref.shape[0]):
-        total = total + nt(grad_ref[member], w_ref[member])
+        total = total + nt(grad_ref[member], w_ref[member, rows])
     return total
 
 
@@ -510,30 +515,23 @@
     step = depth // count
     return pl.pallas_call(
         functools.partial(grads_kernel, half, count),
-        in_specs=[away()] + [here()] * 15,
+        in_specs=[here()] * 16,
         out_specs=[here()] * 2,
         out_shape=[
             jax.ShapeDtypeStruct((members, size, columns), BF16),
             jax.ShapeDtypeStruct((size, step), BF16),
         ],
         scratch_shapes=[
-            pltpu.VMEM((members, step, columns), BF16),
             pltpu.VMEM((heads, 2, width, width), BF16),
-            pltpu.SemaphoreType.DMA(()),
         ],
         compiler_params=limit(24),
         name="grads",
     )(weights, unit, scale, col, u, wk, dbt, ktt, gt, out_grad, *weighed, own, recv)
 
 
-def others_kernel(count, w_hbm, grad_ref, *refs):
-    outs, (w_scr, sem) = refs[: count - 1], refs[count - 1 :]
-    copies = [fetch(w_hbm, w_scr.at[i], sem.at[i], i + 1, count) for i in range(count - 1)]
-    for copy in copies:
-        copy.start()
-    for i, copy in enumerate(copies):
-        copy.wait()
-        outs[i][...] = spread_grads(grad_ref, w_scr.at[i]).astype(outs[i].dtype)
+def others_kernel(count, w_ref, grad_ref, *outs):
+    for i, out_ref in enumerate(outs):
+        out_ref[...] = spread_grads(grad_ref, w_ref, i + 1, count).astype(out_ref.dtype)
 
 
 def others(weights, grad):
@@ -544,14 +542,10 @@
     kinds = [BF16] + [F32] * 2 if count == 4 else [BF16] * (count - 2) + [F32]
     return pl.pallas_call(
         functools.partial(others_kernel, count),
-        in_specs=[away(), here()],
+        in_specs=[here()] * 2,
         out_specs=[here()] * (count - 1),
         out_shape=[jax.ShapeDtypeStruct((size, step), k) for k in kinds],
-        scratch_shapes=[
-            pltpu.VMEM((count - 1, members, step, columns), BF16),
-            pltpu.SemaphoreType.DMA((count - 1,)),
-        ],
-        compiler_params=limit(24),
+        compiler_params=limit(16),
         name="others",
     )(weights, grad)
 
@@ -562,11 +556,10 @@
 
 def edges_by_pairs(keep, send, count):
     recv = swap(send, "seq", count, 1)
-    low, high = join_pair(keep, recv, 2)
-    near = swap(low, "seq", count, 2)
-    far = swap(high, "seq", count, 4)
-    cross = swap(high, "seq", count, 6)
-    own, other = scan_chips(keep, recv, near, far, cross)
+    pay = join_pair(keep, recv, count // 2)
+    same = [list(range(core, count, 2)) for core in range(2)]
+    got = lax.all_to_all(pay, "seq", 0, 0, axis_index_groups=same)
+    own, other = scan_chips(keep, recv, got)
     return own, swap(other, "seq", count, 1)
 
 
@@ -625,7 +618,7 @@
     count = lax.axis_size("seq")
     paired = heads % 2 == 0 and count == 8
     half = heads // 2 if paired else 0
-    unit, scale, lanes, col, u, wk, dbt, ktt, gt, keep, send = prepare(
+    held, kept_grad, unit, scale, lanes, col, u, wk, dbt, ktt, gt, keep, send = prepare(
         tokens, qkv_weight, beta_logit, log_decay, out_grad, half
     )
     if paired:
@@ -634,8 +627,8 @@
         own, recv = edges_by_gather(keep, count)
     weighed = weigh(lanes, col, heads)
     prepared = (unit, scale, col, u, wk, dbt, ktt, gt)
-    grad, end = grads(qkv_weight, prepared, out_grad, weighed, own, recv, half)
-    rest = others(qkv_weight, grad)
+    grad, end = grads(held, prepared, kept_grad, weighed, own, recv, half)
+    rest = others(held, grad)
     if lax.axis_size("head") == 4:
         return sum_of_four(end, *rest)
     return sum_on_line([rest[-1], end, *rest[:-1]])

time: 58.5 us -> 54.8 us (0.937)
  blocking collectives: 0 us -> 13.7 us
  waiting for transfers between devices: 22.2 us -> 15.3 us
  local copies, waits for them, and re-layouts: 6.33 us -> 0 us
  starting transfers between devices: 13.9 us -> 9.47 us
    all_to_all x0 -> x1, blocking collectives: none -> 13.7 us  [edges_by_pairs(): got = lax.all_to_all(pay, 'seq', 0, 0, axis_index_groups=same)]
    ppermute x5 -> x2, waiting for transfers between devices: 9.58 us -> 1.86 us  [swap(): return lax.ppermute(value, axis, [(i, i ^ mask) for i in range(count)])]
    unnamed x12 -> x0, local copies, waits for them, and re-layouts: 6.33 us -> none
    ppermute x5 -> x2, starting transfers between devices: 5.07 us -> 0.64 us  [swap(): return lax.ppermute(value, axis, [(i, i ^ mask) for i in range(count)])]
    pallas_call x1, Pallas kernels: 7.17 us -> 9.21 us  [prepare(): pl.pallas_call(functools.partial(prepare_kernel, half, pieces), in_specs=...]
    pallas_call x4, Pallas kernels: 7.1 us -> 5.43 us  [the longest x1 3.11 us: grads(): pl.pallas_call(functools.partial(grads_kernel, half, count), in_specs=[he...]
    ppermute x1, waiting for transfers between devices: 1.52 us -> 2.43 us  [sum_of_four(): outer = lax.ppermute(end, 'head', [(0, 1), (3, 2)])]
  transfers between devices with their start and end apart: 9 -> 6, of which waited for: 8 -> 5; matrix products, arithmetic and copies ran while one was open for 0% -> 0% of each run, Pallas kernels for 5% -> 4%
where the time goes in v3:
time: 54.8 us; the launch traced here: 54.6 us
  waiting for transfers between devices  15.3 us (28%)
  Pallas kernels  15.2 us (28%)
  blocking collectives  13.7 us (25%)
  starting transfers between devices  9.47 us (17%)
  other arithmetic  0.91 us (2%)
    all_to_all x1, blocking collectives, edges_by_pairs(): got = lax.all_to_all(pay, 'seq', 0, 0, axis_index_groups=same)  13.7 us
    pallas_call x1, Pallas kernels, prepare(): pl.pallas_call(functools.partial(prepare_kernel, half, pieces), in_specs=...  9.21 us
    ppermute x1, waiting for transfers between devices, sum_of_four(): joint = lax.ppermute(joint, 'head', [(0, 1), (1, 3), (3, 2), (2, 0)])  7.97 us
    ppermute x1, starting transfers between devices, sum_of_four(): outer = lax.ppermute(end, 'head', [(0, 1), (3, 2)])  3.5 us
    pallas_call x1, Pallas kernels, grads(): pl.pallas_call(functools.partial(grads_kernel, half, count), in_specs=[he...  3.11 us
    ppermute x1, waiting for transfers between devices, sum_of_four(): ring = lax.ppermute(first, 'head', [(0, 2), (2, 3), (3, 1), (1, 0)])  3.06 us
    ppermute x1, starting transfers between devices, sum_of_four(): joint = lax.ppermute(joint, 'head', [(0, 1), (1, 3), (3, 2), (2, 0)])  2.53 us
    ppermute x1, waiting for transfers between devices, sum_of_four(): outer = lax.ppermute(end, 'head', [(0, 1), (3, 2)])  2.43 us
  transfers between devices with their start and end apart: 6, of which 5 were waited for; matrix products, arithmetic and copies ran while one was open for 0% of the time, Pallas kernels for 4%

profile of v3, /device:TPU:0, one launch (start us, length us, event | category | flops | bytes accessed | tf_op | source)
XLA Modules:
  0.0 54.6 jit_solution(16997586083015319749)
XLA Ops:
  0.0 9.2 %prepare.1 = (bf16[3,2048,512]{2,1,0:T(8,128)(2,1)S(1)}, bf16[256,512]{1,0:T(8,128)(2,1)S(1)}, f32[2,256,512]{2,1,0:T(8,128)S(1)}, f32[256,8]{1,0:T(8,128)S(1)},...) custom-call(bf16[256,2048]{1,0:T(8,128)(2,1)} %tok_hbm.1, ...), custom_call_target="tpu_custom_call" | custom-call | tf_op jit(solution)/shard_map/prepare/pallas_call | solution.py:280
  9.2 0.6 %collective-permute-start = (bf16[2,3,128,128]{3,2,1,0:T(8,128)(2,1)S(1)}, bf16[2,3,128,128]{3,2,1,0:T(8,128)(2,1)S(1)}, u32[]{:S(2)}, u32[]{:S(2)}) collective-permute-start(bf16[2,3,128,128]{3,2,1,0:T(8,128)(2,1)S(1)} %get-tuple-element.45), channel_id=1, source_target_pairs={{0,4},{4,0},{8,12},{12,8},{16,20},{20,16},{24,28},{28,24},{1,5},{5... | collective-permute-start | bytes 589832 | tf_op jit(solution)/shard_map/ppermute | solution.py:554
  9.8 1.1 %collective-permute-done.recv_ref = bf16[2,3,128,128]{3,2,1,0:T(8,128)(2,1)S(1)} collective-permute-done((bf16[2,3,128,128]{3,2,1,0:T(8,128)(2,1)S(1)}, bf16[2,3,128,128]{3,2,1,0:T(8,128)(2,1)S(1)}, u32[]{:S(2)}, u32[]{:S(2)}) %collective-permute-start) | collective-permute-done | bytes 196640 | tf_op jit(solution)/shard_map/ppermute | solution.py:554
  10.9 0.2 join_pair.1
  11.1 13.7 %all_to_all.5.got_ref = bf16[4,2,2,128,128]{4,3,2,1,0:T(8,128)(2,1)S(1)} all-to-all(bf16[4,2,2,128,128]{4,3,2,1,0:T(8,128)(2,1)S(1)} %join_pair.1), channel_id=1, replica_groups={{0,8,16,24},{4,12,20,28},{1,9,17,25},{5,13,21,29},{2,10,18,26},{6,14,22..., dimensions={0} | all-to-all | bytes 1048576 | tf_op jit(solution)/shard_map/all_to_all | solution.py:561
  24.7 0.7 %scan_chips.1 = (bf16[2,2,128,128]{3,2,1,0:T(8,128)(2,1)S(1)}, bf16[2,2,128,128]{3,2,1,0:T(8,128)(2,1)S(1)}) custom-call(bf16[2,3,128,128]{3,2,1,0:T(8,128)(2,1)S(1)} %get-tuple-element.44.keep_ref, bf16[2,3,128,128]{3,2,1,0:T(8,128)(2,1)S(1)} %collective-permute-done.recv_ref, bf16[4,2,2,128,128]{4,3,2,1,0:T(8,128)(2,1)S(1)} %all_to_all.5.got_ref), custom_call_target="tpu_custom_call" | custom-call | tf_op jit(solution)/shard_map/scan_chips/pallas_call | solution.py:429
  25.4 0.1 collective-permute-start.1
  25.5 0.5 weigh.1
  26.1 0.8 %collective-permute-done.1.recv_ref = bf16[2,2,128,128]{3,2,1,0:T(8,128)(2,1)S(1)} collective-permute-done((bf16[2,2,128,128]{3,2,1,0:T(8,128)(2,1)S(1)}, bf16[2,2,128,128]{3,2,1,0:T(8,128)(2,1)S(1)}, u32[]{:S(2)}, u32[]{:S(2)}) %collective-permute-start.1) | collective-permute-done | bytes 131104 | tf_op jit(solution)/shard_map/ppermute | solution.py:554
  26.9 3.1 %grads.1 = (bf16[3,256,512]{2,1,0:T(8,128)(2,1)S(1)}, bf16[256,512]{1,0:T(8,128)(2,1)S(1)}) custom-call(bf16[3,2048,512]{2,1,0:T(8,128)(2,1)S(1)} %get-tuple-element.29.w_ref, f32[2,256,512]{2,1,0:T(8,128)S(1)} %get-tuple-element.30.unit_ref, f32[256,8]{1,0:T(8,128)S(1)} %get-tuple-element.31.scale_ref, f32[256,8]{1,0:T(8,128)S(1)} %get-tuple-element.32.col_ref, ...), custom_call_target="tpu_custom_call" | custom-call | tf_op jit(solution)/shard_map/grads/pallas_call | solution.py:516
  30.0 3.5 %collective-permute-start.4 = (bf16[256,512]{1,0:T(8,128)(2,1)S(1)}, bf16[256,512]{1,0:T(8,128)(2,1)S(1)}, u32[]{:S(2)}, u32[]{:S(2)}) collective-permute-start(bf16[256,512]{1,0:T(8,128)(2,1)S(1)} %get-tuple-element.50), channel_id=1, source_target_pairs={{0,1},{3,2},{4,5},{7,6},{8,9},{11,10},{12,13},{15,14},{16,17},{19,... | collective-permute-start | bytes 786440 | tf_op jit(solution)/shard_map/ppermute | solution.py:607
  33.5 0.7 %collective-permute-start.2 = (bf16[256,512]{1,0:T(8,128)(2,1)S(1)}, bf16[256,512]{1,0:T(8,128)(2,1)S(1)}, u32[]{:S(2)}, u32[]{:S(2)}) collective-permute-start(bf16[256,512]{1,0:T(8,128)(2,1)S(1)} %get-tuple-element.50), channel_id=1, source_target_pairs={{1,2},{2,1},{5,6},{6,5},{9,10},{10,9},{13,14},{14,13},{17,18},{18,... | collective-permute-start | bytes 786440 | tf_op jit(solution)/shard_map/ppermute | solution.py:608
  34.2 1.4 %others.1 = (bf16[256,512]{1,0:T(8,128)(2,1)S(1)}, f32[256,512]{1,0:T(8,128)S(1)}, f32[256,512]{1,0:T(8,128)S(1)}) custom-call(bf16[3,2048,512]{2,1,0:T(8,128)(2,1)S(1)} %get-tuple-element.29.w_ref, bf16[3,256,512]{2,1,0:T(8,128)(2,1)S(1)} %get-tuple-element.48.grad_ref), custom_call_target="tpu_custom_call" | custom-call | tf_op jit(solution)/shard_map/others/pallas_call | solution.py:543
  35.6 2.1 %collective-permute-start.3 = (bf16[256,512]{1,0:T(8,128)(2,1)S(1)}, bf16[256,512]{1,0:T(8,128)(2,1)S(1)}, u32[]{:S(2)}, u32[]{:S(2)}) collective-permute-start(bf16[256,512]{1,0:T(8,128)(2,1)S(1)} %get-tuple-element.51), channel_id=1, source_target_pairs={{0,2},{2,3},{3,1},{1,0},{4,6},{6,7},{7,5},{5,4},{8,10},{10,11},{11... | collective-permute-start | bytes 786440 | tf_op jit(solution)/shard_map/ppermute | solution.py:609
  37.7 2.4 %collective-permute-done.4 = bf16[256,512]{1,0:T(8,128)(2,1)S(1)} collective-permute-done((bf16[256,512]{1,0:T(8,128)(2,1)S(1)}, bf16[256,512]{1,0:T(8,128)(2,1)S(1)}, u32[]{:S(2)}, u32[]{:S(2)}) %collective-permute-start.4) | collective-permute-done | bytes 262176 | tf_op jit(solution)/shard_map/ppermute | solution.py:607
  40.1 0.1 add_convert_fusion.1
  40.2 2.5 %collective-permute-start.5 = (bf16[256,512]{1,0:T(8,128)(2,1)S(1)}, bf16[256,512]{1,0:T(8,128)(2,1)S(1)}, u32[]{:S(2)}, u32[]{:S(2)}) collective-permute-start(bf16[256,512]{1,0:T(8,128)(2,1)S(1)} %add_convert_fusion.1), channel_id=1, source_target_pairs={{0,1},{1,3},{3,2},{2,0},{4,5},{5,7},{7,6},{6,4},{8,9},{9,11},{11,1... | collective-permute-start | bytes 786440 | tf_op jit(solution)/shard_map/ppermute | solution.py:611
  42.7 3.1 %collective-permute-done.3 = bf16[256,512]{1,0:T(8,128)(2,1)S(1)} collective-permute-done((bf16[256,512]{1,0:T(8,128)(2,1)S(1)}, bf16[256,512]{1,0:T(8,128)(2,1)S(1)}, u32[]{:S(2)}, u32[]{:S(2)}) %collective-permute-start.3) | collective-permute-done | bytes 262176 | tf_op jit(solution)/shard_map/ppermute | solution.py:609
  45.8 0.0 collective-permute-done.2
  45.8 8.0 %collective-permute-done.5 = bf16[256,512]{1,0:T(8,128)(2,1)S(1)} collective-permute-done((bf16[256,512]{1,0:T(8,128)(2,1)S(1)}, bf16[256,512]{1,0:T(8,128)(2,1)S(1)}, u32[]{:S(2)}, u32[]{:S(2)}) %collective-permute-start.5) | collective-permute-done | bytes 262176 | tf_op jit(solution)/shard_map/ppermute | solution.py:611
  53.8 0.8 %add_convert_fusion = bf16[256,512]{1,0:T(8,128)(2,1)} fusion(bf16[256,512]{1,0:T(8,128)(2,1)S(1)} %collective-permute-done.5, bf16[256,512]{1,0:T(8,128)(2,1)S(1)} %collective-permute-done.3, f32[256,512]{1,0:T(8,128)S(1)} %get-tuple-element.49, bf16[256,512]{1,0:T(8,128)(2,1)S(1)} %collective-permute-done.2), kind=kLoop, calls=%fused_computation | loop fusion | flops 917504 | bytes 1572864 | tf_op jit(solution)/shard_map/convert_element_type | solution.py:613
Async XLA Ops:
  9.2 1.6 %collective-permute-start = (bf16[2,3,128,128]{3,2,1,0:T(8,128)(2,1)S(1)}, bf16[2,3,128,128]{3,2,1,0:T(8,128)(2,1)S(1)}, u32[]{:S(2)}, u32[]{:S(2)}) collective-permute-start(bf16[2,3,128,128]{3,2,1,0:T(8,128)(2,1)S(1)} %get-tuple-element.45), channel_id=1, source_target_pairs={{0,4},{4,0},{8,12},{12,8},{16,20},{20,16},{24,28},{28,24},{1,5},{5... | collective-permute-start | bytes 589832 | tf_op jit(solution)/shard_map/ppermute | solution.py:554
  25.4 1.4 %collective-permute-start.1 = (bf16[2,2,128,128]{3,2,1,0:T(8,128)(2,1)S(1)}, bf16[2,2,128,128]{3,2,1,0:T(8,128)(2,1)S(1)}, u32[]{:S(2)}, u32[]{:S(2)}) collective-permute-start(bf16[2,2,128,128]{3,2,1,0:T(8,128)(2,1)S(1)} %get-tuple-element.47), channel_id=1, source_target_pairs={{0,4},{4,0},{8,12},{12,8},{16,20},{20,16},{24,28},{28,24},{1,5},{5... | collective-permute-start | bytes 393224 | tf_op jit(solution)/shard_map/ppermute | solution.py:554
  30.0 10.2 %collective-permute-start.4 = (bf16[256,512]{1,0:T(8,128)(2,1)S(1)}, bf16[256,512]{1,0:T(8,128)(2,1)S(1)}, u32[]{:S(2)}, u32[]{:S(2)}) collective-permute-start(bf16[256,512]{1,0:T(8,128)(2,1)S(1)} %get-tuple-element.50), channel_id=1, source_target_pairs={{0,1},{3,2},{4,5},{7,6},{8,9},{11,10},{12,13},{15,14},{16,17},{19,... | collective-permute-start | bytes 786440 | tf_op jit(solution)/shard_map/ppermute | solution.py:607
  33.5 12.3 %collective-permute-start.2 = (bf16[256,512]{1,0:T(8,128)(2,1)S(1)}, bf16[256,512]{1,0:T(8,128)(2,1)S(1)}, u32[]{:S(2)}, u32[]{:S(2)}) collective-permute-start(bf16[256,512]{1,0:T(8,128)(2,1)S(1)} %get-tuple-element.50), channel_id=1, source_target_pairs={{1,2},{2,1},{5,6},{6,5},{9,10},{10,9},{13,14},{14,13},{17,18},{18,... | collective-permute-start | bytes 786440 | tf_op jit(solution)/shard_map/ppermute | solution.py:608
  35.6 10.2 %collective-permute-start.3 = (bf16[256,512]{1,0:T(8,128)(2,1)S(1)}, bf16[256,512]{1,0:T(8,128)(2,1)S(1)}, u32[]{:S(2)}, u32[]{:S(2)}) collective-permute-start(bf16[256,512]{1,0:T(8,128)(2,1)S(1)} %get-tuple-element.51), channel_id=1, source_target_pairs={{0,2},{2,3},{3,1},{1,0},{4,6},{6,7},{7,5},{5,4},{8,10},{10,11},{11... | collective-permute-start | bytes 786440 | tf_op jit(solution)/shard_map/ppermute | solution.py:609
  40.2 13.6 %collective-permute-start.5 = (bf16[256,512]{1,0:T(8,128)(2,1)S(1)}, bf16[256,512]{1,0:T(8,128)(2,1)S(1)}, u32[]{:S(2)}, u32[]{:S(2)}) collective-permute-start(bf16[256,512]{1,0:T(8,128)(2,1)S(1)} %add_convert_fusion.1), channel_id=1, source_target_pairs={{0,1},{1,3},{3,2},{2,0},{4,5},{5,7},{7,6},{6,4},{8,9},{9,11},{11,1... | collective-permute-start | bytes 786440 | tf_op jit(solution)/shard_map/ppermute | solution.py:611

commit v4 on v3

--- a/solution.py
+++ b/solution.py
@@ -7,6 +7,7 @@
 from jax.experimental.pallas import tpu as pltpu
 from jax.sharding import PartitionSpec as P
 
+
 F32 = jnp.float32
 BF16 = jnp.bfloat16
 HIGH = lax.Precision.HIGHEST
@@ -19,12 +20,6 @@
 
 def nt(a, b):
     return lax.dot_general(a, b, (((1,), (1,)), ((), ())), preferred_element_type=F32)
-
-
-def fine(a, b, dims=(1, 0)):
-    return lax.dot_general(
-        a, b, (((dims[0],), (dims[1],)), ((), ())), precision=HIGH, preferred_element_type=F32
-    )
 
 
 def grid_ids(size):
@@ -59,7 +54,7 @@
     return tensor * scale, scale
 
 
-def unit_lower_inverse(couplings):
+def unit_lower_inverse(couplings, fill):
     size = couplings[0].shape[0]
     base = size // 4
     lane_block = lax.broadcasted_iota(jnp.int32, (base, size), 1) // base
@@ -82,6 +77,7 @@
         narrow = [p.astype(BF16) for p in power]
         if reach == 1:
             power = [nn(p, spread(p)) for p in narrow]
+            fill()
         else:
             both = [
                 nn(jnp.concatenate([n.astype(BF16), p], axis=0), spread(p))
@@ -89,20 +85,24 @@
             ]
             rest = [n + p + x[:base] for n, p, x in zip(rest, power, both)]
             power = [x[base:] for x in both]
+            fill()
         reach *= 2
     if reach > 1:
         narrow = [p.astype(BF16) for p in power]
         rest = [n + p + nn(n.astype(BF16), spread(b)) for n, p, b in zip(rest, power, narrow)]
+        fill()
 
     outer = [jnp.where(on[0], strip(a, 1), 0.0) + jnp.where(on[2], strip(a, 3), 0.0) for a in couplings]
     wide = [n.astype(BF16) for n in rest]
     half = [g + nn(g.astype(BF16), spread(n)) for g, n in zip(outer, wide)]
     half_b = [y.astype(BF16) for y in half]
+    fill()
     late = [jnp.where(odd, n, 0.0) for n in rest]
     cross = [
         y + nn(l.astype(BF16), jnp.concatenate([none, b * masks[0], none, b * masks[2]], axis=0))
         for y, l, b in zip(half, late, half_b)
     ]
+    fill()
     below = [l - z for l, z in zip(late, cross)]
     above = [jnp.where(odd, 0.0, n) for n in rest]
     mid = size // 2
@@ -110,6 +110,7 @@
     later = [jnp.concatenate([t[:, mid:], b[:, mid:]], axis=0).astype(BF16) for t, b in zip(above, below)]
     corner = [a[mid:, :mid] for a in couplings]
     half = [c + nn(c.astype(BF16), e) for c, e in zip(corner, early)]
+    fill()
     cross = [y + nn(l, y.astype(BF16)) for y, l in zip(half, later)]
     blank = jnp.zeros((mid, mid), BF16)
     return [
@@ -128,7 +129,7 @@
     half, pieces, tok_hbm, w_hbm, logit_hbm, decay_hbm, og_hbm,
     w_ref, og_ref, unit_ref, scale_ref, lane_ref, col_ref, u_ref, wk_ref, dbt_ref, ktt_ref, gt_ref,
     keep_ref, send_ref,
-    tok_scr, logit_ref, decay_ref, value_scr, pay_scr, tok_sem, w_sem, more_sem,
+    tok_scr, logit_ref, decay_ref, value_scr, pay_scr, gamma_scr, pair_scr, tok_sem, w_sem, more_sem,
 ):
     heads, size = decay_ref.shape
     members, depth, columns = w_ref.shape
@@ -152,41 +153,25 @@
     ]
     small = [(logit_hbm, logit_ref), (decay_hbm, decay_ref), (og_hbm, og_ref)]
     small = [pltpu.make_async_copy(a, b, more_sem.at[i]) for i, (a, b) in enumerate(small)]
-    for copy in small[:2]:
+    for copy in small:
         copy.start()
     for turn, p in enumerate(members_in_turn):
         for i in range(pieces):
             if turn == 0:
                 tok_copies[i].start()
             w_copies[p][i].start()
-            if turn == 0 and i == 0:
-                small[2].start()
-    for copy in small[:2]:
+
+    def product(p, i):
+        span = slice(i * chunk, (i + 1) * chunk)
+        return nn(tok_scr[:, span], w_ref[p, span])
+
+    every = range(heads)
+    spans = [slice(h * width, (h + 1) * width) for h in every]
+    for copy in small:
         copy.wait()
-
     lanes, cols_of = gates(logit_ref[...], decay_ref[...])
     lane_ref[...] = lanes
     col_ref[...] = cols_of
-    every = range(heads)
-    spans = [slice(h * width, (h + 1) * width) for h in every]
-    for turn, p in enumerate(members_in_turn):
-        total = None
-        for i in range(pieces):
-            if turn == 0:
-                tok_copies[i].wait()
-            w_copies[p][i].wait()
-            here = slice(i * chunk, (i + 1) * chunk)
-            result = nn(tok_scr[:, here], w_ref[p, here])
-            total = result if total is None else total + result
-        if p == 2:
-            value_scr[...] = total
-        else:
-            for h in every:
-                unit, scale = unit_rows(total[:, spans[h]])
-                unit_ref[p, :, spans[h]] = unit
-                scale_ref[:, p * heads + h : p * heads + h + 1] = scale
-
-    small[2].wait()
     for h in every:
         gt_ref[h] = og_ref[:, spans[h]].astype(F32).T.astype(BF16)
     rows, cols = grid_ids(size)
@@ -195,15 +180,48 @@
     run_col = [cols_of[:, h : h + 1] for h in every]
     run_row = [lanes[h : h + 1, :] for h in every]
     beta = [cols_of[:, heads + h : heads + h + 1] for h in every]
+
+    total = None
+    for i in range(pieces):
+        tok_copies[i].wait()
+        w_copies[1][i].wait()
+        result = product(1, i)
+        total = result if total is None else total + result
+
+    def normalize(p, total):
+        for h in every:
+            unit, scale = unit_rows(total[:, spans[h]])
+            unit_ref[p, :, spans[h]] = unit
+            scale_ref[:, p * heads + h : p * heads + h + 1] = scale
+
+    normalize(1, total)
     keys = [unit_ref[1, :, s] for s in spans]
     key_b = [k.astype(BF16) for k in keys]
-    gamma = [jnp.exp(jnp.where(causal, run_col[h] - run_row[h], FAR)) for h in every]
-    couplings = [
-        jnp.where(strict, beta[h] * gamma[h] * nt(key_b[h], key_b[h]), 0.0) for h in every
-    ]
+    for h in every:
+        gamma = jnp.exp(jnp.where(causal, run_col[h] - run_row[h], FAR))
+        gamma_scr[h] = gamma
+        pair_scr[h] = jnp.where(strict, beta[h] * gamma * nt(key_b[h], key_b[h]), 0.0)
+    for i in range(pieces):
+        w_copies[2][i].wait()
+    waiting = [(p, i) for p in (2, 0) for i in range(pieces)]
+    totals = {2: None, 0: None}
+
+    def fill():
+        if waiting:
+            p, i = waiting.pop(0)
+            if p == 0 and i == 0:
+                for copy in w_copies[0]:
+                    copy.wait()
+            result = product(p, i)
+            totals[p] = result if totals[p] is None else totals[p] + result
+
+    inverse = unit_lower_inverse([pair_scr[h] for h in every], fill)
+    while waiting:
+        fill()
+    value_scr[...] = totals[2]
+    normalize(0, totals[0])
     queries = [unit_ref[0, :, s] for s in spans]
-    scores = [(gamma[h] * nt(queries[h].astype(BF16), key_b[h])).astype(BF16) for h in every]
-    inverse = unit_lower_inverse(couplings)
+    scores = [(gamma_scr[h] * nt(queries[h].astype(BF16), key_b[h])).astype(BF16) for h in every]
     last = [run_col[h][size - 1 : size, :] for h in every]
     open_col = [jnp.exp(run_col[h]) for h in every]
     fade_row = [jnp.exp(last[h] - run_row[h]) for h in every]
@@ -288,6 +306,8 @@
             pltpu.VMEM((heads, size), F32),
             pltpu.VMEM((size, columns), F32),
             pltpu.VMEM((heads, 3, width, width), BF16),
+            pltpu.VMEM((heads, size, size), F32),
+            pltpu.VMEM((heads, size, size), F32),
             pltpu.SemaphoreType.DMA((pieces,)),
             pltpu.SemaphoreType.DMA((members, pieces)),
             pltpu.SemaphoreType.DMA((3,)),
@@ -325,7 +345,7 @@
     )(lanes, cols)
 
 
-def pair_kernel(keep_ref, recv_ref, pay_ref):
+def pair_kernel(levels, keep_ref, recv_ref, *pay_refs):
     place = lax.axis_index("seq")
     first = lax.rem(place, 2) == 0
     chip = place // 2
@@ -337,9 +357,10 @@
             up = ahead[:, :width] + late[h, 1].astype(F32)
             down = nn(late[h, 2], early[h, 0]) + early[h, 2].astype(F32)
             joint = ahead[:, width:].astype(BF16)
-            for target in range(pay_ref.shape[0]):
-                pay_ref[target, h, 0] = joint
-                pay_ref[target, h, 1] = jnp.where(chip < target, up, down).astype(BF16)
+            for level in range(levels):
+                upward = lax.rem(chip // (1 << level), 2) == 0
+                pay_refs[level][h, 0] = joint
+                pay_refs[level][h, 1] = jnp.where(upward, up, down).astype(BF16)
 
     @pl.when(first)
     def _():
@@ -350,13 +371,14 @@
         join(recv_ref, keep_ref)
 
 
-def join_pair(keep, recv, chips):
+def join_pair(keep, recv, levels):
     half, _, width, _ = keep.shape
+    shape = jax.ShapeDtypeStruct((half, 2, width, width), BF16)
     return pl.pallas_call(
-        pair_kernel,
+        functools.partial(pair_kernel, levels),
         in_specs=[here()] * 2,
-        out_specs=here(),
-        out_shape=jax.ShapeDtypeStruct((chips, half, 2, width, width), BF16),
+        out_specs=[here()] * levels,
+        out_shape=[shape] * levels,
         compiler_params=limit(8),
         name="join_pair",
     )(keep, recv)
@@ -367,14 +389,13 @@
     return high, (value - high.astype(F32)).astype(BF16)
 
 
-def scan_kernel(keep_ref, recv_ref, got_ref, own_ref, send_ref, enter, leave):
+def scan_kernel(keep_ref, recv_ref, near_ref, far_ref, cross_ref, own_ref, send_ref, enter, leave):
     place = lax.axis_index("seq")
     first = lax.rem(place, 2) == 0
     chip = place // 2
     low = lax.rem(chip, 2) == 1
     high = chip // 2 == 1
     every = range(keep_ref.shape[0])
-    near_ref, far_ref, cross_ref = (got_ref.at[chip ^ i] for i in (1, 2, 3))
 
     def pairs(one, two):
         for h in every:
@@ -423,18 +444,18 @@
         within(recv_ref, keep_ref, send_ref, own_ref)
 
 
-def scan_chips(keep, recv, got):
+def scan_chips(keep, recv, near, far, cross):
     half, _, width, _ = keep.shape
     shape = jax.ShapeDtypeStruct((half, 2, width, width), BF16)
     return pl.pallas_call(
         scan_kernel,
-        in_specs=[here()] * 3,
+        in_specs=[here()] * 5,
         out_specs=[here()] * 2,
         out_shape=[shape] * 2,
         scratch_shapes=[pltpu.VMEM((half, width, width), F32)] * 2,
         compiler_params=limit(8),
         name="scan_chips",
-    )(keep, recv, got)
+    )(keep, recv, near, far, cross)
 
 
 def part_at(slot, count):
@@ -450,12 +471,17 @@
     return jnp.where(place < 2, ends, jnp.where(place == 2, high[0], high[1]))
 
 
+def early_parts(count):
+    return 2 if count == 4 else 1
+
+
 def grads_kernel(
     half, count, w_ref, unit_ref, scale_ref, col_ref, u_ref, wk_ref, dbt_ref, ktt_ref, gt_ref, og_ref,
     gamma_ref, turned_ref, strong_ref, strong_t_ref, own_ref, recv_ref,
-    grad_ref, out_ref, edge_scr,
+    grad_ref, *rest,
 ):
     heads, size, width = u_ref.shape
+    outs, edge_scr = rest[:-1], rest[-1]
     if half:
         core = lax.rem(lax.axis_index("seq"), 2)
         edge_scr[pl.ds(core * half, half)] = own_ref[...]
@@ -471,6 +497,8 @@
     update = [(u_ref[h] - nn(wk_ref[h], edge_scr[h, 0])).astype(BF16) for h in every]
     delta_t = [dbt_ref[h] + nn(edge_scr[h, 1], ktt_ref[h]) for h in every]
     delta = [d.T for d in delta_t]
+    totals = [None] * len(outs)
+    group = 2 if heads % 2 == 0 else 1
     for h in every:
         span = spans[h]
         rows = jnp.concatenate([og_ref[:, span], delta[h].astype(BF16)], axis=0)
@@ -495,15 +523,21 @@
             along = jnp.sum(unit * slope, axis=-1, keepdims=True)
             grad_ref[slot, :, span] = (scale * (slope - unit * along)).astype(BF16)
         grad_ref[2, :, span] = (beta[h] * delta[h]).astype(BF16)
-    out_ref[...] = spread_grads(grad_ref, w_ref, 0, count).astype(out_ref.dtype)
-
-
-def spread_grads(grad_ref, w_ref, slot, count):
+        if h % group == group - 1:
+            ready = slice((h - group + 1) * width, (h + 1) * width)
+            for slot in range(len(outs)):
+                part = spread_grads(grad_ref, w_ref, slot, count, ready)
+                totals[slot] = part if h < group else totals[slot] + part
+    for out_ref, total in zip(outs, totals):
+        out_ref[...] = total.astype(out_ref.dtype)
+
+
+def spread_grads(grad_ref, w_ref, slot, count, span=slice(None)):
     step = w_ref.shape[1] // count
     rows = pl.ds(pl.multiple_of(part_at(slot, count) * step, step), step)
-    total = nt(grad_ref[0], w_ref[0, rows])
+    total = nt(grad_ref[0, :, span], w_ref[0, rows, span])
     for member in range(1, grad_ref.shape[0]):
-        total = total + nt(grad_ref[member], w_ref[member, rows])
+        total = total + nt(grad_ref[member, :, span], w_ref[member, rows, span])
     return total
 
 
@@ -513,14 +547,13 @@
     members, depth, columns = weights.shape
     count = lax.axis_size("head")
     step = depth // count
+    early = early_parts(count)
     return pl.pallas_call(
         functools.partial(grads_kernel, half, count),
         in_specs=[here()] * 16,
-        out_specs=[here()] * 2,
-        out_shape=[
-            jax.ShapeDtypeStruct((members, size, columns), BF16),
-            jax.ShapeDtypeStruct((size, step), BF16),
-        ],
+        out_specs=[here()] * (1 + early),
+        out_shape=[jax.ShapeDtypeStruct((members, size, columns), BF16)]
+        + [jax.ShapeDtypeStruct((size, step), BF16)] * early,
         scratch_shapes=[
             pltpu.VMEM((heads, 2, width, width), BF16),
         ],
@@ -531,19 +564,19 @@
 
 def others_kernel(count, w_ref, grad_ref, *outs):
     for i, out_ref in enumerate(outs):
-        out_ref[...] = spread_grads(grad_ref, w_ref, i + 1, count).astype(out_ref.dtype)
+        out_ref[...] = spread_grads(grad_ref, w_ref, i + early_parts(count), count).astype(out_ref.dtype)
 
 
 def others(weights, grad):
-    members, depth, columns = weights.shape
+    _, depth, _ = weights.shape
     size = grad.shape[1]
     count = lax.axis_size("head")
     step = depth // count
-    kinds = [BF16] + [F32] * 2 if count == 4 else [BF16] * (count - 2) + [F32]
+    kinds = [F32] * 2 if count == 4 else [BF16] * (count - 2) + [F32]
     return pl.pallas_call(
         functools.partial(others_kernel, count),
         in_specs=[here()] * 2,
-        out_specs=[here()] * (count - 1),
+        out_specs=[here()] * len(kinds),
         out_shape=[jax.ShapeDtypeStruct((size, step), k) for k in kinds],
         compiler_params=limit(16),
         name="others",
@@ -556,10 +589,11 @@
 
 def edges_by_pairs(keep, send, count):
     recv = swap(send, "seq", count, 1)
-    pay = join_pair(keep, recv, count // 2)
-    same = [list(range(core, count, 2)) for core in range(2)]
-    got = lax.all_to_all(pay, "seq", 0, 0, axis_index_groups=same)
-    own, other = scan_chips(keep, recv, got)
+    low, high = join_pair(keep, recv, 2)
+    near = swap(low, "seq", count, 2)
+    far = swap(high, "seq", count, 4)
+    cross = swap(high, "seq", count, 6)
+    own, other = scan_chips(keep, recv, near, far, cross)
     return own, swap(other, "seq", count, 1)
 
 
@@ -613,7 +647,7 @@
     return total.astype(BF16)
 
 
-def on_device(tokens, qkv_weight, beta_logit, log_decay, out_grad):
+def step_on_device(tokens, qkv_weight, beta_logit, log_decay, out_grad):
     heads = beta_logit.shape[0]
     count = lax.axis_size("seq")
     paired = heads % 2 == 0 and count == 8
@@ -627,16 +661,16 @@
         own, recv = edges_by_gather(keep, count)
     weighed = weigh(lanes, col, heads)
     prepared = (unit, scale, col, u, wk, dbt, ktt, gt)
-    grad, end = grads(held, prepared, kept_grad, weighed, own, recv, half)
+    grad, *early = grads(held, prepared, kept_grad, weighed, own, recv, half)
     rest = others(held, grad)
     if lax.axis_size("head") == 4:
-        return sum_of_four(end, *rest)
-    return sum_on_line([rest[-1], end, *rest[:-1]])
+        return sum_of_four(*early, *rest)
+    return sum_on_line([rest[-1], *early, *rest[:-1]])
 
 
 def solution(mesh):
     return jax.shard_map(
-        on_device,
+        step_on_device,
         mesh=mesh,
         in_specs=(
             P("seq", None),

time: 54.8 us -> 53.8 us (0.982)
  blocking collectives: 13.7 us -> 0 us
  waiting for transfers between devices: 15.3 us -> 23.5 us
  starting transfers between devices: 9.47 us -> 13.9 us
    all_to_all x1 -> x0, blocking collectives: 13.7 us -> none  [edges_by_pairs(): got = lax.all_to_all(pay, 'seq', 0, 0, axis_index_groups=same)]
    ppermute x2 -> x5, waiting for transfers between devices: 1.86 us -> 9.6 us  [swap(): return lax.ppermute(value, axis, [(i, i ^ mask) for i in range(count)])]
    ppermute x2 -> x5, starting transfers between devices: 0.64 us -> 5.09 us  [swap(): return lax.ppermute(value, axis, [(i, i ^ mask) for i in range(count)])]
    pallas_call x1, Pallas kernels: 3.11 us -> 4.35 us  [grads(): pl.pallas_call(functools.partial(grads_kernel, half, count), in_specs=[he...]
    pallas_call x1, Pallas kernels: 9.21 us -> 8.54 us  [prepare(): pl.pallas_call(functools.partial(prepare_kernel, half, pieces), in_specs=...]
  transfers between devices with their start and end apart: 6 -> 9, of which waited for: 5 -> 8; matrix products, arithmetic and copies ran while one was open for 0% -> 0% of each run, Pallas kernels for 4% -> 3%
where the time goes in v4:
time: 53.8 us; the launch traced here: 53.7 us
  waiting for transfers between devices  23.5 us (44%)
  Pallas kernels  15.3 us (28%)
  starting transfers between devices  13.9 us (26%)
  other arithmetic  0.91 us (2%)
    ppermute x5, waiting for transfers between devices, swap(): return lax.ppermute(value, axis, [(i, i ^ mask) for i in range(count)])  9.6 us
    pallas_call x1, Pallas kernels, prepare(): pl.pallas_call(functools.partial(prepare_kernel, half, pieces), in_specs=...  8.54 us
    ppermute x1, waiting for transfers between devices, sum_of_four(): joint = lax.ppermute(joint, 'head', [(0, 1), (1, 3), (3, 2), (2, 0)])  7.96 us
    ppermute x5, starting transfers between devices, swap(): return lax.ppermute(value, axis, [(i, i ^ mask) for i in range(count)])  5.09 us
    pallas_call x1, Pallas kernels, grads(): pl.pallas_call(functools.partial(grads_kernel, half, count), in_specs=[he...  4.35 us
    ppermute x1, starting transfers between devices, sum_of_four(): outer = lax.ppermute(end, 'head', [(0, 1), (3, 2)])  3.48 us
    ppermute x1, waiting for transfers between devices, sum_of_four(): ring = lax.ppermute(first, 'head', [(0, 2), (2, 3), (3, 1), (1, 0)])  3.06 us
    ppermute x1, waiting for transfers between devices, sum_of_four(): outer = lax.ppermute(end, 'head', [(0, 1), (3, 2)])  2.84 us
  transfers between devices with their start and end apart: 9, of which 8 were waited for; matrix products, arithmetic and copies ran while one was open for 0% of the time, Pallas kernels for 3%

profile of v4, /device:TPU:0, one launch (start us, length us, event | category | flops | bytes accessed | tf_op | source)
XLA Modules:
  0.0 53.7 jit_solution(1212517006509599854)
XLA Ops:
  0.0 8.5 %prepare.1 = (bf16[3,2048,512]{2,1,0:T(8,128)(2,1)S(1)}, bf16[256,512]{1,0:T(8,128)(2,1)S(1)}, f32[2,256,512]{2,1,0:T(8,128)S(1)}, f32[256,8]{1,0:T(8,128)S(1)},...) custom-call(bf16[256,2048]{1,0:T(8,128)(2,1)} %tok_hbm.1, ...), custom_call_target="tpu_custom_call" | custom-call | tf_op jit(solution)/shard_map/prepare/pallas_call | solution.py:298
  8.5 0.6 %collective-permute-start = (bf16[2,3,128,128]{3,2,1,0:T(8,128)(2,1)S(1)}, bf16[2,3,128,128]{3,2,1,0:T(8,128)(2,1)S(1)}, u32[]{:S(2)}, u32[]{:S(2)}) collective-permute-start(bf16[2,3,128,128]{3,2,1,0:T(8,128)(2,1)S(1)} %get-tuple-element.47), channel_id=1, source_target_pairs={{0,4},{4,0},{8,12},{12,8},{16,20},{20,16},{24,28},{28,24},{1,5},{5... | collective-permute-start | bytes 589832 | tf_op jit(solution)/shard_map/ppermute | solution.py:587
  9.1 1.1 %collective-permute-done.recv_ref = bf16[2,3,128,128]{3,2,1,0:T(8,128)(2,1)S(1)} collective-permute-done((bf16[2,3,128,128]{3,2,1,0:T(8,128)(2,1)S(1)}, bf16[2,3,128,128]{3,2,1,0:T(8,128)(2,1)S(1)}, u32[]{:S(2)}, u32[]{:S(2)}) %collective-permute-start) | collective-permute-done | bytes 196640 | tf_op jit(solution)/shard_map/ppermute | solution.py:587
  10.2 0.2 join_pair.1
  10.4 2.9 %collective-permute-start.1 = (bf16[2,2,128,128]{3,2,1,0:T(8,128)(2,1)S(1)}, bf16[2,2,128,128]{3,2,1,0:T(8,128)(2,1)S(1)}, u32[]{:S(2)}, u32[]{:S(2)}) collective-permute-start(bf16[2,2,128,128]{3,2,1,0:T(8,128)(2,1)S(1)} %get-tuple-element.48), channel_id=1, source_target_pairs={{0,8},{4,12},{8,0},{12,4},{16,24},{20,28},{24,16},{28,20},{1,9},{5... | collective-permute-start | bytes 393224 | tf_op jit(solution)/shard_map/ppermute | solution.py:587
  13.3 1.5 %collective-permute-start.3 = (bf16[2,2,128,128]{3,2,1,0:T(8,128)(2,1)S(1)}, bf16[2,2,128,128]{3,2,1,0:T(8,128)(2,1)S(1)}, u32[]{:S(2)}, u32[]{:S(2)}) collective-permute-start(bf16[2,2,128,128]{3,2,1,0:T(8,128)(2,1)S(1)} %get-tuple-element.49), channel_id=1, source_target_pairs={{0,24},{4,28},{8,16},{12,20},{16,8},{20,12},{24,0},{28,4},{1,25},{... | collective-permute-start | bytes 393224 | tf_op jit(solution)/shard_map/ppermute | solution.py:587
  14.8 0.0 collective-permute-start.2
  14.8 2.6 %collective-permute-done.1.near_ref = bf16[2,2,128,128]{3,2,1,0:T(8,128)(2,1)S(1)} collective-permute-done((bf16[2,2,128,128]{3,2,1,0:T(8,128)(2,1)S(1)}, bf16[2,2,128,128]{3,2,1,0:T(8,128)(2,1)S(1)}, u32[]{:S(2)}, u32[]{:S(2)}) %collective-permute-start.1) | collective-permute-done | bytes 131104 | tf_op jit(solution)/shard_map/ppermute | solution.py:587
  17.5 3.7 %collective-permute-done.3.cross_ref = bf16[2,2,128,128]{3,2,1,0:T(8,128)(2,1)S(1)} collective-permute-done((bf16[2,2,128,128]{3,2,1,0:T(8,128)(2,1)S(1)}, bf16[2,2,128,128]{3,2,1,0:T(8,128)(2,1)S(1)}, u32[]{:S(2)}, u32[]{:S(2)}) %collective-permute-start.3) | collective-permute-done | bytes 131104 | tf_op jit(solution)/shard_map/ppermute | solution.py:587
  21.2 1.4 %collective-permute-done.2.far_ref = bf16[2,2,128,128]{3,2,1,0:T(8,128)(2,1)S(1)} collective-permute-done((bf16[2,2,128,128]{3,2,1,0:T(8,128)(2,1)S(1)}, bf16[2,2,128,128]{3,2,1,0:T(8,128)(2,1)S(1)}, u32[]{:S(2)}, u32[]{:S(2)}) %collective-permute-start.2) | collective-permute-done | bytes 131104 | tf_op jit(solution)/shard_map/ppermute | solution.py:587
  22.6 0.7 %scan_chips.1 = (bf16[2,2,128,128]{3,2,1,0:T(8,128)(2,1)S(1)}, bf16[2,2,128,128]{3,2,1,0:T(8,128)(2,1)S(1)}) custom-call(bf16[2,3,128,128]{3,2,1,0:T(8,128)(2,1)S(1)} %get-tuple-element.46.keep_ref, bf16[2,3,128,128]{3,2,1,0:T(8,128)(2,1)S(1)} %collective-permute-done.recv_ref, bf16[2,2,128,128]{3,2,1,0:T(8,128)(2,1)S(1)} %collective-permute-done.1.near_ref, ...), custom_call_target="tpu_custom_call" | custom-call | tf_op jit(solution)/shard_map/scan_chips/pallas_call | solution.py:450
  23.3 0.1 collective-permute-start.4
  23.4 0.5 %weigh.1 = (f32[4,256,256]{2,1,0:T(8,128)S(1)}, f32[4,256,256]{2,1,0:T(8,128)S(1)}, f32[4,256,256]{2,1,0:T(8,128)S(1)}, f32[4,256,256]{2,1,0:T(8,128)S(1)}) custom-call(f32[8,256]{1,0:T(8,128)S(1)} %get-tuple-element.41.lane_ref, f32[256,8]{1,0:T(8,128)S(1)} %get-tuple-element.34.col_ref), custom_call_target="tpu_custom_call" | custom-call | tf_op jit(solution)/shard_map/weigh/pallas_call | solution.py:338
  23.9 0.8 %collective-permute-done.4.recv_ref = bf16[2,2,128,128]{3,2,1,0:T(8,128)(2,1)S(1)} collective-permute-done((bf16[2,2,128,128]{3,2,1,0:T(8,128)(2,1)S(1)}, bf16[2,2,128,128]{3,2,1,0:T(8,128)(2,1)S(1)}, u32[]{:S(2)}, u32[]{:S(2)}) %collective-permute-start.4) | collective-permute-done | bytes 131104 | tf_op jit(solution)/shard_map/ppermute | solution.py:587
  24.7 4.4 %grads.1 = (bf16[3,256,512]{2,1,0:T(8,128)(2,1)S(1)}, bf16[256,512]{1,0:T(8,128)(2,1)S(1)}, bf16[256,512]{1,0:T(8,128)(2,1)S(1)}) custom-call(bf16[3,2048,512]{2,1,0:T(8,128)(2,1)S(1)} %get-tuple-element.31.w_ref, f32[2,256,512]{2,1,0:T(8,128)S(1)} %get-tuple-element.32.unit_ref, f32[256,8]{1,0:T(8,128)S(1)} %get-tuple-element.33.scale_ref, ...), custom_call_target="tpu_custom_call" | custom-call | tf_op jit(solution)/shard_map/grads/pallas_call | solution.py:551
  29.1 3.5 %collective-permute-start.7 = (bf16[256,512]{1,0:T(8,128)(2,1)S(1)}, bf16[256,512]{1,0:T(8,128)(2,1)S(1)}, u32[]{:S(2)}, u32[]{:S(2)}) collective-permute-start(bf16[256,512]{1,0:T(8,128)(2,1)S(1)} %get-tuple-element.54), channel_id=1, source_target_pairs={{0,1},{3,2},{4,5},{7,6},{8,9},{11,10},{12,13},{15,14},{16,17},{19,... | collective-permute-start | bytes 786440 | tf_op jit(solution)/shard_map/ppermute | solution.py:641
  32.5 0.7 %collective-permute-start.5 = (bf16[256,512]{1,0:T(8,128)(2,1)S(1)}, bf16[256,512]{1,0:T(8,128)(2,1)S(1)}, u32[]{:S(2)}, u32[]{:S(2)}) collective-permute-start(bf16[256,512]{1,0:T(8,128)(2,1)S(1)} %get-tuple-element.54), channel_id=1, source_target_pairs={{1,2},{2,1},{5,6},{6,5},{9,10},{10,9},{13,14},{14,13},{17,18},{18,... | collective-permute-start | bytes 786440 | tf_op jit(solution)/shard_map/ppermute | solution.py:642
  33.2 1.0 %others.1 = (f32[256,512]{1,0:T(8,128)S(1)}, f32[256,512]{1,0:T(8,128)S(1)}) custom-call(bf16[3,2048,512]{2,1,0:T(8,128)(2,1)S(1)} %get-tuple-element.31.w_ref, bf16[3,256,512]{2,1,0:T(8,128)(2,1)S(1)} %get-tuple-element.52.grad_ref), custom_call_target="tpu_custom_call" | custom-call | tf_op jit(solution)/shard_map/others/pallas_call | solution.py:576
  34.3 2.1 %collective-permute-start.6 = (bf16[256,512]{1,0:T(8,128)(2,1)S(1)}, bf16[256,512]{1,0:T(8,128)(2,1)S(1)}, u32[]{:S(2)}, u32[]{:S(2)}) collective-permute-start(bf16[256,512]{1,0:T(8,128)(2,1)S(1)} %get-tuple-element.55), channel_id=1, source_target_pairs={{0,2},{2,3},{3,1},{1,0},{4,6},{6,7},{7,5},{5,4},{8,10},{10,11},{11... | collective-permute-start | bytes 786440 | tf_op jit(solution)/shard_map/ppermute | solution.py:643
  36.4 2.8 %collective-permute-done.7 = bf16[256,512]{1,0:T(8,128)(2,1)S(1)} collective-permute-done((bf16[256,512]{1,0:T(8,128)(2,1)S(1)}, bf16[256,512]{1,0:T(8,128)(2,1)S(1)}, u32[]{:S(2)}, u32[]{:S(2)}) %collective-permute-start.7) | collective-permute-done | bytes 262176 | tf_op jit(solution)/shard_map/ppermute | solution.py:641
  39.2 0.1 add_convert_fusion.1
  39.3 2.5 %collective-permute-start.8 = (bf16[256,512]{1,0:T(8,128)(2,1)S(1)}, bf16[256,512]{1,0:T(8,128)(2,1)S(1)}, u32[]{:S(2)}, u32[]{:S(2)}) collective-permute-start(bf16[256,512]{1,0:T(8,128)(2,1)S(1)} %add_convert_fusion.1), channel_id=1, source_target_pairs={{0,1},{1,3},{3,2},{2,0},{4,5},{5,7},{7,6},{6,4},{8,9},{9,11},{11,1... | collective-permute-start | bytes 786440 | tf_op jit(solution)/shard_map/ppermute | solution.py:645
  41.8 3.1 %collective-permute-done.6 = bf16[256,512]{1,0:T(8,128)(2,1)S(1)} collective-permute-done((bf16[256,512]{1,0:T(8,128)(2,1)S(1)}, bf16[256,512]{1,0:T(8,128)(2,1)S(1)}, u32[]{:S(2)}, u32[]{:S(2)}) %collective-permute-start.6) | collective-permute-done | bytes 262176 | tf_op jit(solution)/shard_map/ppermute | solution.py:643
  44.9 0.0 collective-permute-done.5
  44.9 8.0 %collective-permute-done.8 = bf16[256,512]{1,0:T(8,128)(2,1)S(1)} collective-permute-done((bf16[256,512]{1,0:T(8,128)(2,1)S(1)}, bf16[256,512]{1,0:T(8,128)(2,1)S(1)}, u32[]{:S(2)}, u32[]{:S(2)}) %collective-permute-start.8) | collective-permute-done | bytes 262176 | tf_op jit(solution)/shard_map/ppermute | solution.py:645
  52.8 0.8 %add_convert_fusion = bf16[256,512]{1,0:T(8,128)(2,1)} fusion(bf16[256,512]{1,0:T(8,128)(2,1)S(1)} %collective-permute-done.8, bf16[256,512]{1,0:T(8,128)(2,1)S(1)} %collective-permute-done.6, f32[256,512]{1,0:T(8,128)S(1)} %get-tuple-element.53, bf16[256,512]{1,0:T(8,128)(2,1)S(1)} %collective-permute-done.5), kind=kLoop, calls=%fused_computation | loop fusion | flops 917504 | bytes 1572864 | tf_op jit(solution)/shard_map/convert_element_type | solution.py:647
Async XLA Ops:
  8.5 1.6 %collective-permute-start = (bf16[2,3,128,128]{3,2,1,0:T(8,128)(2,1)S(1)}, bf16[2,3,128,128]{3,2,1,0:T(8,128)(2,1)S(1)}, u32[]{:S(2)}, u32[]{:S(2)}) collective-permute-start(bf16[2,3,128,128]{3,2,1,0:T(8,128)(2,1)S(1)} %get-tuple-element.47), channel_id=1, source_target_pairs={{0,4},{4,0},{8,12},{12,8},{16,20},{20,16},{24,28},{28,24},{1,5},{5... | collective-permute-start | bytes 589832 | tf_op jit(solution)/shard_map/ppermute | solution.py:587
  10.4 7.1 %collective-permute-start.1 = (bf16[2,2,128,128]{3,2,1,0:T(8,128)(2,1)S(1)}, bf16[2,2,128,128]{3,2,1,0:T(8,128)(2,1)S(1)}, u32[]{:S(2)}, u32[]{:S(2)}) collective-permute-start(bf16[2,2,128,128]{3,2,1,0:T(8,128)(2,1)S(1)} %get-tuple-element.48), channel_id=1, source_target_pairs={{0,8},{4,12},{8,0},{12,4},{16,24},{20,28},{24,16},{28,20},{1,9},{5... | collective-permute-start | bytes 393224 | tf_op jit(solution)/shard_map/ppermute | solution.py:587
  13.3 7.9 %collective-permute-start.3 = (bf16[2,2,128,128]{3,2,1,0:T(8,128)(2,1)S(1)}, bf16[2,2,128,128]{3,2,1,0:T(8,128)(2,1)S(1)}, u32[]{:S(2)}, u32[]{:S(2)}) collective-permute-start(bf16[2,2,128,128]{3,2,1,0:T(8,128)(2,1)S(1)} %get-tuple-element.49), channel_id=1, source_target_pairs={{0,24},{4,28},{8,16},{12,20},{16,8},{20,12},{24,0},{28,4},{1,25},{... | collective-permute-start | bytes 393224 | tf_op jit(solution)/shard_map/ppermute | solution.py:587
  14.8 7.8 %collective-permute-start.2 = (bf16[2,2,128,128]{3,2,1,0:T(8,128)(2,1)S(1)}, bf16[2,2,128,128]{3,2,1,0:T(8,128)(2,1)S(1)}, u32[]{:S(2)}, u32[]{:S(2)}) collective-permute-start(bf16[2,2,128,128]{3,2,1,0:T(8,128)(2,1)S(1)} %get-tuple-element.49), channel_id=1, source_target_pairs={{0,16},{4,20},{8,24},{12,28},{16,0},{20,4},{24,8},{28,12},{1,17},{... | collective-permute-start | bytes 393224 | tf_op jit(solution)/shard_map/ppermute | solution.py:587
  23.3 1.4 %collective-permute-start.4 = (bf16[2,2,128,128]{3,2,1,0:T(8,128)(2,1)S(1)}, bf16[2,2,128,128]{3,2,1,0:T(8,128)(2,1)S(1)}, u32[]{:S(2)}, u32[]{:S(2)}) collective-permute-start(bf16[2,2,128,128]{3,2,1,0:T(8,128)(2,1)S(1)} %get-tuple-element.51), channel_id=1, source_target_pairs={{0,4},{4,0},{8,12},{12,8},{16,20},{20,16},{24,28},{28,24},{1,5},{5... | collective-permute-start | bytes 393224 | tf_op jit(solution)/shard_map/ppermute | solution.py:587
  29.1 10.2 %collective-permute-start.7 = (bf16[256,512]{1,0:T(8,128)(2,1)S(1)}, bf16[256,512]{1,0:T(8,128)(2,1)S(1)}, u32[]{:S(2)}, u32[]{:S(2)}) collective-permute-start(bf16[256,512]{1,0:T(8,128)(2,1)S(1)} %get-tuple-element.54), channel_id=1, source_target_pairs={{0,1},{3,2},{4,5},{7,6},{8,9},{11,10},{12,13},{15,14},{16,17},{19,... | collective-permute-start | bytes 786440 | tf_op jit(solution)/shard_map/ppermute | solution.py:641
  32.5 12.3 %collective-permute-start.5 = (bf16[256,512]{1,0:T(8,128)(2,1)S(1)}, bf16[256,512]{1,0:T(8,128)(2,1)S(1)}, u32[]{:S(2)}, u32[]{:S(2)}) collective-permute-start(bf16[256,512]{1,0:T(8,128)(2,1)S(1)} %get-tuple-element.54), channel_id=1, source_target_pairs={{1,2},{2,1},{5,6},{6,5},{9,10},{10,9},{13,14},{14,13},{17,18},{18,... | collective-permute-start | bytes 786440 | tf_op jit(solution)/shard_map/ppermute | solution.py:642
  34.3 10.6 %collective-permute-start.6 = (bf16[256,512]{1,0:T(8,128)(2,1)S(1)}, bf16[256,512]{1,0:T(8,128)(2,1)S(1)}, u32[]{:S(2)}, u32[]{:S(2)}) collective-permute-start(bf16[256,512]{1,0:T(8,128)(2,1)S(1)} %get-tuple-element.55), channel_id=1, source_target_pairs={{0,2},{2,3},{3,1},{1,0},{4,6},{6,7},{7,5},{5,4},{8,10},{10,11},{11... | collective-permute-start | bytes 786440 | tf_op jit(solution)/shard_map/ppermute | solution.py:643
  39.3 13.6 %collective-permute-start.8 = (bf16[256,512]{1,0:T(8,128)(2,1)S(1)}, bf16[256,512]{1,0:T(8,128)(2,1)S(1)}, u32[]{:S(2)}, u32[]{:S(2)}) collective-permute-start(bf16[256,512]{1,0:T(8,128)(2,1)S(1)} %add_convert_fusion.1), channel_id=1, source_target_pairs={{0,1},{1,3},{3,2},{2,0},{4,5},{5,7},{7,6},{6,4},{8,9},{9,11},{11,1... | collective-permute-start | bytes 786440 | tf_op jit(solution)/shard_map/ppermute | solution.py:645

commit v5 on v4

--- a/solution.py
+++ b/solution.py
@@ -135,7 +135,6 @@
     members, depth, columns = w_ref.shape
     width = columns // heads
     chunk = depth // pieces
-    members_in_turn = (1, 2, 0)
 
     def part(i):
         return pl.ds(i * chunk, chunk)
@@ -153,13 +152,12 @@
     ]
     small = [(logit_hbm, logit_ref), (decay_hbm, decay_ref), (og_hbm, og_ref)]
     small = [pltpu.make_async_copy(a, b, more_sem.at[i]) for i, (a, b) in enumerate(small)]
-    for copy in small:
+    for copy in small[:2]:
         copy.start()
-    for turn, p in enumerate(members_in_turn):
-        for i in range(pieces):
-            if turn == 0:
-                tok_copies[i].start()
-            w_copies[p][i].start()
+    for i in range(pieces):
+        tok_copies[i].start()
+        w_copies[1][i].start()
+    small[2].start()
 
     def product(p, i):
         span = slice(i * chunk, (i + 1) * chunk)
@@ -167,13 +165,11 @@
 
     every = range(heads)
     spans = [slice(h * width, (h + 1) * width) for h in every]
-    for copy in small:
+    for copy in small[:2]:
         copy.wait()
     lanes, cols_of = gates(logit_ref[...], decay_ref[...])
     lane_ref[...] = lanes
     col_ref[...] = cols_of
-    for h in every:
-        gt_ref[h] = og_ref[:, spans[h]].astype(F32).T.astype(BF16)
     rows, cols = grid_ids(size)
     causal = rows >= cols
     strict = rows > cols
@@ -185,6 +181,10 @@
     for i in range(pieces):
         tok_copies[i].wait()
         w_copies[1][i].wait()
+        if i == 0:
+            for p in (2, 0):
+                for copy in w_copies[p]:
+                    copy.start()
         result = product(1, i)
         total = result if total is None else total + result
 
@@ -194,6 +194,9 @@
             unit_ref[p, :, spans[h]] = unit
             scale_ref[:, p * heads + h : p * heads + h + 1] = scale
 
+    small[2].wait()
+    for h in every:
+        gt_ref[h] = og_ref[:, spans[h]].astype(F32).T.astype(BF16)
     normalize(1, total)
     keys = [unit_ref[1, :, s] for s in spans]
     key_b = [k.astype(BF16) for k in keys]
@@ -312,7 +315,7 @@
             pltpu.SemaphoreType.DMA((members, pieces)),
             pltpu.SemaphoreType.DMA((3,)),
         ],
-        compiler_params=limit(28),
+        compiler_params=limit(16),
         name="prepare",
     )(*(pltpu.with_memory_space_constraint(x, pltpu.HBM) for x in (tokens, weights, logit, decay, out_grad)))
 
@@ -471,8 +474,8 @@
     return jnp.where(place < 2, ends, jnp.where(place == 2, high[0], high[1]))
 
 
-def early_parts(count):
-    return 2 if count == 4 else 1
+def early_parts():
+    return 1
 
 
 def grads_kernel(
@@ -547,7 +550,7 @@
     members, depth, columns = weights.shape
     count = lax.axis_size("head")
     step = depth // count
-    early = early_parts(count)
+    early = early_parts()
     return pl.pallas_call(
         functools.partial(grads_kernel, half, count),
         in_specs=[here()] * 16,
@@ -557,14 +560,14 @@
         scratch_shapes=[
             pltpu.VMEM((heads, 2, width, width), BF16),
         ],
-        compiler_params=limit(24),
+        compiler_params=limit(12),
         name="grads",
     )(weights, unit, scale, col, u, wk, dbt, ktt, gt, out_grad, *weighed, own, recv)
 
 
 def others_kernel(count, w_ref, grad_ref, *outs):
     for i, out_ref in enumerate(outs):
-        out_ref[...] = spread_grads(grad_ref, w_ref, i + early_parts(count), count).astype(out_ref.dtype)
+        out_ref[...] = spread_grads(grad_ref, w_ref, i + early_parts(), count).astype(out_ref.dtype)
 
 
 def others(weights, grad):
@@ -572,13 +575,13 @@
     size = grad.shape[1]
     count = lax.axis_size("head")
     step = depth // count
-    kinds = [F32] * 2 if count == 4 else [BF16] * (count - 2) + [F32]
+    kinds = [BF16] + [F32] * 2 if count == 4 else [BF16] * (count - 2) + [F32]
     return pl.pallas_call(
         functools.partial(others_kernel, count),
         in_specs=[here()] * 2,
         out_specs=[here()] * len(kinds),
         out_shape=[jax.ShapeDtypeStruct((size, step), k) for k in kinds],
-        compiler_params=limit(16),
+        compiler_params=limit(8),
         name="others",
     )(weights, grad)
 
@@ -590,9 +593,9 @@
 def edges_by_pairs(keep, send, count):
     recv = swap(send, "seq", count, 1)
     low, high = join_pair(keep, recv, 2)
-    near = swap(low, "seq", count, 2)
     far = swap(high, "seq", count, 4)
     cross = swap(high, "seq", count, 6)
+    near = swap(low, "seq", count, 2)
     own, other = scan_chips(keep, recv, near, far, cross)
     return own, swap(other, "seq", count, 1)
 
@@ -637,12 +640,36 @@
     return total.astype(BF16)
 
 
+def join_kernel(joint_ref, outer_ref, out_ref):
+    place = lax.axis_index("head")
+    inside = jnp.logical_or(place == 1, place == 2)
+
+    @pl.when(inside)
+    def _():
+        out_ref[...] = (joint_ref[...] + outer_ref[...].astype(F32)).astype(BF16)
+
+    @pl.when(jnp.logical_not(inside))
+    def _():
+        out_ref[...] = joint_ref[...].astype(BF16)
+
+
+def join_outer(joint, outer):
+    return pl.pallas_call(
+        join_kernel,
+        in_specs=[here()] * 2,
+        out_specs=here(),
+        out_shape=jax.ShapeDtypeStruct(joint.shape, BF16),
+        compiler_params=limit(8),
+        name="join_outer",
+    )(joint, outer)
+
+
 def sum_of_four(end, first, joint, own):
-    outer = lax.ppermute(end, "head", [(0, 1), (3, 2)])
+    outer = lax.ppermute(end, "head", [(0, 1), (1, 0), (2, 3), (3, 2)])
     inner = lax.ppermute(end, "head", [(1, 2), (2, 1)])
+    joint = join_outer(joint, outer)
+    joint = lax.ppermute(joint, "head", [(0, 1), (1, 3), (3, 2), (2, 0)])
     ring = lax.ppermute(first, "head", [(0, 2), (2, 3), (3, 1), (1, 0)])
-    joint = (joint + outer.astype(F32)).astype(BF16)
-    joint = lax.ppermute(joint, "head", [(0, 1), (1, 3), (3, 2), (2, 0)])
     total = own + inner.astype(F32) + ring.astype(F32) + joint.astype(F32)
     return total.astype(BF16)
 

time: 53.8 us -> 51.1 us (0.950)
  Pallas kernels: 15.3 us -> 13.1 us
  starting transfers between devices: 13.9 us -> 12.9 us
    ppermute x1, waiting for transfers between devices: 2.84 us -> 0.79 us  [sum_of_four(): outer = lax.ppermute(end, 'head', [(0, 1), (1, 0), (2, 3), (3, 2)])]
    ppermute x1, starting transfers between devices: 3.48 us -> 1.64 us  [sum_of_four(): outer = lax.ppermute(end, 'head', [(0, 1), (1, 0), (2, 3), (3, 2)])]
    ppermute x1, starting transfers between devices: 2.12 us -> 3.89 us  [sum_of_four(): ring = lax.ppermute(first, 'head', [(0, 2), (2, 3), (3, 1), (1, 0)])]
    pallas_call x1, Pallas kernels: 8.54 us -> 6.99 us  [prepare(): pl.pallas_call(functools.partial(prepare_kernel, half, pieces), in_specs=...]
    ppermute x1, waiting for transfers between devices: 7.96 us -> 9.37 us  [sum_of_four(): joint = lax.ppermute(joint, 'head', [(0, 1), (1, 3), (3, 2), (2, 0)])]
    ppermute x1, waiting for transfers between devices: 3.06 us -> 4.22 us  [sum_of_four(): ring = lax.ppermute(first, 'head', [(0, 2), (2, 3), (3, 1), (1, 0)])]
    pallas_call x1, Pallas kernels: 4.35 us -> 3.25 us  [grads(): pl.pallas_call(functools.partial(grads_kernel, half, count), in_specs=[he...]
    ppermute x1, starting transfers between devices: 2.53 us -> 1.65 us  [sum_of_four(): joint = lax.ppermute(joint, 'head', [(0, 1), (1, 3), (3, 2), (2, 0)])]
  transfers between devices with their start and end apart: 9 -> 9, of which waited for: 8 -> 8; matrix products, arithmetic and copies ran while one was open for 0% -> 0% of each run, Pallas kernels for 3% -> 4%
where the time goes in v5:
time: 51.1 us; the launch traced here: 50.9 us
  waiting for transfers between devices  24 us (47%)
  Pallas kernels  13.1 us (26%)
  starting transfers between devices  12.9 us (25%)
  other arithmetic  0.84 us (2%)
    ppermute x5, waiting for transfers between devices, swap(): return lax.ppermute(value, axis, [(i, i ^ mask) for i in range(count)])  9.59 us
    ppermute x1, waiting for transfers between devices, sum_of_four(): joint = lax.ppermute(joint, 'head', [(0, 1), (1, 3), (3, 2), (2, 0)])  9.37 us
    pallas_call x1, Pallas kernels, prepare(): pl.pallas_call(functools.partial(prepare_kernel, half, pieces), in_specs=...  6.99 us
    ppermute x5, starting transfers between devices, swap(): return lax.ppermute(value, axis, [(i, i ^ mask) for i in range(count)])  5.07 us
    ppermute x1, waiting for transfers between devices, sum_of_four(): ring = lax.ppermute(first, 'head', [(0, 2), (2, 3), (3, 1), (1, 0)])  4.22 us
    ppermute x1, starting transfers between devices, sum_of_four(): ring = lax.ppermute(first, 'head', [(0, 2), (2, 3), (3, 1), (1, 0)])  3.89 us
    pallas_call x1, Pallas kernels, grads(): pl.pallas_call(functools.partial(grads_kernel, half, count), in_specs=[he...  3.25 us
    ppermute x1, starting transfers between devices, sum_of_four(): joint = lax.ppermute(joint, 'head', [(0, 1), (1, 3), (3, 2), (2, 0)])  1.65 us
  transfers between devices with their start and end apart: 9, of which 8 were waited for; matrix products, arithmetic and copies ran while one was open for 0% of the time, Pallas kernels for 4%

profile of v5, /device:TPU:0, one launch (start us, length us, event | category | flops | bytes accessed | tf_op | source)
XLA Modules:
  0.0 50.9 jit_solution(6514487952735262583)
XLA Ops:
  0.0 7.0 %prepare.1 = (bf16[3,2048,512]{2,1,0:T(8,128)(2,1)S(1)}, bf16[256,512]{1,0:T(8,128)(2,1)S(1)}, f32[2,256,512]{2,1,0:T(8,128)S(1)}, f32[256,8]{1,0:T(8,128)S(1)},...) custom-call(bf16[256,2048]{1,0:T(8,128)(2,1)} %tok_hbm.1, ...), custom_call_target="tpu_custom_call" | custom-call | tf_op jit(solution)/shard_map/prepare/pallas_call | solution.py:301
  7.0 0.5 %collective-permute-start = (bf16[2,3,128,128]{3,2,1,0:T(8,128)(2,1)S(1)}, bf16[2,3,128,128]{3,2,1,0:T(8,128)(2,1)S(1)}, u32[]{:S(2)}, u32[]{:S(2)}) collective-permute-start(bf16[2,3,128,128]{3,2,1,0:T(8,128)(2,1)S(1)} %get-tuple-element.47), channel_id=1, source_target_pairs={{0,4},{4,0},{8,12},{12,8},{16,20},{20,16},{24,28},{28,24},{1,5},{5... | collective-permute-start | bytes 589832 | tf_op jit(solution)/shard_map/ppermute | solution.py:590
  7.5 1.1 %collective-permute-done.recv_ref = bf16[2,3,128,128]{3,2,1,0:T(8,128)(2,1)S(1)} collective-permute-done((bf16[2,3,128,128]{3,2,1,0:T(8,128)(2,1)S(1)}, bf16[2,3,128,128]{3,2,1,0:T(8,128)(2,1)S(1)}, u32[]{:S(2)}, u32[]{:S(2)}) %collective-permute-start) | collective-permute-done | bytes 196640 | tf_op jit(solution)/shard_map/ppermute | solution.py:590
  8.6 0.2 join_pair.1
  8.8 2.9 %collective-permute-start.1 = (bf16[2,2,128,128]{3,2,1,0:T(8,128)(2,1)S(1)}, bf16[2,2,128,128]{3,2,1,0:T(8,128)(2,1)S(1)}, u32[]{:S(2)}, u32[]{:S(2)}) collective-permute-start(bf16[2,2,128,128]{3,2,1,0:T(8,128)(2,1)S(1)} %get-tuple-element.48), channel_id=1, source_target_pairs={{0,8},{4,12},{8,0},{12,4},{16,24},{20,28},{24,16},{28,20},{1,9},{5... | collective-permute-start | bytes 393224 | tf_op jit(solution)/shard_map/ppermute | solution.py:590
  11.7 1.5 %collective-permute-start.3 = (bf16[2,2,128,128]{3,2,1,0:T(8,128)(2,1)S(1)}, bf16[2,2,128,128]{3,2,1,0:T(8,128)(2,1)S(1)}, u32[]{:S(2)}, u32[]{:S(2)}) collective-permute-start(bf16[2,2,128,128]{3,2,1,0:T(8,128)(2,1)S(1)} %get-tuple-element.49), channel_id=1, source_target_pairs={{0,24},{4,28},{8,16},{12,20},{16,8},{20,12},{24,0},{28,4},{1,25},{... | collective-permute-start | bytes 393224 | tf_op jit(solution)/shard_map/ppermute | solution.py:590
  13.2 0.0 collective-permute-start.2
  13.3 2.6 %collective-permute-done.1.near_ref = bf16[2,2,128,128]{3,2,1,0:T(8,128)(2,1)S(1)} collective-permute-done((bf16[2,2,128,128]{3,2,1,0:T(8,128)(2,1)S(1)}, bf16[2,2,128,128]{3,2,1,0:T(8,128)(2,1)S(1)}, u32[]{:S(2)}, u32[]{:S(2)}) %collective-permute-start.1) | collective-permute-done | bytes 131104 | tf_op jit(solution)/shard_map/ppermute | solution.py:590
  15.9 3.7 %collective-permute-done.3.cross_ref = bf16[2,2,128,128]{3,2,1,0:T(8,128)(2,1)S(1)} collective-permute-done((bf16[2,2,128,128]{3,2,1,0:T(8,128)(2,1)S(1)}, bf16[2,2,128,128]{3,2,1,0:T(8,128)(2,1)S(1)}, u32[]{:S(2)}, u32[]{:S(2)}) %collective-permute-start.3) | collective-permute-done | bytes 131104 | tf_op jit(solution)/shard_map/ppermute | solution.py:590
  19.7 1.4 %collective-permute-done.2.far_ref = bf16[2,2,128,128]{3,2,1,0:T(8,128)(2,1)S(1)} collective-permute-done((bf16[2,2,128,128]{3,2,1,0:T(8,128)(2,1)S(1)}, bf16[2,2,128,128]{3,2,1,0:T(8,128)(2,1)S(1)}, u32[]{:S(2)}, u32[]{:S(2)}) %collective-permute-start.2) | collective-permute-done | bytes 131104 | tf_op jit(solution)/shard_map/ppermute | solution.py:590
  21.0 0.7 %scan_chips.1 = (bf16[2,2,128,128]{3,2,1,0:T(8,128)(2,1)S(1)}, bf16[2,2,128,128]{3,2,1,0:T(8,128)(2,1)S(1)}) custom-call(bf16[2,3,128,128]{3,2,1,0:T(8,128)(2,1)S(1)} %get-tuple-element.46.keep_ref, bf16[2,3,128,128]{3,2,1,0:T(8,128)(2,1)S(1)} %collective-permute-done.recv_ref, bf16[2,2,128,128]{3,2,1,0:T(8,128)(2,1)S(1)} %collective-permute-done.1.near_ref, ...), custom_call_target="tpu_custom_call" | custom-call | tf_op jit(solution)/shard_map/scan_chips/pallas_call | solution.py:453
  21.7 0.1 collective-permute-start.4
  21.8 0.5 %weigh.1 = (f32[4,256,256]{2,1,0:T(8,128)S(1)}, f32[4,256,256]{2,1,0:T(8,128)S(1)}, f32[4,256,256]{2,1,0:T(8,128)S(1)}, f32[4,256,256]{2,1,0:T(8,128)S(1)}) custom-call(f32[8,256]{1,0:T(8,128)S(1)} %get-tuple-element.41.lane_ref, f32[256,8]{1,0:T(8,128)S(1)} %get-tuple-element.34.col_ref), custom_call_target="tpu_custom_call" | custom-call | tf_op jit(solution)/shard_map/weigh/pallas_call | solution.py:341
  22.3 0.8 %collective-permute-done.4.recv_ref = bf16[2,2,128,128]{3,2,1,0:T(8,128)(2,1)S(1)} collective-permute-done((bf16[2,2,128,128]{3,2,1,0:T(8,128)(2,1)S(1)}, bf16[2,2,128,128]{3,2,1,0:T(8,128)(2,1)S(1)}, u32[]{:S(2)}, u32[]{:S(2)}) %collective-permute-start.4) | collective-permute-done | bytes 131104 | tf_op jit(solution)/shard_map/ppermute | solution.py:590
  23.1 3.2 %grads.1 = (bf16[3,256,512]{2,1,0:T(8,128)(2,1)S(1)}, bf16[256,512]{1,0:T(8,128)(2,1)S(1)}) custom-call(bf16[3,2048,512]{2,1,0:T(8,128)(2,1)S(1)} %get-tuple-element.31.w_ref, f32[2,256,512]{2,1,0:T(8,128)S(1)} %get-tuple-element.32.unit_ref, f32[256,8]{1,0:T(8,128)S(1)} %get-tuple-element.33.scale_ref, f32[256,8]{1,0:T(8,128)S(1)} %get-tuple-element.34.col_ref, ...), custom_call_target="tpu_custom_call" | custom-call | tf_op jit(solution)/shard_map/grads/pallas_call | solution.py:554
  26.4 1.6 %collective-permute-start.7 = (bf16[256,512]{1,0:T(8,128)(2,1)S(1)}, bf16[256,512]{1,0:T(8,128)(2,1)S(1)}, u32[]{:S(2)}, u32[]{:S(2)}) collective-permute-start(bf16[256,512]{1,0:T(8,128)(2,1)S(1)} %get-tuple-element.54), channel_id=1, source_target_pairs={{0,1},{1,0},{2,3},{3,2},{4,5},{5,4},{6,7},{7,6},{8,9},{9,8},{10,11... | collective-permute-start | bytes 786440 | tf_op jit(solution)/shard_map/ppermute | solution.py:668
  28.0 0.7 %collective-permute-start.5 = (bf16[256,512]{1,0:T(8,128)(2,1)S(1)}, bf16[256,512]{1,0:T(8,128)(2,1)S(1)}, u32[]{:S(2)}, u32[]{:S(2)}) collective-permute-start(bf16[256,512]{1,0:T(8,128)(2,1)S(1)} %get-tuple-element.54), channel_id=1, source_target_pairs={{1,2},{2,1},{5,6},{6,5},{9,10},{10,9},{13,14},{14,13},{17,18},{18,... | collective-permute-start | bytes 786440 | tf_op jit(solution)/shard_map/ppermute | solution.py:669
  28.7 1.4 %others.1 = (bf16[256,512]{1,0:T(8,128)(2,1)S(1)}, f32[256,512]{1,0:T(8,128)S(1)}, f32[256,512]{1,0:T(8,128)S(1)}) custom-call(bf16[3,2048,512]{2,1,0:T(8,128)(2,1)S(1)} %get-tuple-element.31.w_ref, bf16[3,256,512]{2,1,0:T(8,128)(2,1)S(1)} %get-tuple-element.52.grad_ref), custom_call_target="tpu_custom_call" | custom-call | tf_op jit(solution)/shard_map/others/pallas_call | solution.py:579
  30.1 3.9 %collective-permute-start.6 = (bf16[256,512]{1,0:T(8,128)(2,1)S(1)}, bf16[256,512]{1,0:T(8,128)(2,1)S(1)}, u32[]{:S(2)}, u32[]{:S(2)}) collective-permute-start(bf16[256,512]{1,0:T(8,128)(2,1)S(1)} %get-tuple-element.55), channel_id=1, source_target_pairs={{0,2},{2,3},{3,1},{1,0},{4,6},{6,7},{7,5},{5,4},{8,10},{10,11},{11... | collective-permute-start | bytes 786440 | tf_op jit(solution)/shard_map/ppermute | solution.py:672
  34.0 0.8 %collective-permute-done.7.outer_ref = bf16[256,512]{1,0:T(8,128)(2,1)S(1)} collective-permute-done((bf16[256,512]{1,0:T(8,128)(2,1)S(1)}, bf16[256,512]{1,0:T(8,128)(2,1)S(1)}, u32[]{:S(2)}, u32[]{:S(2)}) %collective-permute-start.7) | collective-permute-done | bytes 262176 | tf_op jit(solution)/shard_map/ppermute | solution.py:668
  34.8 1.7 %collective-permute-start.8 = (bf16[256,512]{1,0:T(8,128)(2,1)S(1)}, bf16[256,512]{1,0:T(8,128)(2,1)S(1)}, u32[]{:S(2)}, u32[]{:S(2)}) collective-permute-start(bf16[256,512]{1,0:T(8,128)(2,1)S(1)} %join_outer.1), channel_id=1, source_target_pairs={{0,1},{1,3},{3,2},{2,0},{4,5},{5,7},{7,6},{6,4},{8,9},{9,11},{11,1... | collective-permute-start | bytes 786440 | tf_op jit(solution)/shard_map/ppermute | solution.py:671
  36.5 4.2 %collective-permute-done.6 = bf16[256,512]{1,0:T(8,128)(2,1)S(1)} collective-permute-done((bf16[256,512]{1,0:T(8,128)(2,1)S(1)}, bf16[256,512]{1,0:T(8,128)(2,1)S(1)}, u32[]{:S(2)}, u32[]{:S(2)}) %collective-permute-start.6) | collective-permute-done | bytes 262176 | tf_op jit(solution)/shard_map/ppermute | solution.py:672
  40.7 0.0 collective-permute-done.5
  40.7 9.4 %collective-permute-done.8 = bf16[256,512]{1,0:T(8,128)(2,1)S(1)} collective-permute-done((bf16[256,512]{1,0:T(8,128)(2,1)S(1)}, bf16[256,512]{1,0:T(8,128)(2,1)S(1)}, u32[]{:S(2)}, u32[]{:S(2)}) %collective-permute-start.8) | collective-permute-done | bytes 262176 | tf_op jit(solution)/shard_map/ppermute | solution.py:671
  50.1 0.8 %add_convert_fusion = bf16[256,512]{1,0:T(8,128)(2,1)} fusion(bf16[256,512]{1,0:T(8,128)(2,1)S(1)} %collective-permute-done.8, bf16[256,512]{1,0:T(8,128)(2,1)S(1)} %collective-permute-done.6, f32[256,512]{1,0:T(8,128)S(1)} %get-tuple-element.53, bf16[256,512]{1,0:T(8,128)(2,1)S(1)} %collective-permute-done.5), kind=kLoop, calls=%fused_computation | loop fusion | flops 917504 | bytes 1572864 | tf_op jit(solution)/shard_map/convert_element_type | solution.py:674
  (1 shorter events, 0.0 us)
Async XLA Ops:
  7.0 1.6 %collective-permute-start = (bf16[2,3,128,128]{3,2,1,0:T(8,128)(2,1)S(1)}, bf16[2,3,128,128]{3,2,1,0:T(8,128)(2,1)S(1)}, u32[]{:S(2)}, u32[]{:S(2)}) collective-permute-start(bf16[2,3,128,128]{3,2,1,0:T(8,128)(2,1)S(1)} %get-tuple-element.47), channel_id=1, source_target_pairs={{0,4},{4,0},{8,12},{12,8},{16,20},{20,16},{24,28},{28,24},{1,5},{5... | collective-permute-start | bytes 589832 | tf_op jit(solution)/shard_map/ppermute | solution.py:590
  8.8 7.1 %collective-permute-start.1 = (bf16[2,2,128,128]{3,2,1,0:T(8,128)(2,1)S(1)}, bf16[2,2,128,128]{3,2,1,0:T(8,128)(2,1)S(1)}, u32[]{:S(2)}, u32[]{:S(2)}) collective-permute-start(bf16[2,2,128,128]{3,2,1,0:T(8,128)(2,1)S(1)} %get-tuple-element.48), channel_id=1, source_target_pairs={{0,8},{4,12},{8,0},{12,4},{16,24},{20,28},{24,16},{28,20},{1,9},{5... | collective-permute-start | bytes 393224 | tf_op jit(solution)/shard_map/ppermute | solution.py:590
  11.7 7.9 %collective-permute-start.3 = (bf16[2,2,128,128]{3,2,1,0:T(8,128)(2,1)S(1)}, bf16[2,2,128,128]{3,2,1,0:T(8,128)(2,1)S(1)}, u32[]{:S(2)}, u32[]{:S(2)}) collective-permute-start(bf16[2,2,128,128]{3,2,1,0:T(8,128)(2,1)S(1)} %get-tuple-element.49), channel_id=1, source_target_pairs={{0,24},{4,28},{8,16},{12,20},{16,8},{20,12},{24,0},{28,4},{1,25},{... | collective-permute-start | bytes 393224 | tf_op jit(solution)/shard_map/ppermute | solution.py:590
  13.2 7.8 %collective-permute-start.2 = (bf16[2,2,128,128]{3,2,1,0:T(8,128)(2,1)S(1)}, bf16[2,2,128,128]{3,2,1,0:T(8,128)(2,1)S(1)}, u32[]{:S(2)}, u32[]{:S(2)}) collective-permute-start(bf16[2,2,128,128]{3,2,1,0:T(8,128)(2,1)S(1)} %get-tuple-element.49), channel_id=1, source_target_pairs={{0,16},{4,20},{8,24},{12,28},{16,0},{20,4},{24,8},{28,12},{1,17},{... | collective-permute-start | bytes 393224 | tf_op jit(solution)/shard_map/ppermute | solution.py:590
  21.7 1.4 %collective-permute-start.4 = (bf16[2,2,128,128]{3,2,1,0:T(8,128)(2,1)S(1)}, bf16[2,2,128,128]{3,2,1,0:T(8,128)(2,1)S(1)}, u32[]{:S(2)}, u32[]{:S(2)}) collective-permute-start(bf16[2,2,128,128]{3,2,1,0:T(8,128)(2,1)S(1)} %get-tuple-element.51), channel_id=1, source_target_pairs={{0,4},{4,0},{8,12},{12,8},{16,20},{20,16},{24,28},{28,24},{1,5},{5... | collective-permute-start | bytes 393224 | tf_op jit(solution)/shard_map/ppermute | solution.py:590
  26.4 8.4 %collective-permute-start.7 = (bf16[256,512]{1,0:T(8,128)(2,1)S(1)}, bf16[256,512]{1,0:T(8,128)(2,1)S(1)}, u32[]{:S(2)}, u32[]{:S(2)}) collective-permute-start(bf16[256,512]{1,0:T(8,128)(2,1)S(1)} %get-tuple-element.54), channel_id=1, source_target_pairs={{0,1},{1,0},{2,3},{3,2},{4,5},{5,4},{6,7},{7,6},{8,9},{9,8},{10,11... | collective-permute-start | bytes 786440 | tf_op jit(solution)/shard_map/ppermute | solution.py:668
  28.0 12.7 %collective-permute-start.5 = (bf16[256,512]{1,0:T(8,128)(2,1)S(1)}, bf16[256,512]{1,0:T(8,128)(2,1)S(1)}, u32[]{:S(2)}, u32[]{:S(2)}) collective-permute-start(bf16[256,512]{1,0:T(8,128)(2,1)S(1)} %get-tuple-element.54), channel_id=1, source_target_pairs={{1,2},{2,1},{5,6},{6,5},{9,10},{10,9},{13,14},{14,13},{17,18},{18,... | collective-permute-start | bytes 786440 | tf_op jit(solution)/shard_map/ppermute | solution.py:669
  30.1 10.6 %collective-permute-start.6 = (bf16[256,512]{1,0:T(8,128)(2,1)S(1)}, bf16[256,512]{1,0:T(8,128)(2,1)S(1)}, u32[]{:S(2)}, u32[]{:S(2)}) collective-permute-start(bf16[256,512]{1,0:T(8,128)(2,1)S(1)} %get-tuple-element.55), channel_id=1, source_target_pairs={{0,2},{2,3},{3,1},{1,0},{4,6},{6,7},{7,5},{5,4},{8,10},{10,11},{11... | collective-permute-start | bytes 786440 | tf_op jit(solution)/shard_map/ppermute | solution.py:672
  34.8 15.2 %collective-permute-start.8 = (bf16[256,512]{1,0:T(8,128)(2,1)S(1)}, bf16[256,512]{1,0:T(8,128)(2,1)S(1)}, u32[]{:S(2)}, u32[]{:S(2)}) collective-permute-start(bf16[256,512]{1,0:T(8,128)(2,1)S(1)} %join_outer.1), channel_id=1, source_target_pairs={{0,1},{1,3},{3,2},{2,0},{4,5},{5,7},{7,6},{6,4},{8,9},{9,11},{11,1... | collective-permute-start | bytes 786440 | tf_op jit(solution)/shard_map/ppermute | solution.py:671

commit v6 on v5

--- a/solution.py
+++ b/solution.py
@@ -40,7 +40,8 @@
     rows, cols = grid_ids(size)
     upper = jnp.where(rows <= cols, 1.0, 0.0).astype(BF16)
     high, mid, low = exact_terms(decay)
-    run = nn(high, upper) + nn(mid, upper) + nn(low, upper)
+    run = nn(jnp.concatenate([high, mid, low], axis=0), upper)
+    run = run[:heads] + run[heads : 2 * heads] + run[2 * heads :]
     lanes = [run, 1.0 / (1.0 + jnp.exp(-logit))]
     spare = -2 * heads % 8
     if spare:
@@ -49,8 +50,14 @@
     return lanes, lanes.T
 
 
+def two_terms(value):
+    high = value.astype(BF16)
+    return high, (value - high.astype(F32)).astype(BF16)
+
+
 def unit_rows(tensor):
     scale = lax.rsqrt(jnp.sum(tensor * tensor, axis=-1, keepdims=True) + 1e-06)
+    scale = jnp.broadcast_to(scale, tensor.shape)
     return tensor * scale, scale
 
 
@@ -192,7 +199,7 @@
         for h in every:
             unit, scale = unit_rows(total[:, spans[h]])
             unit_ref[p, :, spans[h]] = unit
-            scale_ref[:, p * heads + h : p * heads + h + 1] = scale
+            scale_ref[p, :, spans[h]] = scale
 
     small[2].wait()
     for h in every:
@@ -287,7 +294,7 @@
         ((members, depth, columns), BF16),
         ((size, columns), BF16),
         ((2, size, columns), F32),
-        ((size, 2 * heads), F32),
+        ((2, size, columns), F32),
         ((gate_rows, size), F32),
         ((size, gate_rows), F32),
         ((heads, size, width), F32),
@@ -387,11 +394,6 @@
     )(keep, recv)
 
 
-def two_terms(value):
-    high = value.astype(BF16)
-    return high, (value - high.astype(F32)).astype(BF16)
-
-
 def scan_kernel(keep_ref, recv_ref, near_ref, far_ref, cross_ref, own_ref, send_ref, enter, leave):
     place = lax.axis_index("seq")
     first = lax.rem(place, 2) == 0
@@ -500,9 +502,10 @@
     update = [(u_ref[h] - nn(wk_ref[h], edge_scr[h, 0])).astype(BF16) for h in every]
     delta_t = [dbt_ref[h] + nn(edge_scr[h, 1], ktt_ref[h]) for h in every]
     delta = [d.T for d in delta_t]
-    totals = [None] * len(outs)
-    group = 2 if heads % 2 == 0 else 1
-    for h in every:
+    ones = jnp.ones((width, width), BF16)
+    slopes = {}
+
+    def contract(h):
         span = spans[h]
         rows = jnp.concatenate([og_ref[:, span], delta[h].astype(BF16)], axis=0)
         lanes = nt(rows, update[h])
@@ -511,26 +514,43 @@
         attend_t = (turned_ref[h] * turned[:, :size]).astype(BF16)
         mix = (strong_ref[h] * lanes[size:] + strong_t_ref[h] * turned[:, size:]).astype(BF16)
         edge = nt(rows, edge_scr[h, 0])
-        query = unit_ref[0, :, span]
-        key = unit_ref[1, :, span]
-        key_b = key.astype(BF16)
-        dq = open_col[h] * edge[:size] + nn(attend, key_b)
+        key_b = unit_ref[1, :, span].astype(BF16)
+        inner = nn(jnp.concatenate([attend, mix], axis=0), key_b)
+        dq = open_col[h] * edge[:size] + inner[:size]
         dk = (
-            nn(attend_t, query.astype(BF16))
-            - nn(mix, key_b)
+            nn(attend_t, unit_ref[0, :, span].astype(BF16))
+            - inner[size:]
             + fade_col[h] * nn(update[h], edge_scr[h, 1])
             - beta[h] * open_col[h] * edge[size:]
         )
-        for slot, unit, slope in ((0, query, dq), (1, key, dk)):
-            scale = scale_ref[:, slot * heads + h : slot * heads + h + 1]
-            along = jnp.sum(unit * slope, axis=-1, keepdims=True)
-            grad_ref[slot, :, span] = (scale * (slope - unit * along)).astype(BF16)
+        slopes[h] = (dq, dk)
         grad_ref[2, :, span] = (beta[h] * delta[h]).astype(BF16)
-        if h % group == group - 1:
-            ready = slice((h - group + 1) * width, (h + 1) * width)
-            for slot in range(len(outs)):
-                part = spread_grads(grad_ref, w_ref, slot, count, ready)
-                totals[slot] = part if h < group else totals[slot] + part
+
+    def project_out(h):
+        span = spans[h]
+        for slot, slope in enumerate(slopes[h]):
+            unit = unit_ref[slot, :, span]
+            along = nn((unit * slope).astype(BF16), ones)
+            grad_ref[slot, :, span] = (scale_ref[slot, :, span] * (slope - unit * along)).astype(BF16)
+
+    totals = [None] * len(outs)
+
+    def emit(group):
+        ready = slice(group[0] * width, (group[-1] + 1) * width)
+        for slot in range(len(outs)):
+            part = spread_grads(grad_ref, w_ref, slot, count, ready)
+            totals[slot] = part if totals[slot] is None else totals[slot] + part
+
+    group = 2 if heads % 2 == 0 else 1
+    groups = [list(range(g, g + group)) for g in range(0, heads, group)]
+    for turn, members in enumerate(groups):
+        for h in members:
+            contract(h)
+        if turn:
+            emit(groups[turn - 1])
+        for h in members:
+            project_out(h)
+    emit(groups[-1])
     for out_ref, total in zip(outs, totals):
         out_ref[...] = total.astype(out_ref.dtype)
 
@@ -538,8 +558,9 @@
 def spread_grads(grad_ref, w_ref, slot, count, span=slice(None)):
     step = w_ref.shape[1] // count
     rows = pl.ds(pl.multiple_of(part_at(slot, count) * step, step), step)
-    total = nt(grad_ref[0, :, span], w_ref[0, rows, span])
-    for member in range(1, grad_ref.shape[0]):
+    last = grad_ref.shape[0] - 1
+    total = nt(grad_ref[last, :, span], w_ref[last, rows, span])
+    for member in range(last):
         total = total + nt(grad_ref[member, :, span], w_ref[member, rows, span])
     return total
 

time: 51.1 us -> 50.2 us (0.982)
  Pallas kernels: 13.1 us -> 12.2 us
    pallas_call x1, Pallas kernels: 3.25 us -> 2.38 us  [grads(): pl.pallas_call(functools.partial(grads_kernel, half, count), in_specs=[he...]
where the time goes in v6:
time: 50.2 us; the launch traced here: 50 us
  waiting for transfers between devices  24 us (48%)
  starting transfers between devices  12.9 us (26%)
  Pallas kernels  12.2 us (24%)
  other arithmetic  0.84 us (2%)
    ppermute x5, waiting for transfers between devices, swap(): return lax.ppermute(value, axis, [(i, i ^ mask) for i in range(count)])  9.58 us
    ppermute x1, waiting for transfers between devices, sum_of_four(): joint = lax.ppermute(joint, 'head', [(0, 1), (1, 3), (3, 2), (2, 0)])  9.36 us
    pallas_call x1, Pallas kernels, prepare(): pl.pallas_call(functools.partial(prepare_kernel, half, pieces), in_specs=...  6.95 us
    ppermute x5, starting transfers between devices, swap(): return lax.ppermute(value, axis, [(i, i ^ mask) for i in range(count)])  5.09 us
    ppermute x1, waiting for transfers between devices, sum_of_four(): ring = lax.ppermute(first, 'head', [(0, 2), (2, 3), (3, 1), (1, 0)])  4.21 us
    ppermute x1, starting transfers between devices, sum_of_four(): ring = lax.ppermute(first, 'head', [(0, 2), (2, 3), (3, 1), (1, 0)])  3.87 us
    pallas_call x1, Pallas kernels, grads(): pl.pallas_call(functools.partial(grads_kernel, half, count), in_specs=[he...  2.38 us
    ppermute x1, starting transfers between devices, sum_of_four(): joint = lax.ppermute(joint, 'head', [(0, 1), (1, 3), (3, 2), (2, 0)])  1.65 us
  transfers between devices with their start and end apart: 9, of which 8 were waited for; matrix products, arithmetic and copies ran while one was open for 0% of the time, Pallas kernels for 4%

profile of v6, /device:TPU:0, one launch (start us, length us, event | category | flops | bytes accessed | tf_op | source)
XLA Modules:
  0.0 50.0 jit_solution(11434095095980534888)
XLA Ops:
  0.0 6.9 %prepare.1 = (bf16[3,2048,512]{2,1,0:T(8,128)(2,1)S(1)}, bf16[256,512]{1,0:T(8,128)(2,1)S(1)}, f32[2,256,512]{2,1,0:T(8,128)S(1)}, f32[2,256,512]{2,1,0:T(8,128)...) custom-call(bf16[256,2048]{1,0:T(8,128)(2,1)} %tok_hbm.1, ...), custom_call_target="tpu_custom_call" | custom-call | tf_op jit(solution)/shard_map/prepare/pallas_call | solution.py:308
  7.0 0.6 %collective-permute-start = (bf16[2,3,128,128]{3,2,1,0:T(8,128)(2,1)S(1)}, bf16[2,3,128,128]{3,2,1,0:T(8,128)(2,1)S(1)}, u32[]{:S(2)}, u32[]{:S(2)}) collective-permute-start(bf16[2,3,128,128]{3,2,1,0:T(8,128)(2,1)S(1)} %get-tuple-element.47), channel_id=1, source_target_pairs={{0,4},{4,0},{8,12},{12,8},{16,20},{20,16},{24,28},{28,24},{1,5},{5... | collective-permute-start | bytes 589832 | tf_op jit(solution)/shard_map/ppermute | solution.py:611
  7.5 1.1 %collective-permute-done.recv_ref = bf16[2,3,128,128]{3,2,1,0:T(8,128)(2,1)S(1)} collective-permute-done((bf16[2,3,128,128]{3,2,1,0:T(8,128)(2,1)S(1)}, bf16[2,3,128,128]{3,2,1,0:T(8,128)(2,1)S(1)}, u32[]{:S(2)}, u32[]{:S(2)}) %collective-permute-start) | collective-permute-done | bytes 196640 | tf_op jit(solution)/shard_map/ppermute | solution.py:611
  8.6 0.2 join_pair.1
  8.8 2.9 %collective-permute-start.1 = (bf16[2,2,128,128]{3,2,1,0:T(8,128)(2,1)S(1)}, bf16[2,2,128,128]{3,2,1,0:T(8,128)(2,1)S(1)}, u32[]{:S(2)}, u32[]{:S(2)}) collective-permute-start(bf16[2,2,128,128]{3,2,1,0:T(8,128)(2,1)S(1)} %get-tuple-element.48), channel_id=1, source_target_pairs={{0,8},{4,12},{8,0},{12,4},{16,24},{20,28},{24,16},{28,20},{1,9},{5... | collective-permute-start | bytes 393224 | tf_op jit(solution)/shard_map/ppermute | solution.py:611
  11.7 1.5 %collective-permute-start.3 = (bf16[2,2,128,128]{3,2,1,0:T(8,128)(2,1)S(1)}, bf16[2,2,128,128]{3,2,1,0:T(8,128)(2,1)S(1)}, u32[]{:S(2)}, u32[]{:S(2)}) collective-permute-start(bf16[2,2,128,128]{3,2,1,0:T(8,128)(2,1)S(1)} %get-tuple-element.49), channel_id=1, source_target_pairs={{0,24},{4,28},{8,16},{12,20},{16,8},{20,12},{24,0},{28,4},{1,25},{... | collective-permute-start | bytes 393224 | tf_op jit(solution)/shard_map/ppermute | solution.py:611
  13.2 0.1 collective-permute-start.2
  13.3 2.6 %collective-permute-done.1.near_ref = bf16[2,2,128,128]{3,2,1,0:T(8,128)(2,1)S(1)} collective-permute-done((bf16[2,2,128,128]{3,2,1,0:T(8,128)(2,1)S(1)}, bf16[2,2,128,128]{3,2,1,0:T(8,128)(2,1)S(1)}, u32[]{:S(2)}, u32[]{:S(2)}) %collective-permute-start.1) | collective-permute-done | bytes 131104 | tf_op jit(solution)/shard_map/ppermute | solution.py:611
  15.9 3.7 %collective-permute-done.3.cross_ref = bf16[2,2,128,128]{3,2,1,0:T(8,128)(2,1)S(1)} collective-permute-done((bf16[2,2,128,128]{3,2,1,0:T(8,128)(2,1)S(1)}, bf16[2,2,128,128]{3,2,1,0:T(8,128)(2,1)S(1)}, u32[]{:S(2)}, u32[]{:S(2)}) %collective-permute-start.3) | collective-permute-done | bytes 131104 | tf_op jit(solution)/shard_map/ppermute | solution.py:611
  19.6 1.4 %collective-permute-done.2.far_ref = bf16[2,2,128,128]{3,2,1,0:T(8,128)(2,1)S(1)} collective-permute-done((bf16[2,2,128,128]{3,2,1,0:T(8,128)(2,1)S(1)}, bf16[2,2,128,128]{3,2,1,0:T(8,128)(2,1)S(1)}, u32[]{:S(2)}, u32[]{:S(2)}) %collective-permute-start.2) | collective-permute-done | bytes 131104 | tf_op jit(solution)/shard_map/ppermute | solution.py:611
  21.0 0.7 %scan_chips.1 = (bf16[2,2,128,128]{3,2,1,0:T(8,128)(2,1)S(1)}, bf16[2,2,128,128]{3,2,1,0:T(8,128)(2,1)S(1)}) custom-call(bf16[2,3,128,128]{3,2,1,0:T(8,128)(2,1)S(1)} %get-tuple-element.46.keep_ref, bf16[2,3,128,128]{3,2,1,0:T(8,128)(2,1)S(1)} %collective-permute-done.recv_ref, bf16[2,2,128,128]{3,2,1,0:T(8,128)(2,1)S(1)} %collective-permute-done.1.near_ref, ...), custom_call_target="tpu_custom_call" | custom-call | tf_op jit(solution)/shard_map/scan_chips/pallas_call | solution.py:455
  21.7 0.1 collective-permute-start.4
  21.8 0.5 %weigh.1 = (f32[4,256,256]{2,1,0:T(8,128)S(1)}, f32[4,256,256]{2,1,0:T(8,128)S(1)}, f32[4,256,256]{2,1,0:T(8,128)S(1)}, f32[4,256,256]{2,1,0:T(8,128)S(1)}) custom-call(f32[8,256]{1,0:T(8,128)S(1)} %get-tuple-element.41.lane_ref, f32[256,8]{1,0:T(8,128)S(1)} %get-tuple-element.34.col_ref), custom_call_target="tpu_custom_call" | custom-call | tf_op jit(solution)/shard_map/weigh/pallas_call | solution.py:348
  22.3 0.8 %collective-permute-done.4.recv_ref = bf16[2,2,128,128]{3,2,1,0:T(8,128)(2,1)S(1)} collective-permute-done((bf16[2,2,128,128]{3,2,1,0:T(8,128)(2,1)S(1)}, bf16[2,2,128,128]{3,2,1,0:T(8,128)(2,1)S(1)}, u32[]{:S(2)}, u32[]{:S(2)}) %collective-permute-start.4) | collective-permute-done | bytes 131104 | tf_op jit(solution)/shard_map/ppermute | solution.py:611
  23.1 2.4 %grads.1 = (bf16[3,256,512]{2,1,0:T(8,128)(2,1)S(1)}, bf16[256,512]{1,0:T(8,128)(2,1)S(1)}) custom-call(bf16[3,2048,512]{2,1,0:T(8,128)(2,1)S(1)} %get-tuple-element.31.w_ref, f32[2,256,512]{2,1,0:T(8,128)S(1)} %get-tuple-element.32.unit_ref, f32[2,256,512]{2,1,0:T(8,128)S(1)} %get-tuple-element.33.scale_ref, f32[256,8]{1,0:T(8,128)S(1)} %get-tuple-element.34.col_ref, ...), custom_call_target="tpu_custom_call" | custom-call | tf_op jit(solution)/shard_map/grads/pallas_call | solution.py:575
  25.5 1.6 %collective-permute-start.7 = (bf16[256,512]{1,0:T(8,128)(2,1)S(1)}, bf16[256,512]{1,0:T(8,128)(2,1)S(1)}, u32[]{:S(2)}, u32[]{:S(2)}) collective-permute-start(bf16[256,512]{1,0:T(8,128)(2,1)S(1)} %get-tuple-element.54), channel_id=1, source_target_pairs={{0,1},{1,0},{2,3},{3,2},{4,5},{5,4},{6,7},{7,6},{8,9},{9,8},{10,11... | collective-permute-start | bytes 786440 | tf_op jit(solution)/shard_map/ppermute | solution.py:689
  27.1 0.7 %collective-permute-start.5 = (bf16[256,512]{1,0:T(8,128)(2,1)S(1)}, bf16[256,512]{1,0:T(8,128)(2,1)S(1)}, u32[]{:S(2)}, u32[]{:S(2)}) collective-permute-start(bf16[256,512]{1,0:T(8,128)(2,1)S(1)} %get-tuple-element.54), channel_id=1, source_target_pairs={{1,2},{2,1},{5,6},{6,5},{9,10},{10,9},{13,14},{14,13},{17,18},{18,... | collective-permute-start | bytes 786440 | tf_op jit(solution)/shard_map/ppermute | solution.py:690
  27.8 1.4 %others.1 = (bf16[256,512]{1,0:T(8,128)(2,1)S(1)}, f32[256,512]{1,0:T(8,128)S(1)}, f32[256,512]{1,0:T(8,128)S(1)}) custom-call(bf16[3,2048,512]{2,1,0:T(8,128)(2,1)S(1)} %get-tuple-element.31.w_ref, bf16[3,256,512]{2,1,0:T(8,128)(2,1)S(1)} %get-tuple-element.52.grad_ref), custom_call_target="tpu_custom_call" | custom-call | tf_op jit(solution)/shard_map/others/pallas_call | solution.py:600
  29.2 3.9 %collective-permute-start.6 = (bf16[256,512]{1,0:T(8,128)(2,1)S(1)}, bf16[256,512]{1,0:T(8,128)(2,1)S(1)}, u32[]{:S(2)}, u32[]{:S(2)}) collective-permute-start(bf16[256,512]{1,0:T(8,128)(2,1)S(1)} %get-tuple-element.55), channel_id=1, source_target_pairs={{0,2},{2,3},{3,1},{1,0},{4,6},{6,7},{7,5},{5,4},{8,10},{10,11},{11... | collective-permute-start | bytes 786440 | tf_op jit(solution)/shard_map/ppermute | solution.py:693
  33.1 0.8 %collective-permute-done.7.outer_ref = bf16[256,512]{1,0:T(8,128)(2,1)S(1)} collective-permute-done((bf16[256,512]{1,0:T(8,128)(2,1)S(1)}, bf16[256,512]{1,0:T(8,128)(2,1)S(1)}, u32[]{:S(2)}, u32[]{:S(2)}) %collective-permute-start.7) | collective-permute-done | bytes 262176 | tf_op jit(solution)/shard_map/ppermute | solution.py:689
  33.9 1.7 %collective-permute-start.8 = (bf16[256,512]{1,0:T(8,128)(2,1)S(1)}, bf16[256,512]{1,0:T(8,128)(2,1)S(1)}, u32[]{:S(2)}, u32[]{:S(2)}) collective-permute-start(bf16[256,512]{1,0:T(8,128)(2,1)S(1)} %join_outer.1), channel_id=1, source_target_pairs={{0,1},{1,3},{3,2},{2,0},{4,5},{5,7},{7,6},{6,4},{8,9},{9,11},{11,1... | collective-permute-start | bytes 786440 | tf_op jit(solution)/shard_map/ppermute | solution.py:692
  35.6 4.2 %collective-permute-done.6 = bf16[256,512]{1,0:T(8,128)(2,1)S(1)} collective-permute-done((bf16[256,512]{1,0:T(8,128)(2,1)S(1)}, bf16[256,512]{1,0:T(8,128)(2,1)S(1)}, u32[]{:S(2)}, u32[]{:S(2)}) %collective-permute-start.6) | collective-permute-done | bytes 262176 | tf_op jit(solution)/shard_map/ppermute | solution.py:693
  39.8 0.0 collective-permute-done.5
  39.8 9.4 %collective-permute-done.8 = bf16[256,512]{1,0:T(8,128)(2,1)S(1)} collective-permute-done((bf16[256,512]{1,0:T(8,128)(2,1)S(1)}, bf16[256,512]{1,0:T(8,128)(2,1)S(1)}, u32[]{:S(2)}, u32[]{:S(2)}) %collective-permute-start.8) | collective-permute-done | bytes 262176 | tf_op jit(solution)/shard_map/ppermute | solution.py:692
  49.2 0.8 %add_convert_fusion = bf16[256,512]{1,0:T(8,128)(2,1)} fusion(bf16[256,512]{1,0:T(8,128)(2,1)S(1)} %collective-permute-done.8, bf16[256,512]{1,0:T(8,128)(2,1)S(1)} %collective-permute-done.6, f32[256,512]{1,0:T(8,128)S(1)} %get-tuple-element.53, bf16[256,512]{1,0:T(8,128)(2,1)S(1)} %collective-permute-done.5), kind=kLoop, calls=%fused_computation | loop fusion | flops 917504 | bytes 1572864 | tf_op jit(solution)/shard_map/convert_element_type | solution.py:695
  (1 shorter events, 0.0 us)
Async XLA Ops:
  7.0 1.6 %collective-permute-start = (bf16[2,3,128,128]{3,2,1,0:T(8,128)(2,1)S(1)}, bf16[2,3,128,128]{3,2,1,0:T(8,128)(2,1)S(1)}, u32[]{:S(2)}, u32[]{:S(2)}) collective-permute-start(bf16[2,3,128,128]{3,2,1,0:T(8,128)(2,1)S(1)} %get-tuple-element.47), channel_id=1, source_target_pairs={{0,4},{4,0},{8,12},{12,8},{16,20},{20,16},{24,28},{28,24},{1,5},{5... | collective-permute-start | bytes 589832 | tf_op jit(solution)/shard_map/ppermute | solution.py:611
  8.8 7.1 %collective-permute-start.1 = (bf16[2,2,128,128]{3,2,1,0:T(8,128)(2,1)S(1)}, bf16[2,2,128,128]{3,2,1,0:T(8,128)(2,1)S(1)}, u32[]{:S(2)}, u32[]{:S(2)}) collective-permute-start(bf16[2,2,128,128]{3,2,1,0:T(8,128)(2,1)S(1)} %get-tuple-element.48), channel_id=1, source_target_pairs={{0,8},{4,12},{8,0},{12,4},{16,24},{20,28},{24,16},{28,20},{1,9},{5... | collective-permute-start | bytes 393224 | tf_op jit(solution)/shard_map/ppermute | solution.py:611
  11.7 7.9 %collective-permute-start.3 = (bf16[2,2,128,128]{3,2,1,0:T(8,128)(2,1)S(1)}, bf16[2,2,128,128]{3,2,1,0:T(8,128)(2,1)S(1)}, u32[]{:S(2)}, u32[]{:S(2)}) collective-permute-start(bf16[2,2,128,128]{3,2,1,0:T(8,128)(2,1)S(1)} %get-tuple-element.49), channel_id=1, source_target_pairs={{0,24},{4,28},{8,16},{12,20},{16,8},{20,12},{24,0},{28,4},{1,25},{... | collective-permute-start | bytes 393224 | tf_op jit(solution)/shard_map/ppermute | solution.py:611
  13.2 7.8 %collective-permute-start.2 = (bf16[2,2,128,128]{3,2,1,0:T(8,128)(2,1)S(1)}, bf16[2,2,128,128]{3,2,1,0:T(8,128)(2,1)S(1)}, u32[]{:S(2)}, u32[]{:S(2)}) collective-permute-start(bf16[2,2,128,128]{3,2,1,0:T(8,128)(2,1)S(1)} %get-tuple-element.49), channel_id=1, source_target_pairs={{0,16},{4,20},{8,24},{12,28},{16,0},{20,4},{24,8},{28,12},{1,17},{... | collective-permute-start | bytes 393224 | tf_op jit(solution)/shard_map/ppermute | solution.py:611
  21.7 1.4 %collective-permute-start.4 = (bf16[2,2,128,128]{3,2,1,0:T(8,128)(2,1)S(1)}, bf16[2,2,128,128]{3,2,1,0:T(8,128)(2,1)S(1)}, u32[]{:S(2)}, u32[]{:S(2)}) collective-permute-start(bf16[2,2,128,128]{3,2,1,0:T(8,128)(2,1)S(1)} %get-tuple-element.51), channel_id=1, source_target_pairs={{0,4},{4,0},{8,12},{12,8},{16,20},{20,16},{24,28},{28,24},{1,5},{5... | collective-permute-start | bytes 393224 | tf_op jit(solution)/shard_map/ppermute | solution.py:611
  25.5 8.4 %collective-permute-start.7 = (bf16[256,512]{1,0:T(8,128)(2,1)S(1)}, bf16[256,512]{1,0:T(8,128)(2,1)S(1)}, u32[]{:S(2)}, u32[]{:S(2)}) collective-permute-start(bf16[256,512]{1,0:T(8,128)(2,1)S(1)} %get-tuple-element.54), channel_id=1, source_target_pairs={{0,1},{1,0},{2,3},{3,2},{4,5},{5,4},{6,7},{7,6},{8,9},{9,8},{10,11... | collective-permute-start | bytes 786440 | tf_op jit(solution)/shard_map/ppermute | solution.py:689
  27.1 12.7 %collective-permute-start.5 = (bf16[256,512]{1,0:T(8,128)(2,1)S(1)}, bf16[256,512]{1,0:T(8,128)(2,1)S(1)}, u32[]{:S(2)}, u32[]{:S(2)}) collective-permute-start(bf16[256,512]{1,0:T(8,128)(2,1)S(1)} %get-tuple-element.54), channel_id=1, source_target_pairs={{1,2},{2,1},{5,6},{6,5},{9,10},{10,9},{13,14},{14,13},{17,18},{18,... | collective-permute-start | bytes 786440 | tf_op jit(solution)/shard_map/ppermute | solution.py:690
  29.2 10.6 %collective-permute-start.6 = (bf16[256,512]{1,0:T(8,128)(2,1)S(1)}, bf16[256,512]{1,0:T(8,128)(2,1)S(1)}, u32[]{:S(2)}, u32[]{:S(2)}) collective-permute-start(bf16[256,512]{1,0:T(8,128)(2,1)S(1)} %get-tuple-element.55), channel_id=1, source_target_pairs={{0,2},{2,3},{3,1},{1,0},{4,6},{6,7},{7,5},{5,4},{8,10},{10,11},{11... | collective-permute-start | bytes 786440 | tf_op jit(solution)/shard_map/ppermute | solution.py:693
  33.9 15.2 %collective-permute-start.8 = (bf16[256,512]{1,0:T(8,128)(2,1)S(1)}, bf16[256,512]{1,0:T(8,128)(2,1)S(1)}, u32[]{:S(2)}, u32[]{:S(2)}) collective-permute-start(bf16[256,512]{1,0:T(8,128)(2,1)S(1)} %join_outer.1), channel_id=1, source_target_pairs={{0,1},{1,3},{3,2},{2,0},{4,5},{5,7},{7,6},{6,4},{8,9},{9,11},{11,1... | collective-permute-start | bytes 786440 | tf_op jit(solution)/shard_map/ppermute | solution.py:692

commit v7 on v6

--- a/solution.py
+++ b/solution.py
@@ -327,11 +327,16 @@
     )(*(pltpu.with_memory_space_constraint(x, pltpu.HBM) for x in (tokens, weights, logit, decay, out_grad)))
 
 
-def weigh_kernel(heads, lane_ref, col_ref, gamma_ref, turned_ref, strong_ref, strong_t_ref):
+def weigh_kernel(
+    heads, lane_ref, col_ref,
+    gamma_ref, turned_ref, strong_ref, strong_t_ref, open_ref, fade_ref, beta_ref,
+):
     size = lane_ref.shape[1]
+    width = open_ref.shape[2]
     rows, cols = grid_ids(size)
     for h in range(heads):
-        gap = col_ref[:, h : h + 1] - lane_ref[h : h + 1, :]
+        run = col_ref[:, h : h + 1]
+        gap = run - lane_ref[h : h + 1, :]
         gamma = jnp.exp(jnp.where(rows >= cols, gap, FAR))
         turned = jnp.exp(jnp.where(rows <= cols, -gap, FAR))
         gamma_ref[h] = gamma
@@ -340,16 +345,20 @@
         beta_row = lane_ref[heads + h : heads + h + 1, :]
         strong_ref[h] = jnp.where(rows > cols, beta * gamma, 0.0)
         strong_t_ref[h] = jnp.where(rows < cols, beta_row * turned, 0.0)
-
-
-def weigh(lanes, cols, heads):
+        open_ref[h] = jnp.broadcast_to(jnp.exp(run), (size, width))
+        fade_ref[h] = jnp.broadcast_to(jnp.exp(run[size - 1 :, :] - run), (size, width))
+        beta_ref[h] = jnp.broadcast_to(beta, (size, width))
+
+
+def weigh(lanes, cols, heads, width):
     size = lanes.shape[1]
-    shape = jax.ShapeDtypeStruct((heads, size, size), F32)
+    shapes = [jax.ShapeDtypeStruct((heads, size, size), F32)] * 4
+    shapes += [jax.ShapeDtypeStruct((heads, size, width), F32)] * 3
     return pl.pallas_call(
         functools.partial(weigh_kernel, heads),
         in_specs=[here()] * 2,
-        out_specs=[here()] * 4,
-        out_shape=[shape] * 4,
+        out_specs=[here()] * len(shapes),
+        out_shape=shapes,
         compiler_params=limit(8),
         name="weigh",
     )(lanes, cols)
@@ -476,135 +485,152 @@
     return jnp.where(place < 2, ends, jnp.where(place == 2, high[0], high[1]))
 
 
-def early_parts():
-    return 1
-
-
-def grads_kernel(
-    half, count, w_ref, unit_ref, scale_ref, col_ref, u_ref, wk_ref, dbt_ref, ktt_ref, gt_ref, og_ref,
-    gamma_ref, turned_ref, strong_ref, strong_t_ref, own_ref, recv_ref,
-    grad_ref, *rest,
-):
-    heads, size, width = u_ref.shape
-    outs, edge_scr = rest[:-1], rest[-1]
-    if half:
-        core = lax.rem(lax.axis_index("seq"), 2)
-        edge_scr[pl.ds(core * half, half)] = own_ref[...]
-        edge_scr[pl.ds((1 - core) * half, half)] = recv_ref[...]
-    else:
-        edge_scr[...] = own_ref[...]
-    every = range(heads)
-    spans = [slice(h * width, (h + 1) * width) for h in every]
-    run_col = [col_ref[:, h : h + 1] for h in every]
-    beta = [col_ref[:, heads + h : heads + h + 1] for h in every]
-    open_col = [jnp.exp(run_col[h]) for h in every]
-    fade_col = [jnp.exp(run_col[h][size - 1 : size, :] - run_col[h]) for h in every]
-    update = [(u_ref[h] - nn(wk_ref[h], edge_scr[h, 0])).astype(BF16) for h in every]
-    delta_t = [dbt_ref[h] + nn(edge_scr[h, 1], ktt_ref[h]) for h in every]
+def base_of(part, many):
+    if part is None:
+        return 0
+    core = lax.rem(lax.axis_index("seq"), 2)
+    return many * (core if part == 0 else 1 - core)
+
+
+def lanes_from(head, width, many=1):
+    if isinstance(head, int):
+        return slice(head * width, (head + many) * width)
+    return pl.ds(pl.multiple_of(head * width, width * many), many * width)
+
+
+def contract(base, refs, edge_ref, grad_ref):
+    (unit_ref, u_ref, wk_ref, dbt_ref, ktt_ref, gt_ref, og_ref) = refs[:7]
+    (gamma_ref, turned_ref, strong_ref, strong_t_ref, open_ref, fade_ref, beta_ref) = refs[7:]
+    _, size, width = u_ref.shape
+    every = range(edge_ref.shape[0])
+    update = [(u_ref[base + i] - nn(wk_ref[base + i], edge_ref[i, 0])).astype(BF16) for i in every]
+    delta_t = [dbt_ref[base + i] + nn(edge_ref[i, 1], ktt_ref[base + i]) for i in every]
     delta = [d.T for d in delta_t]
-    ones = jnp.ones((width, width), BF16)
-    slopes = {}
-
-    def contract(h):
-        span = spans[h]
-        rows = jnp.concatenate([og_ref[:, span], delta[h].astype(BF16)], axis=0)
-        lanes = nt(rows, update[h])
-        turned = nn(update[h], jnp.concatenate([gt_ref[h], delta_t[h].astype(BF16)], axis=1))
+    slopes = []
+    for i in every:
+        h = base + i
+        span = lanes_from(h, width)
+        rows = jnp.concatenate([og_ref[:, span], delta[i].astype(BF16)], axis=0)
+        lanes = nt(rows, update[i])
+        turned = nn(update[i], jnp.concatenate([gt_ref[h], delta_t[i].astype(BF16)], axis=1))
         attend = (gamma_ref[h] * lanes[:size]).astype(BF16)
         attend_t = (turned_ref[h] * turned[:, :size]).astype(BF16)
         mix = (strong_ref[h] * lanes[size:] + strong_t_ref[h] * turned[:, size:]).astype(BF16)
-        edge = nt(rows, edge_scr[h, 0])
+        edge = nt(rows, edge_ref[i, 0])
         key_b = unit_ref[1, :, span].astype(BF16)
         inner = nn(jnp.concatenate([attend, mix], axis=0), key_b)
-        dq = open_col[h] * edge[:size] + inner[:size]
+        dq = open_ref[h] * edge[:size] + inner[:size]
         dk = (
             nn(attend_t, unit_ref[0, :, span].astype(BF16))
             - inner[size:]
-            + fade_col[h] * nn(update[h], edge_scr[h, 1])
-            - beta[h] * open_col[h] * edge[size:]
+            + fade_ref[h] * nn(update[i], edge_ref[i, 1])
+            - beta_ref[h] * open_ref[h] * edge[size:]
         )
-        slopes[h] = (dq, dk)
-        grad_ref[2, :, span] = (beta[h] * delta[h]).astype(BF16)
-
-    def project_out(h):
-        span = spans[h]
-        for slot, slope in enumerate(slopes[h]):
+        grad_ref[2, :, lanes_from(i, width)] = (beta_ref[h] * delta[i]).astype(BF16)
+        slopes.append((dq, dk))
+    return slopes
+
+
+def project_out(base, slopes, unit_ref, scale_ref, grad_ref):
+    width = slopes[0][0].shape[1]
+    ones = jnp.ones((width, width), BF16)
+    for i, pair in enumerate(slopes):
+        span = lanes_from(base + i, width)
+        for slot, slope in enumerate(pair):
             unit = unit_ref[slot, :, span]
             along = nn((unit * slope).astype(BF16), ones)
-            grad_ref[slot, :, span] = (scale_ref[slot, :, span] * (slope - unit * along)).astype(BF16)
-
-    totals = [None] * len(outs)
-
-    def emit(group):
-        ready = slice(group[0] * width, (group[-1] + 1) * width)
-        for slot in range(len(outs)):
-            part = spread_grads(grad_ref, w_ref, slot, count, ready)
-            totals[slot] = part if totals[slot] is None else totals[slot] + part
-
-    group = 2 if heads % 2 == 0 else 1
-    groups = [list(range(g, g + group)) for g in range(0, heads, group)]
-    for turn, members in enumerate(groups):
-        for h in members:
-            contract(h)
-        if turn:
-            emit(groups[turn - 1])
-        for h in members:
-            project_out(h)
-    emit(groups[-1])
-    for out_ref, total in zip(outs, totals):
-        out_ref[...] = total.astype(out_ref.dtype)
-
-
-def spread_grads(grad_ref, w_ref, slot, count, span=slice(None)):
+            change = scale_ref[slot, :, span] * (slope - unit * along)
+            grad_ref[slot, :, lanes_from(i, width)] = change.astype(BF16)
+
+
+def spread_grads(groups, w_ref, slot, count):
     step = w_ref.shape[1] // count
     rows = pl.ds(pl.multiple_of(part_at(slot, count) * step, step), step)
-    last = grad_ref.shape[0] - 1
-    total = nt(grad_ref[last, :, span], w_ref[last, rows, span])
-    for member in range(last):
-        total = total + nt(grad_ref[member, :, span], w_ref[member, rows, span])
+    total = None
+    for base, width, grad_ref in groups:
+        span = lanes_from(base, width, grad_ref.shape[2] // width)
+        for member in (2, 0, 1):
+            part = nt(grad_ref[member], w_ref[member, rows, span])
+            total = part if total is None else total + part
     return total
 
 
-def grads(weights, prepared, out_grad, weighed, own, recv, half):
-    unit, scale, col, u, wk, dbt, ktt, gt = prepared
-    heads, size, width = u.shape
-    members, depth, columns = weights.shape
+def own_kernel(edge_ref, scale_ref, *refs):
+    refs, grad_ref = refs[:-1], refs[-1]
+    base = base_of(0, edge_ref.shape[0])
+    slopes = contract(base, refs, edge_ref, grad_ref)
+    project_out(base, slopes, refs[0], scale_ref, grad_ref)
+
+
+def own_grads(edge, scale, prepared):
+    many, _, width, _ = edge.shape
+    size = scale.shape[1]
+    return pl.pallas_call(
+        own_kernel,
+        in_specs=[here()] * (2 + len(prepared)),
+        out_specs=here(),
+        out_shape=jax.ShapeDtypeStruct((3, size, many * width), BF16),
+        compiler_params=limit(12),
+        name="own_grads",
+    )(edge, scale, *prepared)
+
+
+def grads_kernel(part, count, w_ref, edge_ref, scale_ref, *refs):
+    refs, (grad_ref, out_ref) = refs[:-2], refs[-2:]
+    done = []
+    many, _, width, _ = edge_ref.shape
+    base = base_of(part, many)
+    if part is not None:
+        refs, done = refs[:-1], [(base_of(0, many), width, refs[-1])]
+    slopes = contract(base, refs, edge_ref, grad_ref)
+    total = spread_grads(done, w_ref, 0, count)
+    project_out(base, slopes, refs[0], scale_ref, grad_ref)
+    last = spread_grads([(base, width, grad_ref)], w_ref, 0, count)
+    out_ref[...] = (last if total is None else total + last).astype(out_ref.dtype)
+
+
+def grads(weights, edge, scale, prepared, own):
+    many, _, width, _ = edge.shape
+    size = scale.shape[1]
+    depth = weights.shape[1]
     count = lax.axis_size("head")
-    step = depth // count
-    early = early_parts()
+    more = [] if own is None else [own]
     return pl.pallas_call(
-        functools.partial(grads_kernel, half, count),
-        in_specs=[here()] * 16,
-        out_specs=[here()] * (1 + early),
-        out_shape=[jax.ShapeDtypeStruct((members, size, columns), BF16)]
-        + [jax.ShapeDtypeStruct((size, step), BF16)] * early,
-        scratch_shapes=[
-            pltpu.VMEM((heads, 2, width, width), BF16),
+        functools.partial(grads_kernel, None if own is None else 1, count),
+        in_specs=[here()] * (3 + len(prepared) + len(more)),
+        out_specs=[here()] * 2,
+        out_shape=[
+            jax.ShapeDtypeStruct((3, size, many * width), BF16),
+            jax.ShapeDtypeStruct((size, depth // count), BF16),
         ],
         compiler_params=limit(12),
         name="grads",
-    )(weights, unit, scale, col, u, wk, dbt, ktt, gt, out_grad, *weighed, own, recv)
-
-
-def others_kernel(count, w_ref, grad_ref, *outs):
+    )(weights, edge, scale, *prepared, *more)
+
+
+def others_kernel(count, width, parts, w_ref, *refs):
+    grad_refs, outs = refs[: len(parts)], refs[len(parts) :]
+    groups = [
+        (base_of(part, ref.shape[2] // width), width, ref) for part, ref in zip(parts, grad_refs)
+    ]
     for i, out_ref in enumerate(outs):
-        out_ref[...] = spread_grads(grad_ref, w_ref, i + early_parts(), count).astype(out_ref.dtype)
-
-
-def others(weights, grad):
-    _, depth, _ = weights.shape
-    size = grad.shape[1]
+        out_ref[...] = spread_grads(groups, w_ref, i + 1, count).astype(out_ref.dtype)
+
+
+def others(weights, groups, width):
+    size = groups[0].shape[1]
     count = lax.axis_size("head")
-    step = depth // count
+    step = weights.shape[1] // count
     kinds = [BF16] + [F32] * 2 if count == 4 else [BF16] * (count - 2) + [F32]
+    parts = (None,) if len(groups) == 1 else (0, 1)
     return pl.pallas_call(
-        functools.partial(others_kernel, count),
-        in_specs=[here()] * 2,
+        functools.partial(others_kernel, count, width, parts),
+        in_specs=[here()] * (1 + len(groups)),
         out_specs=[here()] * len(kinds),
         out_shape=[jax.ShapeDtypeStruct((size, step), k) for k in kinds],
         compiler_params=limit(8),
         name="others",
-    )(weights, grad)
+    )(weights, *groups)
 
 
 def swap(value, axis, count, mask):
@@ -707,13 +733,19 @@
         own, recv = edges_by_pairs(keep, send, count)
     else:
         own, recv = edges_by_gather(keep, count)
-    weighed = weigh(lanes, col, heads)
-    prepared = (unit, scale, col, u, wk, dbt, ktt, gt)
-    grad, *early = grads(held, prepared, kept_grad, weighed, own, recv, half)
-    rest = others(held, grad)
+    width = qkv_weight.shape[2] // heads
+    prepared = (unit, u, wk, dbt, ktt, gt, kept_grad, *weigh(lanes, col, heads, width))
+    if paired:
+        own_part = own_grads(own, scale, prepared)
+        grad, end = grads(held, recv, scale, prepared, own_part)
+        groups = [own_part, grad]
+    else:
+        grad, end = grads(held, own, scale, prepared, None)
+        groups = [grad]
+    rest = others(held, groups, width)
     if lax.axis_size("head") == 4:
-        return sum_of_four(*early, *rest)
-    return sum_on_line([rest[-1], *early, *rest[:-1]])
+        return sum_of_four(end, *rest)
+    return sum_on_line([rest[-1], end, *rest[:-1]])
 
 
 def solution(mesh):

time: 50.2 us -> 50.4 us (level)
  Pallas kernels: 12.2 us -> 12.8 us
    ppermute x5, waiting for transfers between devices: 9.58 us -> 8.79 us  [swap(): return lax.ppermute(value, axis, [(i, i ^ mask) for i in range(count)])]
    pallas_call x2 -> x3, Pallas kernels: 3.8 us -> 4.16 us  [the longest x1 1.63 us: grads(): pl.pallas_call(functools.partial(grads_kernel, None if own is None else 1...]
  transfers between devices with their start and end apart: 9 -> 9, of which waited for: 8 -> 7; matrix products, arithmetic and copies ran while one was open for 0% -> 0% of each run, Pallas kernels for 4% -> 7%
where the time goes in v7:
time: 50.4 us; the launch traced here: 50.2 us
  waiting for transfers between devices  23.5 us (47%)
  starting transfers between devices  12.9 us (26%)
  Pallas kernels  12.8 us (25%)
  other arithmetic  0.84 us (2%)
    ppermute x1, waiting for transfers between devices, sum_of_four(): joint = lax.ppermute(joint, 'head', [(0, 1), (1, 3), (3, 2), (2, 0)])  9.45 us
    ppermute x5, waiting for transfers between devices, swap(): return lax.ppermute(value, axis, [(i, i ^ mask) for i in range(count)])  8.79 us
    pallas_call x1, Pallas kernels, prepare(): pl.pallas_call(functools.partial(prepare_kernel, half, pieces), in_specs=...  6.95 us
    ppermute x5, starting transfers between devices, swap(): return lax.ppermute(value, axis, [(i, i ^ mask) for i in range(count)])  5.09 us
    ppermute x1, waiting for transfers between devices, sum_of_four(): ring = lax.ppermute(first, 'head', [(0, 2), (2, 3), (3, 1), (1, 0)])  4.14 us
    ppermute x1, starting transfers between devices, sum_of_four(): ring = lax.ppermute(first, 'head', [(0, 2), (2, 3), (3, 1), (1, 0)])  3.89 us
    ppermute x1, starting transfers between devices, sum_of_four(): joint = lax.ppermute(joint, 'head', [(0, 1), (1, 3), (3, 2), (2, 0)])  1.65 us
    ppermute x1, starting transfers between devices, sum_of_four(): outer = lax.ppermute(end, 'head', [(0, 1), (1, 0), (2, 3), (3, 2)])  1.64 us
  transfers between devices with their start and end apart: 9, of which 7 were waited for; matrix products, arithmetic and copies ran while one was open for 0% of the time, Pallas kernels for 7%

profile of v7, /device:TPU:0, one launch (start us, length us, event | category | flops | bytes accessed | tf_op | source)
XLA Modules:
  0.0 50.2 jit_solution(777200598582957751)
XLA Ops:
  0.0 7.0 %prepare.1 = (bf16[3,2048,512]{2,1,0:T(8,128)(2,1)S(1)}, bf16[256,512]{1,0:T(8,128)(2,1)S(1)}, f32[2,256,512]{2,1,0:T(8,128)S(1)}, f32[2,256,512]{2,1,0:T(8,128)...) custom-call(bf16[256,2048]{1,0:T(8,128)(2,1)} %tok_hbm.1, ...), custom_call_target="tpu_custom_call" | custom-call | tf_op jit(solution)/shard_map/prepare/pallas_call | solution.py:308
  7.0 0.6 %collective-permute-start = (bf16[2,3,128,128]{3,2,1,0:T(8,128)(2,1)S(1)}, bf16[2,3,128,128]{3,2,1,0:T(8,128)(2,1)S(1)}, u32[]{:S(2)}, u32[]{:S(2)}) collective-permute-start(bf16[2,3,128,128]{3,2,1,0:T(8,128)(2,1)S(1)} %get-tuple-element.36), channel_id=1, source_target_pairs={{0,4},{4,0},{8,12},{12,8},{16,20},{20,16},{24,28},{28,24},{1,5},{5... | collective-permute-start | bytes 589832 | tf_op jit(solution)/shard_map/ppermute | solution.py:637
  7.5 1.1 %collective-permute-done.recv_ref = bf16[2,3,128,128]{3,2,1,0:T(8,128)(2,1)S(1)} collective-permute-done((bf16[2,3,128,128]{3,2,1,0:T(8,128)(2,1)S(1)}, bf16[2,3,128,128]{3,2,1,0:T(8,128)(2,1)S(1)}, u32[]{:S(2)}, u32[]{:S(2)}) %collective-permute-start) | collective-permute-done | bytes 196640 | tf_op jit(solution)/shard_map/ppermute | solution.py:637
  8.6 0.2 join_pair.1
  8.8 2.9 %collective-permute-start.1 = (bf16[2,2,128,128]{3,2,1,0:T(8,128)(2,1)S(1)}, bf16[2,2,128,128]{3,2,1,0:T(8,128)(2,1)S(1)}, u32[]{:S(2)}, u32[]{:S(2)}) collective-permute-start(bf16[2,2,128,128]{3,2,1,0:T(8,128)(2,1)S(1)} %get-tuple-element.37), channel_id=1, source_target_pairs={{0,8},{4,12},{8,0},{12,4},{16,24},{20,28},{24,16},{28,20},{1,9},{5... | collective-permute-start | bytes 393224 | tf_op jit(solution)/shard_map/ppermute | solution.py:637
  11.7 1.5 %collective-permute-start.3 = (bf16[2,2,128,128]{3,2,1,0:T(8,128)(2,1)S(1)}, bf16[2,2,128,128]{3,2,1,0:T(8,128)(2,1)S(1)}, u32[]{:S(2)}, u32[]{:S(2)}) collective-permute-start(bf16[2,2,128,128]{3,2,1,0:T(8,128)(2,1)S(1)} %get-tuple-element.38), channel_id=1, source_target_pairs={{0,24},{4,28},{8,16},{12,20},{16,8},{20,12},{24,0},{28,4},{1,25},{... | collective-permute-start | bytes 393224 | tf_op jit(solution)/shard_map/ppermute | solution.py:637
  13.2 0.1 collective-permute-start.2
  13.3 2.6 %collective-permute-done.1.near_ref = bf16[2,2,128,128]{3,2,1,0:T(8,128)(2,1)S(1)} collective-permute-done((bf16[2,2,128,128]{3,2,1,0:T(8,128)(2,1)S(1)}, bf16[2,2,128,128]{3,2,1,0:T(8,128)(2,1)S(1)}, u32[]{:S(2)}, u32[]{:S(2)}) %collective-permute-start.1) | collective-permute-done | bytes 131104 | tf_op jit(solution)/shard_map/ppermute | solution.py:637
  15.9 3.7 %collective-permute-done.3.cross_ref = bf16[2,2,128,128]{3,2,1,0:T(8,128)(2,1)S(1)} collective-permute-done((bf16[2,2,128,128]{3,2,1,0:T(8,128)(2,1)S(1)}, bf16[2,2,128,128]{3,2,1,0:T(8,128)(2,1)S(1)}, u32[]{:S(2)}, u32[]{:S(2)}) %collective-permute-start.3) | collective-permute-done | bytes 131104 | tf_op jit(solution)/shard_map/ppermute | solution.py:637
  19.6 1.4 %collective-permute-done.2.far_ref = bf16[2,2,128,128]{3,2,1,0:T(8,128)(2,1)S(1)} collective-permute-done((bf16[2,2,128,128]{3,2,1,0:T(8,128)(2,1)S(1)}, bf16[2,2,128,128]{3,2,1,0:T(8,128)(2,1)S(1)}, u32[]{:S(2)}, u32[]{:S(2)}) %collective-permute-start.2) | collective-permute-done | bytes 131104 | tf_op jit(solution)/shard_map/ppermute | solution.py:637
  21.0 0.7 %scan_chips.1 = (bf16[2,2,128,128]{3,2,1,0:T(8,128)(2,1)S(1)}, bf16[2,2,128,128]{3,2,1,0:T(8,128)(2,1)S(1)}) custom-call(bf16[2,3,128,128]{3,2,1,0:T(8,128)(2,1)S(1)} %get-tuple-element.35.keep_ref, bf16[2,3,128,128]{3,2,1,0:T(8,128)(2,1)S(1)} %collective-permute-done.recv_ref, bf16[2,2,128,128]{3,2,1,0:T(8,128)(2,1)S(1)} %collective-permute-done.1.near_ref, ...), custom_call_target="tpu_custom_call" | custom-call | tf_op jit(solution)/shard_map/scan_chips/pallas_call | solution.py:464
  21.7 0.1 collective-permute-start.4
  21.8 0.8 %weigh.1 = (f32[4,256,256]{2,1,0:T(8,128)S(1)}, f32[4,256,256]{2,1,0:T(8,128)S(1)}, f32[4,256,256]{2,1,0:T(8,128)S(1)}, f32[4,256,256]{2,1,0:T(8,128)S(1)}, f32[...) custom-call(f32[8,256]{1,0:T(8,128)S(1)} %get-tuple-element.48.lane_ref, ...), custom_call_target="tpu_custom_call" | custom-call | tf_op jit(solution)/shard_map/weigh/pallas_call | solution.py:357
  22.5 1.1 %own_grads.1.refs_14_.refs_0_ = bf16[3,256,256]{2,1,0:T(8,128)(2,1)S(1)} custom-call(bf16[2,2,128,128]{3,2,1,0:T(8,128)(2,1)S(1)} %get-tuple-element.39.edge_ref, f32[2,256,512]{2,1,0:T(8,128)S(1)} %get-tuple-element.40.scale_ref, f32[2,256,512]{2,1,0:T(8,128)S(1)} %get-tuple-element.41.refs_0_, f32[4,256,128]{2,1,0:T(8,128)S(1)} %get-tuple-element.42.refs_1_, ...), custom_call_target="tpu_custom_call" | custom-call | tf_op jit(solution)/shard_map/own_grads/pallas_call | solution.py:568
  23.6 0.0 collective-permute-done.4.edge_ref
  23.6 1.6 %grads.1 = (bf16[3,256,256]{2,1,0:T(8,128)(2,1)S(1)}, bf16[256,512]{1,0:T(8,128)(2,1)S(1)}) custom-call(bf16[3,2048,512]{2,1,0:T(8,128)(2,1)S(1)} %get-tuple-element.34.w_ref, bf16[2,2,128,128]{3,2,1,0:T(8,128)(2,1)S(1)} %collective-permute-done.4.edge_ref, f32[2,256,512]{2,1,0:T(8,128)S(1)} %get-tuple-element.40.scale_ref, ...), custom_call_target="tpu_custom_call" | custom-call | tf_op jit(solution)/shard_map/grads/pallas_call | solution.py:598
  25.3 1.6 %collective-permute-start.7 = (bf16[256,512]{1,0:T(8,128)(2,1)S(1)}, bf16[256,512]{1,0:T(8,128)(2,1)S(1)}, u32[]{:S(2)}, u32[]{:S(2)}) collective-permute-start(bf16[256,512]{1,0:T(8,128)(2,1)S(1)} %get-tuple-element.60), channel_id=1, source_target_pairs={{0,1},{1,0},{2,3},{3,2},{4,5},{5,4},{6,7},{7,6},{8,9},{9,8},{10,11... | collective-permute-start | bytes 786440 | tf_op jit(solution)/shard_map/ppermute | solution.py:715
  26.9 0.7 %collective-permute-start.5 = (bf16[256,512]{1,0:T(8,128)(2,1)S(1)}, bf16[256,512]{1,0:T(8,128)(2,1)S(1)}, u32[]{:S(2)}, u32[]{:S(2)}) collective-permute-start(bf16[256,512]{1,0:T(8,128)(2,1)S(1)} %get-tuple-element.60), channel_id=1, source_target_pairs={{1,2},{2,1},{5,6},{6,5},{9,10},{10,9},{13,14},{14,13},{17,18},{18,... | collective-permute-start | bytes 786440 | tf_op jit(solution)/shard_map/ppermute | solution.py:716
  27.6 1.4 %others.1 = (bf16[256,512]{1,0:T(8,128)(2,1)S(1)}, f32[256,512]{1,0:T(8,128)S(1)}, f32[256,512]{1,0:T(8,128)S(1)}) custom-call(bf16[3,2048,512]{2,1,0:T(8,128)(2,1)S(1)} %get-tuple-element.34.w_ref, bf16[3,256,256]{2,1,0:T(8,128)(2,1)S(1)} %own_grads.1.refs_14_.refs_0_, bf16[3,256,256]{2,1,0:T(8,128)(2,1)S(1)} %get-tuple-element.58.refs_1_), custom_call_target="tpu_custom_call" | custom-call | tf_op jit(solution)/shard_map/others/pallas_call | solution.py:626
  29.0 3.9 %collective-permute-start.6 = (bf16[256,512]{1,0:T(8,128)(2,1)S(1)}, bf16[256,512]{1,0:T(8,128)(2,1)S(1)}, u32[]{:S(2)}, u32[]{:S(2)}) collective-permute-start(bf16[256,512]{1,0:T(8,128)(2,1)S(1)} %get-tuple-element.61), channel_id=1, source_target_pairs={{0,2},{2,3},{3,1},{1,0},{4,6},{6,7},{7,5},{5,4},{8,10},{10,11},{11... | collective-permute-start | bytes 786440 | tf_op jit(solution)/shard_map/ppermute | solution.py:719
  32.9 1.2 %collective-permute-done.7.outer_ref = bf16[256,512]{1,0:T(8,128)(2,1)S(1)} collective-permute-done((bf16[256,512]{1,0:T(8,128)(2,1)S(1)}, bf16[256,512]{1,0:T(8,128)(2,1)S(1)}, u32[]{:S(2)}, u32[]{:S(2)}) %collective-permute-start.7) | collective-permute-done | bytes 262176 | tf_op jit(solution)/shard_map/ppermute | solution.py:715
  34.1 1.7 %collective-permute-start.8 = (bf16[256,512]{1,0:T(8,128)(2,1)S(1)}, bf16[256,512]{1,0:T(8,128)(2,1)S(1)}, u32[]{:S(2)}, u32[]{:S(2)}) collective-permute-start(bf16[256,512]{1,0:T(8,128)(2,1)S(1)} %join_outer.1), channel_id=1, source_target_pairs={{0,1},{1,3},{3,2},{2,0},{4,5},{5,7},{7,6},{6,4},{8,9},{9,11},{11,1... | collective-permute-start | bytes 786440 | tf_op jit(solution)/shard_map/ppermute | solution.py:718
  35.8 4.1 %collective-permute-done.6 = bf16[256,512]{1,0:T(8,128)(2,1)S(1)} collective-permute-done((bf16[256,512]{1,0:T(8,128)(2,1)S(1)}, bf16[256,512]{1,0:T(8,128)(2,1)S(1)}, u32[]{:S(2)}, u32[]{:S(2)}) %collective-permute-start.6) | collective-permute-done | bytes 262176 | tf_op jit(solution)/shard_map/ppermute | solution.py:719
  39.9 0.0 collective-permute-done.5
  39.9 9.4 %collective-permute-done.8 = bf16[256,512]{1,0:T(8,128)(2,1)S(1)} collective-permute-done((bf16[256,512]{1,0:T(8,128)(2,1)S(1)}, bf16[256,512]{1,0:T(8,128)(2,1)S(1)}, u32[]{:S(2)}, u32[]{:S(2)}) %collective-permute-start.8) | collective-permute-done | bytes 262176 | tf_op jit(solution)/shard_map/ppermute | solution.py:718
  49.3 0.8 %add_convert_fusion = bf16[256,512]{1,0:T(8,128)(2,1)} fusion(bf16[256,512]{1,0:T(8,128)(2,1)S(1)} %collective-permute-done.8, bf16[256,512]{1,0:T(8,128)(2,1)S(1)} %collective-permute-done.6, f32[256,512]{1,0:T(8,128)S(1)} %get-tuple-element.59, bf16[256,512]{1,0:T(8,128)(2,1)S(1)} %collective-permute-done.5), kind=kLoop, calls=%fused_computation | loop fusion | flops 917504 | bytes 1572864 | tf_op jit(solution)/shard_map/convert_element_type | solution.py:721
  (1 shorter events, 0.0 us)
Async XLA Ops:
  7.0 1.6 %collective-permute-start = (bf16[2,3,128,128]{3,2,1,0:T(8,128)(2,1)S(1)}, bf16[2,3,128,128]{3,2,1,0:T(8,128)(2,1)S(1)}, u32[]{:S(2)}, u32[]{:S(2)}) collective-permute-start(bf16[2,3,128,128]{3,2,1,0:T(8,128)(2,1)S(1)} %get-tuple-element.36), channel_id=1, source_target_pairs={{0,4},{4,0},{8,12},{12,8},{16,20},{20,16},{24,28},{28,24},{1,5},{5... | collective-permute-start | bytes 589832 | tf_op jit(solution)/shard_map/ppermute | solution.py:637
  8.8 7.1 %collective-permute-start.1 = (bf16[2,2,128,128]{3,2,1,0:T(8,128)(2,1)S(1)}, bf16[2,2,128,128]{3,2,1,0:T(8,128)(2,1)S(1)}, u32[]{:S(2)}, u32[]{:S(2)}) collective-permute-start(bf16[2,2,128,128]{3,2,1,0:T(8,128)(2,1)S(1)} %get-tuple-element.37), channel_id=1, source_target_pairs={{0,8},{4,12},{8,0},{12,4},{16,24},{20,28},{24,16},{28,20},{1,9},{5... | collective-permute-start | bytes 393224 | tf_op jit(solution)/shard_map/ppermute | solution.py:637
  11.7 7.9 %collective-permute-start.3 = (bf16[2,2,128,128]{3,2,1,0:T(8,128)(2,1)S(1)}, bf16[2,2,128,128]{3,2,1,0:T(8,128)(2,1)S(1)}, u32[]{:S(2)}, u32[]{:S(2)}) collective-permute-start(bf16[2,2,128,128]{3,2,1,0:T(8,128)(2,1)S(1)} %get-tuple-element.38), channel_id=1, source_target_pairs={{0,24},{4,28},{8,16},{12,20},{16,8},{20,12},{24,0},{28,4},{1,25},{... | collective-permute-start | bytes 393224 | tf_op jit(solution)/shard_map/ppermute | solution.py:637
  13.2 7.8 %collective-permute-start.2 = (bf16[2,2,128,128]{3,2,1,0:T(8,128)(2,1)S(1)}, bf16[2,2,128,128]{3,2,1,0:T(8,128)(2,1)S(1)}, u32[]{:S(2)}, u32[]{:S(2)}) collective-permute-start(bf16[2,2,128,128]{3,2,1,0:T(8,128)(2,1)S(1)} %get-tuple-element.38), channel_id=1, source_target_pairs={{0,16},{4,20},{8,24},{12,28},{16,0},{20,4},{24,8},{28,12},{1,17},{... | collective-permute-start | bytes 393224 | tf_op jit(solution)/shard_map/ppermute | solution.py:637
  21.7 2.0 %collective-permute-start.4 = (bf16[2,2,128,128]{3,2,1,0:T(8,128)(2,1)S(1)}, bf16[2,2,128,128]{3,2,1,0:T(8,128)(2,1)S(1)}, u32[]{:S(2)}, u32[]{:S(2)}) collective-permute-start(bf16[2,2,128,128]{3,2,1,0:T(8,128)(2,1)S(1)} %get-tuple-element.57), channel_id=1, source_target_pairs={{0,4},{4,0},{8,12},{12,8},{16,20},{20,16},{24,28},{28,24},{1,5},{5... | collective-permute-start | bytes 393224 | tf_op jit(solution)/shard_map/ppermute | solution.py:637
  25.3 8.8 %collective-permute-start.7 = (bf16[256,512]{1,0:T(8,128)(2,1)S(1)}, bf16[256,512]{1,0:T(8,128)(2,1)S(1)}, u32[]{:S(2)}, u32[]{:S(2)}) collective-permute-start(bf16[256,512]{1,0:T(8,128)(2,1)S(1)} %get-tuple-element.60), channel_id=1, source_target_pairs={{0,1},{1,0},{2,3},{3,2},{4,5},{5,4},{6,7},{7,6},{8,9},{9,8},{10,11... | collective-permute-start | bytes 786440 | tf_op jit(solution)/shard_map/ppermute | solution.py:715
  26.9 13.0 %collective-permute-start.5 = (bf16[256,512]{1,0:T(8,128)(2,1)S(1)}, bf16[256,512]{1,0:T(8,128)(2,1)S(1)}, u32[]{:S(2)}, u32[]{:S(2)}) collective-permute-start(bf16[256,512]{1,0:T(8,128)(2,1)S(1)} %get-tuple-element.60), channel_id=1, source_target_pairs={{1,2},{2,1},{5,6},{6,5},{9,10},{10,9},{13,14},{14,13},{17,18},{18,... | collective-permute-start | bytes 786440 | tf_op jit(solution)/shard_map/ppermute | solution.py:716
  29.0 10.9 %collective-permute-start.6 = (bf16[256,512]{1,0:T(8,128)(2,1)S(1)}, bf16[256,512]{1,0:T(8,128)(2,1)S(1)}, u32[]{:S(2)}, u32[]{:S(2)}) collective-permute-start(bf16[256,512]{1,0:T(8,128)(2,1)S(1)} %get-tuple-element.61), channel_id=1, source_target_pairs={{0,2},{2,3},{3,1},{1,0},{4,6},{6,7},{7,5},{5,4},{8,10},{10,11},{11... | collective-permute-start | bytes 786440 | tf_op jit(solution)/shard_map/ppermute | solution.py:719
  34.1 15.2 %collective-permute-start.8 = (bf16[256,512]{1,0:T(8,128)(2,1)S(1)}, bf16[256,512]{1,0:T(8,128)(2,1)S(1)}, u32[]{:S(2)}, u32[]{:S(2)}) collective-permute-start(bf16[256,512]{1,0:T(8,128)(2,1)S(1)} %join_outer.1), channel_id=1, source_target_pairs={{0,1},{1,3},{3,2},{2,0},{4,5},{5,7},{7,6},{6,4},{8,9},{9,11},{11,1... | collective-permute-start | bytes 786440 | tf_op jit(solution)/shard_map/ppermute | solution.py:718

commit v8 on v7

--- a/solution.py
+++ b/solution.py
@@ -133,11 +133,11 @@
 
 
 def prepare_kernel(
-    half, pieces, tok_hbm, w_hbm, logit_hbm, decay_hbm, og_hbm,
-    w_ref, og_ref, unit_ref, scale_ref, lane_ref, col_ref, u_ref, wk_ref, dbt_ref, ktt_ref, gt_ref,
-    keep_ref, send_ref,
-    tok_scr, logit_ref, decay_ref, value_scr, pay_scr, gamma_scr, pair_scr, tok_sem, w_sem, more_sem,
+    part, many, pieces, tok_hbm, w_hbm, logit_hbm, decay_hbm, og_hbm,
+    w_ref, og_ref, unit_ref, scale_ref, lane_ref, col_ref, gt_ref, value_scr, gamma_scr, inv_ref, open_ref, beta_ref,
+    *more,
 ):
+    out_refs, (tok_scr, logit_ref, decay_ref, pair_scr, tok_sem, w_sem, more_sem) = more[:5], more[5:]
     heads, size = decay_ref.shape
     members, depth, columns = w_ref.shape
     width = columns // heads
@@ -230,45 +230,57 @@
         fill()
     value_scr[...] = totals[2]
     normalize(0, totals[0])
+    for h in every:
+        inv_ref[h] = inverse[h]
+        open_ref[h] = jnp.broadcast_to(jnp.exp(run_col[h]), (size, width))
+        beta_ref[h] = jnp.broadcast_to(beta[h], (size, width))
+    solve_heads(base_of(part, many), (unit_ref, value_scr, lane_ref, gamma_scr, inv_ref, open_ref, beta_ref, gt_ref), out_refs)
+
+
+def solve_heads(base, refs, out_refs):
+    unit_ref, value_ref, lane_ref, gamma_ref, inv_ref, open_ref, beta_ref, gt_ref = refs
+    u_ref, wk_ref, dbt_ref, fade_ref, pay_ref = out_refs
+    many, size, width = u_ref.shape
+    every = range(many)
+    heads = [base + i for i in every]
+    spans = [lanes_from(h, width) for h in heads]
+    keys = [unit_ref[1, :, s] for s in spans]
     queries = [unit_ref[0, :, s] for s in spans]
-    scores = [(gamma_scr[h] * nt(queries[h].astype(BF16), key_b[h])).astype(BF16) for h in every]
-    last = [run_col[h][size - 1 : size, :] for h in every]
-    open_col = [jnp.exp(run_col[h]) for h in every]
-    fade_row = [jnp.exp(last[h] - run_row[h]) for h in every]
-    write_key = [beta[h] * open_col[h] * keys[h] for h in every]
+    inverse = [inv_ref[h] for h in heads]
+    scores = [
+        (gamma_ref[h] * nt(q.astype(BF16), k.astype(BF16))).astype(BF16)
+        for h, q, k in zip(heads, queries, keys)
+    ]
+    run_row = [lane_ref[pl.ds(h, 1), :] for h in heads]
+    last = [r[:, size - 1 :] for r in run_row]
+    fade_row = [jnp.exp(a - r) for a, r in zip(last, run_row)]
+    write_key = [beta_ref[h] * open_ref[h] * k for h, k in zip(heads, keys)]
     right = [
-        jnp.concatenate([beta[h] * value_scr[:, spans[h]], write_key[h]], axis=1) for h in every
+        jnp.concatenate([beta_ref[h] * value_ref[:, s], w], axis=1)
+        for h, s, w in zip(heads, spans, write_key)
     ]
-    solved = [right[h] + nn(inverse[h], right[h].astype(BF16)) for h in every]
-    fade_t = [keys[h].T * fade_row[h] for h in every]
-    left = [jnp.concatenate([nn(gt_ref[h], scores[h]), fade_t[h]], axis=0) for h in every]
-    back = [left[h] + nn(left[h].astype(BF16), inverse[h]) for h in every]
+    solved = [r + nn(n, r.astype(BF16)) for r, n in zip(right, inverse)]
+    fade_t = [k.T * f for k, f in zip(keys, fade_row)]
+    left = [nn(gt_ref[h], p) for h, p in zip(heads, scores)]
+    back = [x + nn(x.astype(BF16), n) for x, n in zip(left, inverse)]
     e_rows, e_cols = grid_ids(width)
-    for h in every:
-        fade_hi = fade_t[h].astype(BF16)
-        fade_lo = (fade_t[h] - fade_hi.astype(F32)).astype(BF16)
-        solved_hi = solved[h].astype(BF16)
-        solved_lo = (solved[h][:, :width] - solved_hi[:, :width].astype(F32)).astype(BF16)
+    for i, h in enumerate(heads):
+        fade_hi, fade_lo = two_terms(fade_t[i])
+        solved_hi = solved[i].astype(BF16)
+        solved_lo = (solved[i][:, :width] - solved_hi[:, :width].astype(F32)).astype(BF16)
         state = nn(fade_hi, solved_hi)
         fill = state[:, :width] + nn(fade_lo, solved_hi[:, :width]) + nn(fade_hi, solved_lo)
-        unit = jnp.where(e_rows == e_cols, jnp.exp(last[h]), 0.0)
-        seed = nn(gt_ref[h], (open_col[h] * queries[h]).astype(BF16)) - nn(
-            back[h][:width].astype(BF16), write_key[h].astype(BF16)
+        unit = jnp.where(e_rows == e_cols, jnp.exp(last[i]), 0.0)
+        seed = nn(gt_ref[h], (open_ref[h] * queries[i]).astype(BF16)) - nn(
+            back[i].astype(BF16), write_key[i].astype(BF16)
         )
-        pay_scr[h, 0] = (unit - state[:, width:]).astype(BF16)
-        pay_scr[h, 1] = fill.astype(BF16)
-        pay_scr[h, 2] = seed.astype(BF16)
-        u_ref[h] = solved[h][:, :width]
-        wk_ref[h] = solved_hi[:, width:]
-        dbt_ref[h] = back[h][:width]
-        ktt_ref[h] = back[h][width:].astype(BF16)
-    if half:
-        core = lax.rem(lax.axis_index("seq"), 2)
-        keep_ref[...] = pay_scr[pl.ds(core * half, half)]
-        send_ref[...] = pay_scr[pl.ds((1 - core) * half, half)]
-    else:
-        keep_ref[...] = pay_scr[...]
-        send_ref[...] = pay_scr[...]
+        pay_ref[i, 0] = (unit - state[:, width:]).astype(BF16)
+        pay_ref[i, 1] = fill.astype(BF16)
+        pay_ref[i, 2] = seed.astype(BF16)
+        u_ref[i] = solved[i][:, :width]
+        wk_ref[i] = solved_hi[:, width:]
+        dbt_ref[i] = back[i]
+        fade_ref[i] = fade_t[i]
 
 
 def here():
@@ -281,13 +293,22 @@
 
 def limit(mebibytes):
     return pltpu.CompilerParams(vmem_limit_bytes=mebibytes * 2**20)
+
+
+def solved_shapes(many, size, width):
+    return [
+        jax.ShapeDtypeStruct((many, size, width), F32),
+        jax.ShapeDtypeStruct((many, size, width), BF16),
+        jax.ShapeDtypeStruct((many, width, size), F32),
+        jax.ShapeDtypeStruct((many, width, size), F32),
+        jax.ShapeDtypeStruct((many, 3, width, width), BF16),
+    ]
 
 
 def prepare(tokens, weights, logit, decay, out_grad, half):
     heads, size = logit.shape
     members, depth, columns = weights.shape
     width = columns // heads
-    part = half or heads
     pieces = 4 if depth % 512 == 0 else 1
     gate_rows = 2 * heads + -2 * heads % 8
     shapes = [
@@ -297,26 +318,25 @@
         ((2, size, columns), F32),
         ((gate_rows, size), F32),
         ((size, gate_rows), F32),
+        ((heads, width, size), BF16),
+        ((size, columns), F32),
+        ((heads, size, size), F32),
+        ((heads, size, size), BF16),
         ((heads, size, width), F32),
-        ((heads, size, width), BF16),
-        ((heads, width, size), F32),
-        ((heads, width, size), BF16),
-        ((heads, width, size), BF16),
-        ((part, 3, width, width), BF16),
-        ((part, 3, width, width), BF16),
+        ((heads, size, width), F32),
     ]
+    shapes = [jax.ShapeDtypeStruct(*s) for s in shapes]
+    shapes += solved_shapes(half or heads, size, width)
+    args = (tokens, weights, logit, decay, out_grad)
     return pl.pallas_call(
-        functools.partial(prepare_kernel, half, pieces),
+        functools.partial(prepare_kernel, 1 if half else None, half or heads, pieces),
         in_specs=[away()] * 5,
         out_specs=[here()] * len(shapes),
-        out_shape=[jax.ShapeDtypeStruct(*s) for s in shapes],
+        out_shape=shapes,
         scratch_shapes=[
             pltpu.VMEM((size, depth), BF16),
             pltpu.VMEM((heads, size), F32),
             pltpu.VMEM((heads, size), F32),
-            pltpu.VMEM((size, columns), F32),
-            pltpu.VMEM((heads, 3, width, width), BF16),
-            pltpu.VMEM((heads, size, size), F32),
             pltpu.VMEM((heads, size, size), F32),
             pltpu.SemaphoreType.DMA((pieces,)),
             pltpu.SemaphoreType.DMA((members, pieces)),
@@ -324,44 +344,64 @@
         ],
         compiler_params=limit(16),
         name="prepare",
-    )(*(pltpu.with_memory_space_constraint(x, pltpu.HBM) for x in (tokens, weights, logit, decay, out_grad)))
-
-
-def weigh_kernel(
-    heads, lane_ref, col_ref,
-    gamma_ref, turned_ref, strong_ref, strong_t_ref, open_ref, fade_ref, beta_ref,
-):
+    )(*(pltpu.with_memory_space_constraint(x, pltpu.HBM) for x in args))
+
+
+def solve_own_kernel(*refs):
+    solve_heads(base_of(0, refs[8].shape[0]), refs[:8], refs[8:])
+
+
+def solve_own(half, unit, value, lanes, gamma, inverse, opened, beta, gt):
+    _, width, size = gt.shape
+    shapes = solved_shapes(half, size, width)
+    return pl.pallas_call(
+        solve_own_kernel,
+        in_specs=[here()] * 8,
+        out_specs=[here()] * len(shapes),
+        out_shape=shapes,
+        compiler_params=limit(12),
+        name="solve_own",
+    )(unit, value, lanes, gamma, inverse, opened, beta, gt)
+
+
+def weigh_kernel(heads, parts, lane_ref, col_ref, gamma_ref, inv_ref, *refs):
+    fades, ktts = refs[: len(parts)], refs[len(parts) : 2 * len(parts)]
+    turned_ref, strong_ref, strong_t_ref, fade_ref = refs[2 * len(parts) :]
     size = lane_ref.shape[1]
-    width = open_ref.shape[2]
+    width = fade_ref.shape[2]
+    for part, fade_t_ref, ktt_ref in zip(parts, fades, ktts):
+        many = fade_t_ref.shape[0]
+        base = base_of(part, many)
+        for i in range(many):
+            fade_t = fade_t_ref[i]
+            ktt_ref[i] = (fade_t + nn(fade_t.astype(BF16), inv_ref[base + i])).astype(BF16)
     rows, cols = grid_ids(size)
     for h in range(heads):
         run = col_ref[:, h : h + 1]
         gap = run - lane_ref[h : h + 1, :]
-        gamma = jnp.exp(jnp.where(rows >= cols, gap, FAR))
         turned = jnp.exp(jnp.where(rows <= cols, -gap, FAR))
-        gamma_ref[h] = gamma
         turned_ref[h] = turned
         beta = col_ref[:, heads + h : heads + h + 1]
         beta_row = lane_ref[heads + h : heads + h + 1, :]
-        strong_ref[h] = jnp.where(rows > cols, beta * gamma, 0.0)
+        strong_ref[h] = jnp.where(rows > cols, beta * gamma_ref[h], 0.0)
         strong_t_ref[h] = jnp.where(rows < cols, beta_row * turned, 0.0)
-        open_ref[h] = jnp.broadcast_to(jnp.exp(run), (size, width))
         fade_ref[h] = jnp.broadcast_to(jnp.exp(run[size - 1 :, :] - run), (size, width))
-        beta_ref[h] = jnp.broadcast_to(beta, (size, width))
-
-
-def weigh(lanes, cols, heads, width):
-    size = lanes.shape[1]
-    shapes = [jax.ShapeDtypeStruct((heads, size, size), F32)] * 4
-    shapes += [jax.ShapeDtypeStruct((heads, size, width), F32)] * 3
+
+
+def weigh(lanes, cols, gamma, inverse, fades):
+    heads, size, _ = gamma.shape
+    width = fades[0].shape[1]
+    shapes = [jax.ShapeDtypeStruct(f.shape, BF16) for f in fades]
+    shapes += [jax.ShapeDtypeStruct((heads, size, size), F32)] * 3
+    shapes += [jax.ShapeDtypeStruct((heads, size, width), F32)]
     return pl.pallas_call(
-        functools.partial(weigh_kernel, heads),
-        in_specs=[here()] * 2,
+        functools.partial(weigh_kernel, heads, (None,) if len(fades) == 1 else (0, 1)),
+        in_specs=[here()] * (4 + len(fades)),
         out_specs=[here()] * len(shapes),
         out_shape=shapes,
         compiler_params=limit(8),
         name="weigh",
-    )(lanes, cols)
+    )(lanes, cols, gamma, inverse, *fades)
 
 
 def pair_kernel(levels, keep_ref, recv_ref, *pay_refs):
@@ -500,11 +540,11 @@
 
 def contract(base, refs, edge_ref, grad_ref):
     (unit_ref, u_ref, wk_ref, dbt_ref, ktt_ref, gt_ref, og_ref) = refs[:7]
-    (gamma_ref, turned_ref, strong_ref, strong_t_ref, open_ref, fade_ref, beta_ref) = refs[7:]
+    (gamma_ref, open_ref, beta_ref, turned_ref, strong_ref, strong_t_ref, fade_ref) = refs[7:]
     _, size, width = u_ref.shape
     every = range(edge_ref.shape[0])
-    update = [(u_ref[base + i] - nn(wk_ref[base + i], edge_ref[i, 0])).astype(BF16) for i in every]
-    delta_t = [dbt_ref[base + i] + nn(edge_ref[i, 1], ktt_ref[base + i]) for i in every]
+    update = [(u_ref[i] - nn(wk_ref[i], edge_ref[i, 0])).astype(BF16) for i in every]
+    delta_t = [dbt_ref[i] + nn(edge_ref[i, 1], ktt_ref[i]) for i in every]
     delta = [d.T for d in delta_t]
     slopes = []
     for i in every:
@@ -555,38 +595,44 @@
     return total
 
 
-def own_kernel(edge_ref, scale_ref, *refs):
-    refs, grad_ref = refs[:-1], refs[-1]
-    base = base_of(0, edge_ref.shape[0])
+def own_kernel(count, w_ref, edge_ref, scale_ref, *refs):
+    refs, (grad_ref, out_ref) = refs[:-2], refs[-2:]
+    many, _, width, _ = edge_ref.shape
+    base = base_of(0, many)
     slopes = contract(base, refs, edge_ref, grad_ref)
     project_out(base, slopes, refs[0], scale_ref, grad_ref)
-
-
-def own_grads(edge, scale, prepared):
+    out_ref[...] = spread_grads([(base, width, grad_ref)], w_ref, 0, count)
+
+
+def own_grads(weights, edge, scale, prepared):
     many, _, width, _ = edge.shape
     size = scale.shape[1]
+    count = lax.axis_size("head")
     return pl.pallas_call(
-        own_kernel,
-        in_specs=[here()] * (2 + len(prepared)),
-        out_specs=here(),
-        out_shape=jax.ShapeDtypeStruct((3, size, many * width), BF16),
+        functools.partial(own_kernel, count),
+        in_specs=[here()] * (3 + len(prepared)),
+        out_specs=[here()] * 2,
+        out_shape=[
+            jax.ShapeDtypeStruct((3, size, many * width), BF16),
+            jax.ShapeDtypeStruct((size, weights.shape[1] // count), F32),
+        ],
         compiler_params=limit(12),
         name="own_grads",
-    )(edge, scale, *prepared)
+    )(weights, edge, scale, *prepared)
 
 
 def grads_kernel(part, count, w_ref, edge_ref, scale_ref, *refs):
     refs, (grad_ref, out_ref) = refs[:-2], refs[-2:]
-    done = []
     many, _, width, _ = edge_ref.shape
     base = base_of(part, many)
     if part is not None:
-        refs, done = refs[:-1], [(base_of(0, many), width, refs[-1])]
+        refs, done_ref = refs[:-1], refs[-1]
     slopes = contract(base, refs, edge_ref, grad_ref)
-    total = spread_grads(done, w_ref, 0, count)
     project_out(base, slopes, refs[0], scale_ref, grad_ref)
-    last = spread_grads([(base, width, grad_ref)], w_ref, 0, count)
-    out_ref[...] = (last if total is None else total + last).astype(out_ref.dtype)
+    total = spread_grads([(base, width, grad_ref)], w_ref, 0, count)
+    if part is not None:
+        total = total + done_ref[...]
+    out_ref[...] = total.astype(out_ref.dtype)
 
 
 def grads(weights, edge, scale, prepared, own):
@@ -637,14 +683,17 @@
     return lax.ppermute(value, axis, [(i, i ^ mask) for i in range(count)])
 
 
-def edges_by_pairs(keep, send, count):
-    recv = swap(send, "seq", count, 1)
+def swap_pay(pay, count):
+    return swap(pay, "seq", count, 1)
+
+
+def edges_by_pairs(keep, recv, count):
     low, high = join_pair(keep, recv, 2)
     far = swap(high, "seq", count, 4)
     cross = swap(high, "seq", count, 6)
     near = swap(low, "seq", count, 2)
     own, other = scan_chips(keep, recv, near, far, cross)
-    return own, swap(other, "seq", count, 1)
+    return own, other
 
 
 def edges_by_gather(keep, count):
@@ -726,21 +775,32 @@
     count = lax.axis_size("seq")
     paired = heads % 2 == 0 and count == 8
     half = heads // 2 if paired else 0
-    held, kept_grad, unit, scale, lanes, col, u, wk, dbt, ktt, gt, keep, send = prepare(
+    held, kept_grad, unit, scale, lanes, col, gt, value, gamma, inverse, opened, beta, *first = prepare(
         tokens, qkv_weight, beta_logit, log_decay, out_grad, half
     )
+    solved = [first]
     if paired:
-        own, recv = edges_by_pairs(keep, send, count)
+        recv = swap_pay(first[4], count)
+        mine = solve_own(half, unit, value, lanes, gamma, inverse, opened, beta, gt)
+        solved = [mine, first]
+        own, other = edges_by_pairs(mine[4], recv, count)
     else:
-        own, recv = edges_by_gather(keep, count)
+        own, _ = edges_by_gather(first[4], count)
+    weighed = weigh(lanes, col, gamma, inverse, [x[3] for x in solved])
+    ktts, weighed = weighed[: len(solved)], weighed[len(solved) :]
+
+    def group(i):
+        u, wk, dbt = solved[i][:3]
+        return (unit, u, wk, dbt, ktts[i], gt, kept_grad, gamma, opened, beta, *weighed)
+
     width = qkv_weight.shape[2] // heads
-    prepared = (unit, u, wk, dbt, ktt, gt, kept_grad, *weigh(lanes, col, heads, width))
     if paired:
-        own_part = own_grads(own, scale, prepared)
-        grad, end = grads(held, recv, scale, prepared, own_part)
+        recv = swap(other, "seq", count, 1)
+        own_part, own_end = own_grads(held, own, scale, group(0))
+        grad, end = grads(held, recv, scale, group(1), own_end)
         groups = [own_part, grad]
     else:
-        grad, end = grads(held, own, scale, prepared, None)
+        grad, end = grads(held, own, scale, group(0), None)
         groups = [grad]
     rest = others(held, groups, width)
     if lax.axis_size("head") == 4:

time: 50.4 us -> 50.2 us (level)
  waiting for transfers between devices: 23.5 us -> 22.7 us
  Pallas kernels: 12.8 us -> 13.4 us
    ppermute x5, waiting for transfers between devices: 8.79 us -> 8.01 us  [swap(): return lax.ppermute(value, axis, [(i, i ^ mask) for i in range(count)])]
    pallas_call x3 -> x4, Pallas kernels: 8.82 us -> 9.57 us  [the longest x1 6.66 us: prepare(): pl.pallas_call(functools.partial(prepare_kernel, 1 if half else None, hal...]
  transfers between devices with their start and end apart: 9 -> 9, of which waited for: 7 -> 7; matrix products, arithmetic and copies ran while one was open for 0% -> 0% of each run, Pallas kernels for 7% -> 9%
where the time goes in v8:
time: 50.2 us; the launch traced here: 50 us
  waiting for transfers between devices  22.7 us (45%)
  Pallas kernels  13.4 us (27%)
  starting transfers between devices  12.9 us (26%)
  other arithmetic  0.84 us (2%)
    ppermute x1, waiting for transfers between devices, sum_of_four(): joint = lax.ppermute(joint, 'head', [(0, 1), (1, 3), (3, 2), (2, 0)])  9.44 us
    ppermute x5, waiting for transfers between devices, swap(): return lax.ppermute(value, axis, [(i, i ^ mask) for i in range(count)])  8.01 us
    pallas_call x1, Pallas kernels, prepare(): pl.pallas_call(functools.partial(prepare_kernel, 1 if half else None, hal...  6.66 us
    ppermute x5, starting transfers between devices, swap(): return lax.ppermute(value, axis, [(i, i ^ mask) for i in range(count)])  5.07 us
    ppermute x1, waiting for transfers between devices, sum_of_four(): ring = lax.ppermute(first, 'head', [(0, 2), (2, 3), (3, 1), (1, 0)])  4.14 us
    ppermute x1, starting transfers between devices, sum_of_four(): ring = lax.ppermute(first, 'head', [(0, 2), (2, 3), (3, 1), (1, 0)])  3.89 us
    ppermute x1, starting transfers between devices, sum_of_four(): joint = lax.ppermute(joint, 'head', [(0, 1), (1, 3), (3, 2), (2, 0)])  1.65 us
    ppermute x1, starting transfers between devices, sum_of_four(): outer = lax.ppermute(end, 'head', [(0, 1), (1, 0), (2, 3), (3, 2)])  1.64 us
  transfers between devices with their start and end apart: 9, of which 7 were waited for; matrix products, arithmetic and copies ran while one was open for 0% of the time, Pallas kernels for 9%

profile of v8, /device:TPU:0, one launch (start us, length us, event | category | flops | bytes accessed | tf_op | source)
XLA Modules:
  0.0 50.0 jit_solution(10502526002659461370)
XLA Ops:
  0.0 6.7 %prepare.1 = (bf16[3,2048,512]{2,1,0:T(8,128)(2,1)S(1)}, bf16[256,512]{1,0:T(8,128)(2,1)S(1)}, f32[2,256,512]{2,1,0:T(8,128)S(1)}, f32[2,256,512]{2,1,0:T(8,128)...) custom-call(bf16[256,2048]{1,0:T(8,128)(2,1)} %tok_hbm.1, ...), custom_call_target="tpu_custom_call" | custom-call | tf_op jit(solution)/shard_map/prepare/pallas_call | solution.py:331
  6.7 0.5 %collective-permute-start = (bf16[2,3,128,128]{3,2,1,0:T(8,128)(2,1)S(1)}, bf16[2,3,128,128]{3,2,1,0:T(8,128)(2,1)S(1)}, u32[]{:S(2)}, u32[]{:S(2)}) collective-permute-start(bf16[2,3,128,128]{3,2,1,0:T(8,128)(2,1)S(1)} %get-tuple-element.54), channel_id=1, source_target_pairs={{0,4},{4,0},{8,12},{12,8},{16,20},{20,16},{24,28},{28,24},{1,5},{5... | collective-permute-start | bytes 589832 | tf_op jit(solution)/shard_map/ppermute | solution.py:683
  7.2 0.8 %solve_own.1 = (f32[2,256,128]{2,1,0:T(8,128)S(1)}, bf16[2,256,128]{2,1,0:T(8,128)(2,1)S(1)}, f32[2,128,256]{2,1,0:T(8,128)S(1)}, f32[2,128,256]{2,1,0:T(8,128)S(1)}, bf16[2,3,128,128]{3,2,1,0:T(8,128)(2,1)S(1)}) custom-call(f32[2,256,512]{2,1,0:T(8,128)S(1)} %get-tuple-element.45.refs_0_, f32[256,512]{1,0:T(8,128)S(1)} %get-tuple-element.46.refs_1_, ...), custom_call_target="tpu_custom_call" | custom-call | tf_op jit(solution)/shard_map/solve_own/pallas_call | solution.py:357
  8.0 0.3 collective-permute-done.recv_ref
  8.3 0.2 join_pair.1
  8.5 2.9 %collective-permute-start.1 = (bf16[2,2,128,128]{3,2,1,0:T(8,128)(2,1)S(1)}, bf16[2,2,128,128]{3,2,1,0:T(8,128)(2,1)S(1)}, u32[]{:S(2)}, u32[]{:S(2)}) collective-permute-start(bf16[2,2,128,128]{3,2,1,0:T(8,128)(2,1)S(1)} %get-tuple-element.55), channel_id=1, source_target_pairs={{0,8},{4,12},{8,0},{12,4},{16,24},{20,28},{24,16},{28,20},{1,9},{5... | collective-permute-start | bytes 393224 | tf_op jit(solution)/shard_map/ppermute | solution.py:683
  11.4 1.5 %collective-permute-start.3 = (bf16[2,2,128,128]{3,2,1,0:T(8,128)(2,1)S(1)}, bf16[2,2,128,128]{3,2,1,0:T(8,128)(2,1)S(1)}, u32[]{:S(2)}, u32[]{:S(2)}) collective-permute-start(bf16[2,2,128,128]{3,2,1,0:T(8,128)(2,1)S(1)} %get-tuple-element.56), channel_id=1, source_target_pairs={{0,24},{4,28},{8,16},{12,20},{16,8},{20,12},{24,0},{28,4},{1,25},{... | collective-permute-start | bytes 393224 | tf_op jit(solution)/shard_map/ppermute | solution.py:683
  12.9 0.0 collective-permute-start.2
  12.9 2.6 %collective-permute-done.1.near_ref = bf16[2,2,128,128]{3,2,1,0:T(8,128)(2,1)S(1)} collective-permute-done((bf16[2,2,128,128]{3,2,1,0:T(8,128)(2,1)S(1)}, bf16[2,2,128,128]{3,2,1,0:T(8,128)(2,1)S(1)}, u32[]{:S(2)}, u32[]{:S(2)}) %collective-permute-start.1) | collective-permute-done | bytes 131104 | tf_op jit(solution)/shard_map/ppermute | solution.py:683
  15.6 3.7 %collective-permute-done.3.cross_ref = bf16[2,2,128,128]{3,2,1,0:T(8,128)(2,1)S(1)} collective-permute-done((bf16[2,2,128,128]{3,2,1,0:T(8,128)(2,1)S(1)}, bf16[2,2,128,128]{3,2,1,0:T(8,128)(2,1)S(1)}, u32[]{:S(2)}, u32[]{:S(2)}) %collective-permute-start.3) | collective-permute-done | bytes 131104 | tf_op jit(solution)/shard_map/ppermute | solution.py:683
  19.3 1.4 %collective-permute-done.2.far_ref = bf16[2,2,128,128]{3,2,1,0:T(8,128)(2,1)S(1)} collective-permute-done((bf16[2,2,128,128]{3,2,1,0:T(8,128)(2,1)S(1)}, bf16[2,2,128,128]{3,2,1,0:T(8,128)(2,1)S(1)}, u32[]{:S(2)}, u32[]{:S(2)}) %collective-permute-start.2) | collective-permute-done | bytes 131104 | tf_op jit(solution)/shard_map/ppermute | solution.py:683
  20.7 0.7 %scan_chips.1 = (bf16[2,2,128,128]{3,2,1,0:T(8,128)(2,1)S(1)}, bf16[2,2,128,128]{3,2,1,0:T(8,128)(2,1)S(1)}) custom-call(bf16[2,3,128,128]{3,2,1,0:T(8,128)(2,1)S(1)} %get-tuple-element.53.keep_ref, bf16[2,3,128,128]{3,2,1,0:T(8,128)(2,1)S(1)} %collective-permute-done.recv_ref, bf16[2,2,128,128]{3,2,1,0:T(8,128)(2,1)S(1)} %collective-permute-done.1.near_ref, ...), custom_call_target="tpu_custom_call" | custom-call | tf_op jit(solution)/shard_map/scan_chips/pallas_call | solution.py:504
  21.4 0.1 collective-permute-start.4
  21.5 0.6 %weigh.1 = (bf16[2,128,256]{2,1,0:T(8,128)(2,1)S(1)}, bf16[2,128,256]{2,1,0:T(8,128)(2,1)S(1)}, f32[4,256,256]{2,1,0:T(8,128)S(1)}, f32[4,256,256]{2,1,0:T(8,128...) custom-call(f32[8,256]{1,0:T(8,128)S(1)} %get-tuple-element.47.refs_2_.lane_ref, ...), custom_call_target="tpu_custom_call" | custom-call | tf_op jit(solution)/shard_map/weigh/pallas_call | solution.py:397
  22.1 1.5 %own_grads.1 = (bf16[3,256,256]{2,1,0:T(8,128)(2,1)S(1)}, f32[256,512]{1,0:T(8,128)S(1)}) custom-call(bf16[3,2048,512]{2,1,0:T(8,128)(2,1)S(1)} %get-tuple-element.44.w_ref, bf16[2,2,128,128]{3,2,1,0:T(8,128)(2,1)S(1)} %get-tuple-element.57.edge_ref, f32[2,256,512]{2,1,0:T(8,128)S(1)} %get-tuple-element.58.scale_ref, ...), custom_call_target="tpu_custom_call" | custom-call | tf_op jit(solution)/shard_map/own_grads/pallas_call | solution.py:611
  23.6 0.0 collective-permute-done.4.edge_ref
  23.6 1.5 %grads.1 = (bf16[3,256,256]{2,1,0:T(8,128)(2,1)S(1)}, bf16[256,512]{1,0:T(8,128)(2,1)S(1)}) custom-call(bf16[3,2048,512]{2,1,0:T(8,128)(2,1)S(1)} %get-tuple-element.44.w_ref, bf16[2,2,128,128]{3,2,1,0:T(8,128)(2,1)S(1)} %collective-permute-done.4.edge_ref, f32[2,256,512]{2,1,0:T(8,128)S(1)} %get-tuple-element.58.scale_ref, ...), custom_call_target="tpu_custom_call" | custom-call | tf_op jit(solution)/shard_map/grads/pallas_call | solution.py:644
  25.1 1.6 %collective-permute-start.7 = (bf16[256,512]{1,0:T(8,128)(2,1)S(1)}, bf16[256,512]{1,0:T(8,128)(2,1)S(1)}, u32[]{:S(2)}, u32[]{:S(2)}) collective-permute-start(bf16[256,512]{1,0:T(8,128)(2,1)S(1)} %get-tuple-element.80), channel_id=1, source_target_pairs={{0,1},{1,0},{2,3},{3,2},{4,5},{5,4},{6,7},{7,6},{8,9},{9,8},{10,11... | collective-permute-start | bytes 786440 | tf_op jit(solution)/shard_map/ppermute | solution.py:764
  26.8 0.7 %collective-permute-start.5 = (bf16[256,512]{1,0:T(8,128)(2,1)S(1)}, bf16[256,512]{1,0:T(8,128)(2,1)S(1)}, u32[]{:S(2)}, u32[]{:S(2)}) collective-permute-start(bf16[256,512]{1,0:T(8,128)(2,1)S(1)} %get-tuple-element.80), channel_id=1, source_target_pairs={{1,2},{2,1},{5,6},{6,5},{9,10},{10,9},{13,14},{14,13},{17,18},{18,... | collective-permute-start | bytes 786440 | tf_op jit(solution)/shard_map/ppermute | solution.py:765
  27.4 1.4 %others.1 = (bf16[256,512]{1,0:T(8,128)(2,1)S(1)}, f32[256,512]{1,0:T(8,128)S(1)}, f32[256,512]{1,0:T(8,128)S(1)}) custom-call(bf16[3,2048,512]{2,1,0:T(8,128)(2,1)S(1)} %get-tuple-element.44.w_ref, bf16[3,256,256]{2,1,0:T(8,128)(2,1)S(1)} %get-tuple-element.71.refs_0_, bf16[3,256,256]{2,1,0:T(8,128)(2,1)S(1)} %get-tuple-element.78.refs_1_), custom_call_target="tpu_custom_call" | custom-call | tf_op jit(solution)/shard_map/others/pallas_call | solution.py:672
  28.9 3.9 %collective-permute-start.6 = (bf16[256,512]{1,0:T(8,128)(2,1)S(1)}, bf16[256,512]{1,0:T(8,128)(2,1)S(1)}, u32[]{:S(2)}, u32[]{:S(2)}) collective-permute-start(bf16[256,512]{1,0:T(8,128)(2,1)S(1)} %get-tuple-element.81), channel_id=1, source_target_pairs={{0,2},{2,3},{3,1},{1,0},{4,6},{6,7},{7,5},{5,4},{8,10},{10,11},{11... | collective-permute-start | bytes 786440 | tf_op jit(solution)/shard_map/ppermute | solution.py:768
  32.8 1.1 %collective-permute-done.7.outer_ref = bf16[256,512]{1,0:T(8,128)(2,1)S(1)} collective-permute-done((bf16[256,512]{1,0:T(8,128)(2,1)S(1)}, bf16[256,512]{1,0:T(8,128)(2,1)S(1)}, u32[]{:S(2)}, u32[]{:S(2)}) %collective-permute-start.7) | collective-permute-done | bytes 262176 | tf_op jit(solution)/shard_map/ppermute | solution.py:764
  33.9 1.7 %collective-permute-start.8 = (bf16[256,512]{1,0:T(8,128)(2,1)S(1)}, bf16[256,512]{1,0:T(8,128)(2,1)S(1)}, u32[]{:S(2)}, u32[]{:S(2)}) collective-permute-start(bf16[256,512]{1,0:T(8,128)(2,1)S(1)} %join_outer.1), channel_id=1, source_target_pairs={{0,1},{1,3},{3,2},{2,0},{4,5},{5,7},{7,6},{6,4},{8,9},{9,11},{11,1... | collective-permute-start | bytes 786440 | tf_op jit(solution)/shard_map/ppermute | solution.py:767
  35.6 4.1 %collective-permute-done.6 = bf16[256,512]{1,0:T(8,128)(2,1)S(1)} collective-permute-done((bf16[256,512]{1,0:T(8,128)(2,1)S(1)}, bf16[256,512]{1,0:T(8,128)(2,1)S(1)}, u32[]{:S(2)}, u32[]{:S(2)}) %collective-permute-start.6) | collective-permute-done | bytes 262176 | tf_op jit(solution)/shard_map/ppermute | solution.py:768
  39.7 0.0 collective-permute-done.5
  39.7 9.4 %collective-permute-done.8 = bf16[256,512]{1,0:T(8,128)(2,1)S(1)} collective-permute-done((bf16[256,512]{1,0:T(8,128)(2,1)S(1)}, bf16[256,512]{1,0:T(8,128)(2,1)S(1)}, u32[]{:S(2)}, u32[]{:S(2)}) %collective-permute-start.8) | collective-permute-done | bytes 262176 | tf_op jit(solution)/shard_map/ppermute | solution.py:767
  49.2 0.8 %add_convert_fusion = bf16[256,512]{1,0:T(8,128)(2,1)} fusion(bf16[256,512]{1,0:T(8,128)(2,1)S(1)} %collective-permute-done.8, bf16[256,512]{1,0:T(8,128)(2,1)S(1)} %collective-permute-done.6, f32[256,512]{1,0:T(8,128)S(1)} %get-tuple-element.79, bf16[256,512]{1,0:T(8,128)(2,1)S(1)} %collective-permute-done.5), kind=kLoop, calls=%fused_computation | loop fusion | flops 917504 | bytes 1572864 | tf_op jit(solution)/shard_map/convert_element_type | solution.py:770
  (1 shorter events, 0.0 us)
Async XLA Ops:
  6.7 1.6 %collective-permute-start = (bf16[2,3,128,128]{3,2,1,0:T(8,128)(2,1)S(1)}, bf16[2,3,128,128]{3,2,1,0:T(8,128)(2,1)S(1)}, u32[]{:S(2)}, u32[]{:S(2)}) collective-permute-start(bf16[2,3,128,128]{3,2,1,0:T(8,128)(2,1)S(1)} %get-tuple-element.54), channel_id=1, source_target_pairs={{0,4},{4,0},{8,12},{12,8},{16,20},{20,16},{24,28},{28,24},{1,5},{5... | collective-permute-start | bytes 589832 | tf_op jit(solution)/shard_map/ppermute | solution.py:683
  8.5 7.1 %collective-permute-start.1 = (bf16[2,2,128,128]{3,2,1,0:T(8,128)(2,1)S(1)}, bf16[2,2,128,128]{3,2,1,0:T(8,128)(2,1)S(1)}, u32[]{:S(2)}, u32[]{:S(2)}) collective-permute-start(bf16[2,2,128,128]{3,2,1,0:T(8,128)(2,1)S(1)} %get-tuple-element.55), channel_id=1, source_target_pairs={{0,8},{4,12},{8,0},{12,4},{16,24},{20,28},{24,16},{28,20},{1,9},{5... | collective-permute-start | bytes 393224 | tf_op jit(solution)/shard_map/ppermute | solution.py:683
  11.4 7.9 %collective-permute-start.3 = (bf16[2,2,128,128]{3,2,1,0:T(8,128)(2,1)S(1)}, bf16[2,2,128,128]{3,2,1,0:T(8,128)(2,1)S(1)}, u32[]{:S(2)}, u32[]{:S(2)}) collective-permute-start(bf16[2,2,128,128]{3,2,1,0:T(8,128)(2,1)S(1)} %get-tuple-element.56), channel_id=1, source_target_pairs={{0,24},{4,28},{8,16},{12,20},{16,8},{20,12},{24,0},{28,4},{1,25},{... | collective-permute-start | bytes 393224 | tf_op jit(solution)/shard_map/ppermute | solution.py:683
  12.9 7.8 %collective-permute-start.2 = (bf16[2,2,128,128]{3,2,1,0:T(8,128)(2,1)S(1)}, bf16[2,2,128,128]{3,2,1,0:T(8,128)(2,1)S(1)}, u32[]{:S(2)}, u32[]{:S(2)}) collective-permute-start(bf16[2,2,128,128]{3,2,1,0:T(8,128)(2,1)S(1)} %get-tuple-element.56), channel_id=1, source_target_pairs={{0,16},{4,20},{8,24},{12,28},{16,0},{20,4},{24,8},{28,12},{1,17},{... | collective-permute-start | bytes 393224 | tf_op jit(solution)/shard_map/ppermute | solution.py:683
  21.4 2.2 %collective-permute-start.4 = (bf16[2,2,128,128]{3,2,1,0:T(8,128)(2,1)S(1)}, bf16[2,2,128,128]{3,2,1,0:T(8,128)(2,1)S(1)}, u32[]{:S(2)}, u32[]{:S(2)}) collective-permute-start(bf16[2,2,128,128]{3,2,1,0:T(8,128)(2,1)S(1)} %get-tuple-element.72), channel_id=1, source_target_pairs={{0,4},{4,0},{8,12},{12,8},{16,20},{20,16},{24,28},{28,24},{1,5},{5... | collective-permute-start | bytes 393224 | tf_op jit(solution)/shard_map/ppermute | solution.py:683
  25.1 8.8 %collective-permute-start.7 = (bf16[256,512]{1,0:T(8,128)(2,1)S(1)}, bf16[256,512]{1,0:T(8,128)(2,1)S(1)}, u32[]{:S(2)}, u32[]{:S(2)}) collective-permute-start(bf16[256,512]{1,0:T(8,128)(2,1)S(1)} %get-tuple-element.80), channel_id=1, source_target_pairs={{0,1},{1,0},{2,3},{3,2},{4,5},{5,4},{6,7},{7,6},{8,9},{9,8},{10,11... | collective-permute-start | bytes 786440 | tf_op jit(solution)/shard_map/ppermute | solution.py:764
  26.8 13.0 %collective-permute-start.5 = (bf16[256,512]{1,0:T(8,128)(2,1)S(1)}, bf16[256,512]{1,0:T(8,128)(2,1)S(1)}, u32[]{:S(2)}, u32[]{:S(2)}) collective-permute-start(bf16[256,512]{1,0:T(8,128)(2,1)S(1)} %get-tuple-element.80), channel_id=1, source_target_pairs={{1,2},{2,1},{5,6},{6,5},{9,10},{10,9},{13,14},{14,13},{17,18},{18,... | collective-permute-start | bytes 786440 | tf_op jit(solution)/shard_map/ppermute | solution.py:765
  28.9 10.8 %collective-permute-start.6 = (bf16[256,512]{1,0:T(8,128)(2,1)S(1)}, bf16[256,512]{1,0:T(8,128)(2,1)S(1)}, u32[]{:S(2)}, u32[]{:S(2)}) collective-permute-start(bf16[256,512]{1,0:T(8,128)(2,1)S(1)} %get-tuple-element.81), channel_id=1, source_target_pairs={{0,2},{2,3},{3,1},{1,0},{4,6},{6,7},{7,5},{5,4},{8,10},{10,11},{11... | collective-permute-start | bytes 786440 | tf_op jit(solution)/shard_map/ppermute | solution.py:768
  33.9 15.2 %collective-permute-start.8 = (bf16[256,512]{1,0:T(8,128)(2,1)S(1)}, bf16[256,512]{1,0:T(8,128)(2,1)S(1)}, u32[]{:S(2)}, u32[]{:S(2)}) collective-permute-start(bf16[256,512]{1,0:T(8,128)(2,1)S(1)} %join_outer.1), channel_id=1, source_target_pairs={{0,1},{1,3},{3,2},{2,0},{4,5},{5,7},{7,6},{6,4},{8,9},{9,11},{11,1... | collective-permute-start | bytes 786440 | tf_op jit(solution)/shard_map/ppermute | solution.py:767

commit v9 on v8

--- a/solution.py
+++ b/solution.py
@@ -143,16 +143,16 @@
     width = columns // heads
     chunk = depth // pieces
 
-    def part(i):
+    def piece(i):
         return pl.ds(i * chunk, chunk)
 
     tok_copies = [
-        pltpu.make_async_copy(tok_hbm.at[:, part(i)], tok_scr.at[:, part(i)], tok_sem.at[i])
+        pltpu.make_async_copy(tok_hbm.at[:, piece(i)], tok_scr.at[:, piece(i)], tok_sem.at[i])
         for i in range(pieces)
     ]
     w_copies = [
         [
-            pltpu.make_async_copy(w_hbm.at[p, part(i)], w_ref.at[p, part(i)], w_sem.at[p, i])
+            pltpu.make_async_copy(w_hbm.at[p, piece(i)], w_ref.at[p, piece(i)], w_sem.at[p, i])
             for i in range(pieces)
         ]
         for p in range(members)

time: 50.2 us -> 50.2 us (level)
  no operation moved by 1% of the time
where the time goes in v9:
time: 50.2 us; the launch traced here: 50 us
  waiting for transfers between devices  22.7 us (45%)
  Pallas kernels  13.4 us (27%)
  starting transfers between devices  12.9 us (26%)
  other arithmetic  0.84 us (2%)
    ppermute x1, waiting for transfers between devices, sum_of_four(): joint = lax.ppermute(joint, 'head', [(0, 1), (1, 3), (3, 2), (2, 0)])  9.44 us
    ppermute x5, waiting for transfers between devices, swap(): return lax.ppermute(value, axis, [(i, i ^ mask) for i in range(count)])  8.01 us
    pallas_call x1, Pallas kernels, prepare(): pl.pallas_call(functools.partial(prepare_kernel, 1 if half else None, hal...  6.66 us
    ppermute x5, starting transfers between devices, swap(): return lax.ppermute(value, axis, [(i, i ^ mask) for i in range(count)])  5.07 us
    ppermute x1, waiting for transfers between devices, sum_of_four(): ring = lax.ppermute(first, 'head', [(0, 2), (2, 3), (3, 1), (1, 0)])  4.14 us
    ppermute x1, starting transfers between devices, sum_of_four(): ring = lax.ppermute(first, 'head', [(0, 2), (2, 3), (3, 1), (1, 0)])  3.89 us
    ppermute x1, starting transfers between devices, sum_of_four(): joint = lax.ppermute(joint, 'head', [(0, 1), (1, 3), (3, 2), (2, 0)])  1.65 us
    ppermute x1, starting transfers between devices, sum_of_four(): outer = lax.ppermute(end, 'head', [(0, 1), (1, 0), (2, 3), (3, 2)])  1.64 us
  transfers between devices with their start and end apart: 9, of which 7 were waited for; matrix products, arithmetic and copies ran while one was open for 0% of the time, Pallas kernels for 9%

profile of v9, /device:TPU:0, one launch (start us, length us, event | category | flops | bytes accessed | tf_op | source)
XLA Modules:
  0.0 50.0 jit_solution(10502526002659461370)
XLA Ops:
  0.0 6.7 %prepare.1 = (bf16[3,2048,512]{2,1,0:T(8,128)(2,1)S(1)}, bf16[256,512]{1,0:T(8,128)(2,1)S(1)}, f32[2,256,512]{2,1,0:T(8,128)S(1)}, f32[2,256,512]{2,1,0:T(8,128)...) custom-call(bf16[256,2048]{1,0:T(8,128)(2,1)} %tok_hbm.1, ...), custom_call_target="tpu_custom_call" | custom-call | tf_op jit(solution)/shard_map/prepare/pallas_call | solution.py:331
  6.7 0.5 %collective-permute-start = (bf16[2,3,128,128]{3,2,1,0:T(8,128)(2,1)S(1)}, bf16[2,3,128,128]{3,2,1,0:T(8,128)(2,1)S(1)}, u32[]{:S(2)}, u32[]{:S(2)}) collective-permute-start(bf16[2,3,128,128]{3,2,1,0:T(8,128)(2,1)S(1)} %get-tuple-element.54), channel_id=1, source_target_pairs={{0,4},{4,0},{8,12},{12,8},{16,20},{20,16},{24,28},{28,24},{1,5},{5... | collective-permute-start | bytes 589832 | tf_op jit(solution)/shard_map/ppermute | solution.py:683
  7.2 0.8 %solve_own.1 = (f32[2,256,128]{2,1,0:T(8,128)S(1)}, bf16[2,256,128]{2,1,0:T(8,128)(2,1)S(1)}, f32[2,128,256]{2,1,0:T(8,128)S(1)}, f32[2,128,256]{2,1,0:T(8,128)S(1)}, bf16[2,3,128,128]{3,2,1,0:T(8,128)(2,1)S(1)}) custom-call(f32[2,256,512]{2,1,0:T(8,128)S(1)} %get-tuple-element.45.refs_0_, f32[256,512]{1,0:T(8,128)S(1)} %get-tuple-element.46.refs_1_, ...), custom_call_target="tpu_custom_call" | custom-call | tf_op jit(solution)/shard_map/solve_own/pallas_call | solution.py:357
  8.0 0.3 collective-permute-done.recv_ref
  8.3 0.2 join_pair.1
  8.5 2.9 %collective-permute-start.1 = (bf16[2,2,128,128]{3,2,1,0:T(8,128)(2,1)S(1)}, bf16[2,2,128,128]{3,2,1,0:T(8,128)(2,1)S(1)}, u32[]{:S(2)}, u32[]{:S(2)}) collective-permute-start(bf16[2,2,128,128]{3,2,1,0:T(8,128)(2,1)S(1)} %get-tuple-element.55), channel_id=1, source_target_pairs={{0,8},{4,12},{8,0},{12,4},{16,24},{20,28},{24,16},{28,20},{1,9},{5... | collective-permute-start | bytes 393224 | tf_op jit(solution)/shard_map/ppermute | solution.py:683
  11.4 1.5 %collective-permute-start.3 = (bf16[2,2,128,128]{3,2,1,0:T(8,128)(2,1)S(1)}, bf16[2,2,128,128]{3,2,1,0:T(8,128)(2,1)S(1)}, u32[]{:S(2)}, u32[]{:S(2)}) collective-permute-start(bf16[2,2,128,128]{3,2,1,0:T(8,128)(2,1)S(1)} %get-tuple-element.56), channel_id=1, source_target_pairs={{0,24},{4,28},{8,16},{12,20},{16,8},{20,12},{24,0},{28,4},{1,25},{... | collective-permute-start | bytes 393224 | tf_op jit(solution)/shard_map/ppermute | solution.py:683
  12.9 0.0 collective-permute-start.2
  12.9 2.6 %collective-permute-done.1.near_ref = bf16[2,2,128,128]{3,2,1,0:T(8,128)(2,1)S(1)} collective-permute-done((bf16[2,2,128,128]{3,2,1,0:T(8,128)(2,1)S(1)}, bf16[2,2,128,128]{3,2,1,0:T(8,128)(2,1)S(1)}, u32[]{:S(2)}, u32[]{:S(2)}) %collective-permute-start.1) | collective-permute-done | bytes 131104 | tf_op jit(solution)/shard_map/ppermute | solution.py:683
  15.6 3.7 %collective-permute-done.3.cross_ref = bf16[2,2,128,128]{3,2,1,0:T(8,128)(2,1)S(1)} collective-permute-done((bf16[2,2,128,128]{3,2,1,0:T(8,128)(2,1)S(1)}, bf16[2,2,128,128]{3,2,1,0:T(8,128)(2,1)S(1)}, u32[]{:S(2)}, u32[]{:S(2)}) %collective-permute-start.3) | collective-permute-done | bytes 131104 | tf_op jit(solution)/shard_map/ppermute | solution.py:683
  19.3 1.4 %collective-permute-done.2.far_ref = bf16[2,2,128,128]{3,2,1,0:T(8,128)(2,1)S(1)} collective-permute-done((bf16[2,2,128,128]{3,2,1,0:T(8,128)(2,1)S(1)}, bf16[2,2,128,128]{3,2,1,0:T(8,128)(2,1)S(1)}, u32[]{:S(2)}, u32[]{:S(2)}) %collective-permute-start.2) | collective-permute-done | bytes 131104 | tf_op jit(solution)/shard_map/ppermute | solution.py:683
  20.7 0.7 %scan_chips.1 = (bf16[2,2,128,128]{3,2,1,0:T(8,128)(2,1)S(1)}, bf16[2,2,128,128]{3,2,1,0:T(8,128)(2,1)S(1)}) custom-call(bf16[2,3,128,128]{3,2,1,0:T(8,128)(2,1)S(1)} %get-tuple-element.53.keep_ref, bf16[2,3,128,128]{3,2,1,0:T(8,128)(2,1)S(1)} %collective-permute-done.recv_ref, bf16[2,2,128,128]{3,2,1,0:T(8,128)(2,1)S(1)} %collective-permute-done.1.near_ref, ...), custom_call_target="tpu_custom_call" | custom-call | tf_op jit(solution)/shard_map/scan_chips/pallas_call | solution.py:504
  21.4 0.1 collective-permute-start.4
  21.5 0.6 %weigh.1 = (bf16[2,128,256]{2,1,0:T(8,128)(2,1)S(1)}, bf16[2,128,256]{2,1,0:T(8,128)(2,1)S(1)}, f32[4,256,256]{2,1,0:T(8,128)S(1)}, f32[4,256,256]{2,1,0:T(8,128...) custom-call(f32[8,256]{1,0:T(8,128)S(1)} %get-tuple-element.47.refs_2_.lane_ref, ...), custom_call_target="tpu_custom_call" | custom-call | tf_op jit(solution)/shard_map/weigh/pallas_call | solution.py:397
  22.1 1.5 %own_grads.1 = (bf16[3,256,256]{2,1,0:T(8,128)(2,1)S(1)}, f32[256,512]{1,0:T(8,128)S(1)}) custom-call(bf16[3,2048,512]{2,1,0:T(8,128)(2,1)S(1)} %get-tuple-element.44.w_ref, bf16[2,2,128,128]{3,2,1,0:T(8,128)(2,1)S(1)} %get-tuple-element.57.edge_ref, f32[2,256,512]{2,1,0:T(8,128)S(1)} %get-tuple-element.58.scale_ref, ...), custom_call_target="tpu_custom_call" | custom-call | tf_op jit(solution)/shard_map/own_grads/pallas_call | solution.py:611
  23.6 0.0 collective-permute-done.4.edge_ref
  23.6 1.5 %grads.1 = (bf16[3,256,256]{2,1,0:T(8,128)(2,1)S(1)}, bf16[256,512]{1,0:T(8,128)(2,1)S(1)}) custom-call(bf16[3,2048,512]{2,1,0:T(8,128)(2,1)S(1)} %get-tuple-element.44.w_ref, bf16[2,2,128,128]{3,2,1,0:T(8,128)(2,1)S(1)} %collective-permute-done.4.edge_ref, f32[2,256,512]{2,1,0:T(8,128)S(1)} %get-tuple-element.58.scale_ref, ...), custom_call_target="tpu_custom_call" | custom-call | tf_op jit(solution)/shard_map/grads/pallas_call | solution.py:644
  25.1 1.6 %collective-permute-start.7 = (bf16[256,512]{1,0:T(8,128)(2,1)S(1)}, bf16[256,512]{1,0:T(8,128)(2,1)S(1)}, u32[]{:S(2)}, u32[]{:S(2)}) collective-permute-start(bf16[256,512]{1,0:T(8,128)(2,1)S(1)} %get-tuple-element.80), channel_id=1, source_target_pairs={{0,1},{1,0},{2,3},{3,2},{4,5},{5,4},{6,7},{7,6},{8,9},{9,8},{10,11... | collective-permute-start | bytes 786440 | tf_op jit(solution)/shard_map/ppermute | solution.py:764
  26.8 0.7 %collective-permute-start.5 = (bf16[256,512]{1,0:T(8,128)(2,1)S(1)}, bf16[256,512]{1,0:T(8,128)(2,1)S(1)}, u32[]{:S(2)}, u32[]{:S(2)}) collective-permute-start(bf16[256,512]{1,0:T(8,128)(2,1)S(1)} %get-tuple-element.80), channel_id=1, source_target_pairs={{1,2},{2,1},{5,6},{6,5},{9,10},{10,9},{13,14},{14,13},{17,18},{18,... | collective-permute-start | bytes 786440 | tf_op jit(solution)/shard_map/ppermute | solution.py:765
  27.4 1.4 %others.1 = (bf16[256,512]{1,0:T(8,128)(2,1)S(1)}, f32[256,512]{1,0:T(8,128)S(1)}, f32[256,512]{1,0:T(8,128)S(1)}) custom-call(bf16[3,2048,512]{2,1,0:T(8,128)(2,1)S(1)} %get-tuple-element.44.w_ref, bf16[3,256,256]{2,1,0:T(8,128)(2,1)S(1)} %get-tuple-element.71.refs_0_, bf16[3,256,256]{2,1,0:T(8,128)(2,1)S(1)} %get-tuple-element.78.refs_1_), custom_call_target="tpu_custom_call" | custom-call | tf_op jit(solution)/shard_map/others/pallas_call | solution.py:672
  28.9 3.9 %collective-permute-start.6 = (bf16[256,512]{1,0:T(8,128)(2,1)S(1)}, bf16[256,512]{1,0:T(8,128)(2,1)S(1)}, u32[]{:S(2)}, u32[]{:S(2)}) collective-permute-start(bf16[256,512]{1,0:T(8,128)(2,1)S(1)} %get-tuple-element.81), channel_id=1, source_target_pairs={{0,2},{2,3},{3,1},{1,0},{4,6},{6,7},{7,5},{5,4},{8,10},{10,11},{11... | collective-permute-start | bytes 786440 | tf_op jit(solution)/shard_map/ppermute | solution.py:768
  32.8 1.1 %collective-permute-done.7.outer_ref = bf16[256,512]{1,0:T(8,128)(2,1)S(1)} collective-permute-done((bf16[256,512]{1,0:T(8,128)(2,1)S(1)}, bf16[256,512]{1,0:T(8,128)(2,1)S(1)}, u32[]{:S(2)}, u32[]{:S(2)}) %collective-permute-start.7) | collective-permute-done | bytes 262176 | tf_op jit(solution)/shard_map/ppermute | solution.py:764
  33.9 1.7 %collective-permute-start.8 = (bf16[256,512]{1,0:T(8,128)(2,1)S(1)}, bf16[256,512]{1,0:T(8,128)(2,1)S(1)}, u32[]{:S(2)}, u32[]{:S(2)}) collective-permute-start(bf16[256,512]{1,0:T(8,128)(2,1)S(1)} %join_outer.1), channel_id=1, source_target_pairs={{0,1},{1,3},{3,2},{2,0},{4,5},{5,7},{7,6},{6,4},{8,9},{9,11},{11,1... | collective-permute-start | bytes 786440 | tf_op jit(solution)/shard_map/ppermute | solution.py:767
  35.6 4.1 %collective-permute-done.6 = bf16[256,512]{1,0:T(8,128)(2,1)S(1)} collective-permute-done((bf16[256,512]{1,0:T(8,128)(2,1)S(1)}, bf16[256,512]{1,0:T(8,128)(2,1)S(1)}, u32[]{:S(2)}, u32[]{:S(2)}) %collective-permute-start.6) | collective-permute-done | bytes 262176 | tf_op jit(solution)/shard_map/ppermute | solution.py:768
  39.7 0.0 collective-permute-done.5
  39.7 9.4 %collective-permute-done.8 = bf16[256,512]{1,0:T(8,128)(2,1)S(1)} collective-permute-done((bf16[256,512]{1,0:T(8,128)(2,1)S(1)}, bf16[256,512]{1,0:T(8,128)(2,1)S(1)}, u32[]{:S(2)}, u32[]{:S(2)}) %collective-permute-start.8) | collective-permute-done | bytes 262176 | tf_op jit(solution)/shard_map/ppermute | solution.py:767
  49.2 0.8 %add_convert_fusion = bf16[256,512]{1,0:T(8,128)(2,1)} fusion(bf16[256,512]{1,0:T(8,128)(2,1)S(1)} %collective-permute-done.8, bf16[256,512]{1,0:T(8,128)(2,1)S(1)} %collective-permute-done.6, f32[256,512]{1,0:T(8,128)S(1)} %get-tuple-element.79, bf16[256,512]{1,0:T(8,128)(2,1)S(1)} %collective-permute-done.5), kind=kLoop, calls=%fused_computation | loop fusion | flops 917504 | bytes 1572864 | tf_op jit(solution)/shard_map/convert_element_type | solution.py:770
  (1 shorter events, 0.0 us)
Async XLA Ops:
  6.7 1.6 %collective-permute-start = (bf16[2,3,128,128]{3,2,1,0:T(8,128)(2,1)S(1)}, bf16[2,3,128,128]{3,2,1,0:T(8,128)(2,1)S(1)}, u32[]{:S(2)}, u32[]{:S(2)}) collective-permute-start(bf16[2,3,128,128]{3,2,1,0:T(8,128)(2,1)S(1)} %get-tuple-element.54), channel_id=1, source_target_pairs={{0,4},{4,0},{8,12},{12,8},{16,20},{20,16},{24,28},{28,24},{1,5},{5... | collective-permute-start | bytes 589832 | tf_op jit(solution)/shard_map/ppermute | solution.py:683
  8.5 7.1 %collective-permute-start.1 = (bf16[2,2,128,128]{3,2,1,0:T(8,128)(2,1)S(1)}, bf16[2,2,128,128]{3,2,1,0:T(8,128)(2,1)S(1)}, u32[]{:S(2)}, u32[]{:S(2)}) collective-permute-start(bf16[2,2,128,128]{3,2,1,0:T(8,128)(2,1)S(1)} %get-tuple-element.55), channel_id=1, source_target_pairs={{0,8},{4,12},{8,0},{12,4},{16,24},{20,28},{24,16},{28,20},{1,9},{5... | collective-permute-start | bytes 393224 | tf_op jit(solution)/shard_map/ppermute | solution.py:683
  11.4 7.9 %collective-permute-start.3 = (bf16[2,2,128,128]{3,2,1,0:T(8,128)(2,1)S(1)}, bf16[2,2,128,128]{3,2,1,0:T(8,128)(2,1)S(1)}, u32[]{:S(2)}, u32[]{:S(2)}) collective-permute-start(bf16[2,2,128,128]{3,2,1,0:T(8,128)(2,1)S(1)} %get-tuple-element.56), channel_id=1, source_target_pairs={{0,24},{4,28},{8,16},{12,20},{16,8},{20,12},{24,0},{28,4},{1,25},{... | collective-permute-start | bytes 393224 | tf_op jit(solution)/shard_map/ppermute | solution.py:683
  12.9 7.8 %collective-permute-start.2 = (bf16[2,2,128,128]{3,2,1,0:T(8,128)(2,1)S(1)}, bf16[2,2,128,128]{3,2,1,0:T(8,128)(2,1)S(1)}, u32[]{:S(2)}, u32[]{:S(2)}) collective-permute-start(bf16[2,2,128,128]{3,2,1,0:T(8,128)(2,1)S(1)} %get-tuple-element.56), channel_id=1, source_target_pairs={{0,16},{4,20},{8,24},{12,28},{16,0},{20,4},{24,8},{28,12},{1,17},{... | collective-permute-start | bytes 393224 | tf_op jit(solution)/shard_map/ppermute | solution.py:683
  21.4 2.2 %collective-permute-start.4 = (bf16[2,2,128,128]{3,2,1,0:T(8,128)(2,1)S(1)}, bf16[2,2,128,128]{3,2,1,0:T(8,128)(2,1)S(1)}, u32[]{:S(2)}, u32[]{:S(2)}) collective-permute-start(bf16[2,2,128,128]{3,2,1,0:T(8,128)(2,1)S(1)} %get-tuple-element.72), channel_id=1, source_target_pairs={{0,4},{4,0},{8,12},{12,8},{16,20},{20,16},{24,28},{28,24},{1,5},{5... | collective-permute-start | bytes 393224 | tf_op jit(solution)/shard_map/ppermute | solution.py:683
  25.1 8.8 %collective-permute-start.7 = (bf16[256,512]{1,0:T(8,128)(2,1)S(1)}, bf16[256,512]{1,0:T(8,128)(2,1)S(1)}, u32[]{:S(2)}, u32[]{:S(2)}) collective-permute-start(bf16[256,512]{1,0:T(8,128)(2,1)S(1)} %get-tuple-element.80), channel_id=1, source_target_pairs={{0,1},{1,0},{2,3},{3,2},{4,5},{5,4},{6,7},{7,6},{8,9},{9,8},{10,11... | collective-permute-start | bytes 786440 | tf_op jit(solution)/shard_map/ppermute | solution.py:764
  26.8 13.0 %collective-permute-start.5 = (bf16[256,512]{1,0:T(8,128)(2,1)S(1)}, bf16[256,512]{1,0:T(8,128)(2,1)S(1)}, u32[]{:S(2)}, u32[]{:S(2)}) collective-permute-start(bf16[256,512]{1,0:T(8,128)(2,1)S(1)} %get-tuple-element.80), channel_id=1, source_target_pairs={{1,2},{2,1},{5,6},{6,5},{9,10},{10,9},{13,14},{14,13},{17,18},{18,... | collective-permute-start | bytes 786440 | tf_op jit(solution)/shard_map/ppermute | solution.py:765
  28.9 10.8 %collective-permute-start.6 = (bf16[256,512]{1,0:T(8,128)(2,1)S(1)}, bf16[256,512]{1,0:T(8,128)(2,1)S(1)}, u32[]{:S(2)}, u32[]{:S(2)}) collective-permute-start(bf16[256,512]{1,0:T(8,128)(2,1)S(1)} %get-tuple-element.81), channel_id=1, source_target_pairs={{0,2},{2,3},{3,1},{1,0},{4,6},{6,7},{7,5},{5,4},{8,10},{10,11},{11... | collective-permute-start | bytes 786440 | tf_op jit(solution)/shard_map/ppermute | solution.py:768
  33.9 15.2 %collective-permute-start.8 = (bf16[256,512]{1,0:T(8,128)(2,1)S(1)}, bf16[256,512]{1,0:T(8,128)(2,1)S(1)}, u32[]{:S(2)}, u32[]{:S(2)}) collective-permute-start(bf16[256,512]{1,0:T(8,128)(2,1)S(1)} %join_outer.1), channel_id=1, source_target_pairs={{0,1},{1,3},{3,2},{2,0},{4,5},{5,7},{7,6},{6,4},{8,9},{9,11},{11,1... | collective-permute-start | bytes 786440 | tf_op jit(solution)/shard_map/ppermute | solution.py:767
